TPU v7x, 128 devices: a whole 4x4x4 slice. The times are simulated.
128 devices in a mesh: ctx: 32 (over y_lo, z, x), ch: 4 (over y_hi, core).
Axes of the slice: x: 4, y: 4 (y_hi: 2, y_lo: 2; y = y_hi * 2 + y_lo), z: 4, core: 2. Of those that a mesh axis runs over, the one named last changes fastest.
Arguments:
- query_gate: bfloat16 [8192, 4096], P('ctx', 'ch'), may hold values from -6 to 6
- gated_value: bfloat16 [8192, 4096], P('ctx', 'ch'), may hold values from -6 to 6
- long_filter: bfloat16 [8192, 4096], P(None, 'ch'), may hold values from -0.0625 to 0.0625
- out_weight: bfloat16 [4096, 4096], P('ch'), may hold values from -0.125 to 0.125
Outputs:
- output: bfloat16 [8192, 4096], P('ctx', 'ch')
All inputs are finite; a program needn't handle non-finite values.
Results may differ from a plain program's by a relative error of at most 0.019.
Values may be sent and summed in bfloat16 or wider, within the bound.
No kernel may reach another device: no remote copies, remote signals or barrier semaphores. Data moves between devices by JAX's collectives and lax.ppermute only.
A program may use at most 128 MiB of HBM per device.

v0:
```python
import math

import jax
import jax.numpy as jnp
from jax import lax
from jax.sharding import PartitionSpec as P

SPAN = 128


def dot_high(left, right):
    return jnp.dot(left, right, precision=lax.Precision.HIGHEST, preferred_element_type=jnp.float32)


def dot_plain(left, right):
    return jnp.dot(left, right, preferred_element_type=jnp.float32)


def make_tables():
    freq_int = jnp.arange(SPAN + 1, dtype=jnp.int32)[:, None]
    half_int = jnp.arange(SPAN, dtype=jnp.int32)[None, :]
    full_int = jnp.arange(2 * SPAN, dtype=jnp.int32)[None, :]
    half_phase = (freq_int * half_int % (2 * SPAN)).astype(jnp.float32) * (math.pi / SPAN)
    full_phase = (freq_int * full_int % (2 * SPAN)).astype(jnp.float32) * (math.pi / SPAN)
    parity = jnp.where(freq_int % 2 == 0, 1.0, -1.0).astype(jnp.float32)
    x_table = jnp.concatenate([jnp.cos(half_phase), -jnp.sin(half_phase)], 0).astype(jnp.bfloat16)
    filter_table = jnp.concatenate(
        [parity * jnp.cos(full_phase), -parity * jnp.sin(full_phase)], 0
    ).astype(jnp.bfloat16)
    weights = jnp.where((freq_int == 0) | (freq_int == SPAN), 1.0, 2.0).astype(jnp.float32)
    back_phase = half_phase.T
    inverse_table = jnp.concatenate(
        [weights.T * jnp.cos(back_phase), -weights.T * jnp.sin(back_phase)], 1
    ) / (2.0 * SPAN)
    return (x_table, filter_table, inverse_table)


def filter_spectrum(long_filter, filter_table, lag_block):
    first_row = jnp.maximum(lag_block * SPAN - SPAN, 0)
    window = lax.dynamic_slice_in_dim(long_filter, first_row, 2 * SPAN, 0)
    rolled = jnp.concatenate([jnp.zeros_like(window[:SPAN]), window[:SPAN]], 0)
    window = jnp.where(lag_block == 0, rolled, window)
    return dot_plain(filter_table, window)


def complex_times(filter_spec, source_spec, axis):
    freq_rows = SPAN + 1
    filt_real = lax.slice_in_dim(filter_spec, 0, freq_rows, axis=axis)
    filt_imag = lax.slice_in_dim(filter_spec, freq_rows, 2 * freq_rows, axis=axis)
    src_real = lax.slice_in_dim(source_spec, 0, freq_rows, axis=axis)
    src_imag = lax.slice_in_dim(source_spec, freq_rows, 2 * freq_rows, axis=axis)
    return jnp.concatenate(
        [filt_real * src_real - filt_imag * src_imag, filt_real * src_imag + filt_imag * src_real],
        axis,
    )


def block_number(position, axis_count):
    device_block = position // (2 * SPAN)
    second_half = position // SPAN % 2
    return jnp.where(second_half == 0, device_block, 2 * axis_count - 1 - device_block)


def per_device(query_gate, gated_value, long_filter, out_weight):
    x_table, filter_table, inverse_table = make_tables()
    axis_count = lax.axis_size("ctx")
    my_index = lax.axis_index("ctx")
    mine_high = 2 * axis_count - 1 - my_index
    channels = gated_value.shape[1]
    freq_rows = SPAN + 1

    def pair_term(lag_block, source_spec):
        return complex_times(filter_spectrum(long_filter, filter_table, lag_block), source_spec, 0)

    start_totals = jnp.zeros((2, 2 * freq_rows, channels), jnp.float32)
    shard_rows = lax.all_gather(gated_value, "ctx", axis=0, tiled=True)
    block_count = shard_rows.shape[0] // SPAN

    def one_block(block, totals):
        block_rows = lax.dynamic_slice_in_dim(shard_rows, block * SPAN, SPAN, 0)
        source = block_number(block * SPAN, axis_count)

        def include(inner):
            source_spec = dot_plain(x_table, block_rows)
            high_part = inner[1] + pair_term(mine_high - source, source_spec)

            def add_low(low_now):
                return low_now + pair_term(my_index - source, source_spec)

            def keep_low(low_now):
                return low_now

            low_part = lax.cond(source <= my_index, add_low, keep_low, inner[0])
            return jnp.stack([low_part, high_part])

        def skip_block(inner):
            return inner

        return lax.cond(source <= mine_high, include, skip_block, totals)

    totals = lax.fori_loop(0, block_count, one_block, start_totals)
    convolved = jnp.concatenate(
        [dot_high(inverse_table, totals[0]), dot_high(inverse_table, totals[1])], 0
    )
    gated_mix = (query_gate.astype(jnp.float32) * convolved).astype(jnp.bfloat16)
    partial_sum = jnp.dot(gated_mix, out_weight, preferred_element_type=jnp.float32)
    projected = lax.psum_scatter(
        partial_sum.astype(jnp.bfloat16), "ch", scatter_dimension=1, tiled=True
    )
    return projected


def solution(mesh):
    placed = (P("ctx", "ch"), P("ctx", "ch"), P(None, "ch"), P("ch", None))
    return jax.shard_map(
        per_device, mesh=mesh, in_specs=placed, out_specs=P("ctx", "ch"), check_vma=False
    )
```

profile of v0, /device:TPU:1, one launch (start us, length us, event | category | flops | bytes accessed | tf_op | source)
XLA Modules:
  0.0 738.9 jit_solution(10108354678242873776)
XLA Ops:
  10.8 189.1 %all-gather.2.cloned.1.call-done = bf16[8192,1024]{1,0:T(8,128)(2,1)} async-done(((bf16[256,1024]{1,0:T(8,128)(2,1)}), bf16[8192,1024]{1,0:T(8,128)(2,1)}) %all-gather.2.cloned.1.call-update) | async-done | bytes 16777232 | tf_op jit(solution)/shard_map/all_gather | solution.py:76
  201.5 478.4 %while.19 = (s32[]{:T(128)}, f32[2,258,1024]{2,1,0:T(8,128)}, s32[]{:T(128)}, s32[]{:T(128)}, bf16[8192,1024]{1,0:T(8,128)(2,1)}, /*index=5*/bf16[258,128]{1,0:T...) while((s32[]{:T(128)}, f32[2,258,1024]{2,1,0:T(8,128)}, ...), condition=%wide.region_5.6_spmd, body=%wide.region_0.5_spmd.sunk | while | flops 341860384 | bytes 25414548 | solution.py:101
  201.5 10.5 %conditional.3 = (f32[2,258,1024]{2,1,0:T(8,128)}) conditional(s32[]{:T(128)} %convert_element_type.75, f32[2,258,1024]{2,1,0:T(8,128)} %get-tuple-element.461, (s32[]{:T(128)}, s32[]{:T(128)}, f32[2,258,1024]{2,1,0:T(8,128)}, s32[]{:T(128)}, pred[]{:T(512)}, /*index=5*/bf16[8192,1024]{1,0:T(8,128)(2,1)}, bf16[258,128]{1,0:T(8,128)(2,1)}, ...), branch_computations={%region_1.1_spmd, %region_2.4_spmd} | conditional | flops 341860352 | bytes 25413872 | solution.py:99
  212.0 7.4 %conditional.3 = (f32[2,258,1024]{2,1,0:T(8,128)}) conditional(s32[]{:T(128)} %convert_element_type.75, f32[2,258,1024]{2,1,0:T(8,128)} %get-tuple-element.461, (s32[]{:T(128)}, s32[]{:T(128)}, f32[2,258,1024]{2,1,0:T(8,128)}, s32[]{:T(128)}, pred[]{:T(512)}, /*index=5*/bf16[8192,1024]{1,0:T(8,128)(2,1)}, bf16[258,128]{1,0:T(8,128)(2,1)}, ...), branch_computations={%region_1.1_spmd, %region_2.4_spmd} | conditional | flops 341860352 | bytes 25413872 | solution.py:99
  219.4 7.4 %conditional.3 = (f32[2,258,1024]{2,1,0:T(8,128)}) conditional(s32[]{:T(128)} %convert_element_type.75, f32[2,258,1024]{2,1,0:T(8,128)} %get-tuple-element.461, (s32[]{:T(128)}, s32[]{:T(128)}, f32[2,258,1024]{2,1,0:T(8,128)}, s32[]{:T(128)}, pred[]{:T(512)}, /*index=5*/bf16[8192,1024]{1,0:T(8,128)(2,1)}, bf16[258,128]{1,0:T(8,128)(2,1)}, ...), branch_computations={%region_1.1_spmd, %region_2.4_spmd} | conditional | flops 341860352 | bytes 25413872 | solution.py:99
  226.8 7.4 %conditional.3 = (f32[2,258,1024]{2,1,0:T(8,128)}) conditional(s32[]{:T(128)} %convert_element_type.75, f32[2,258,1024]{2,1,0:T(8,128)} %get-tuple-element.461, (s32[]{:T(128)}, s32[]{:T(128)}, f32[2,258,1024]{2,1,0:T(8,128)}, s32[]{:T(128)}, pred[]{:T(512)}, /*index=5*/bf16[8192,1024]{1,0:T(8,128)(2,1)}, bf16[258,128]{1,0:T(8,128)(2,1)}, ...), branch_computations={%region_1.1_spmd, %region_2.4_spmd} | conditional | flops 341860352 | bytes 25413872 | solution.py:99
  234.3 7.4 %conditional.3 = (f32[2,258,1024]{2,1,0:T(8,128)}) conditional(s32[]{:T(128)} %convert_element_type.75, f32[2,258,1024]{2,1,0:T(8,128)} %get-tuple-element.461, (s32[]{:T(128)}, s32[]{:T(128)}, f32[2,258,1024]{2,1,0:T(8,128)}, s32[]{:T(128)}, pred[]{:T(512)}, /*index=5*/bf16[8192,1024]{1,0:T(8,128)(2,1)}, bf16[258,128]{1,0:T(8,128)(2,1)}, ...), branch_computations={%region_1.1_spmd, %region_2.4_spmd} | conditional | flops 341860352 | bytes 25413872 | solution.py:99
  241.7 7.4 %conditional.3 = (f32[2,258,1024]{2,1,0:T(8,128)}) conditional(s32[]{:T(128)} %convert_element_type.75, f32[2,258,1024]{2,1,0:T(8,128)} %get-tuple-element.461, (s32[]{:T(128)}, s32[]{:T(128)}, f32[2,258,1024]{2,1,0:T(8,128)}, s32[]{:T(128)}, pred[]{:T(512)}, /*index=5*/bf16[8192,1024]{1,0:T(8,128)(2,1)}, bf16[258,128]{1,0:T(8,128)(2,1)}, ...), branch_computations={%region_1.1_spmd, %region_2.4_spmd} | conditional | flops 341860352 | bytes 25413872 | solution.py:99
  249.1 7.4 %conditional.3 = (f32[2,258,1024]{2,1,0:T(8,128)}) conditional(s32[]{:T(128)} %convert_element_type.75, f32[2,258,1024]{2,1,0:T(8,128)} %get-tuple-element.461, (s32[]{:T(128)}, s32[]{:T(128)}, f32[2,258,1024]{2,1,0:T(8,128)}, s32[]{:T(128)}, pred[]{:T(512)}, /*index=5*/bf16[8192,1024]{1,0:T(8,128)(2,1)}, bf16[258,128]{1,0:T(8,128)(2,1)}, ...), branch_computations={%region_1.1_spmd, %region_2.4_spmd} | conditional | flops 341860352 | bytes 25413872 | solution.py:99
  256.6 7.4 %conditional.3 = (f32[2,258,1024]{2,1,0:T(8,128)}) conditional(s32[]{:T(128)} %convert_element_type.75, f32[2,258,1024]{2,1,0:T(8,128)} %get-tuple-element.461, (s32[]{:T(128)}, s32[]{:T(128)}, f32[2,258,1024]{2,1,0:T(8,128)}, s32[]{:T(128)}, pred[]{:T(512)}, /*index=5*/bf16[8192,1024]{1,0:T(8,128)(2,1)}, bf16[258,128]{1,0:T(8,128)(2,1)}, ...), branch_computations={%region_1.1_spmd, %region_2.4_spmd} | conditional | flops 341860352 | bytes 25413872 | solution.py:99
  264.0 7.4 %conditional.3 = (f32[2,258,1024]{2,1,0:T(8,128)}) conditional(s32[]{:T(128)} %convert_element_type.75, f32[2,258,1024]{2,1,0:T(8,128)} %get-tuple-element.461, (s32[]{:T(128)}, s32[]{:T(128)}, f32[2,258,1024]{2,1,0:T(8,128)}, s32[]{:T(128)}, pred[]{:T(512)}, /*index=5*/bf16[8192,1024]{1,0:T(8,128)(2,1)}, bf16[258,128]{1,0:T(8,128)(2,1)}, ...), branch_computations={%region_1.1_spmd, %region_2.4_spmd} | conditional | flops 341860352 | bytes 25413872 | solution.py:99
  271.4 7.4 %conditional.3 = (f32[2,258,1024]{2,1,0:T(8,128)}) conditional(s32[]{:T(128)} %convert_element_type.75, f32[2,258,1024]{2,1,0:T(8,128)} %get-tuple-element.461, (s32[]{:T(128)}, s32[]{:T(128)}, f32[2,258,1024]{2,1,0:T(8,128)}, s32[]{:T(128)}, pred[]{:T(512)}, /*index=5*/bf16[8192,1024]{1,0:T(8,128)(2,1)}, bf16[258,128]{1,0:T(8,128)(2,1)}, ...), branch_computations={%region_1.1_spmd, %region_2.4_spmd} | conditional | flops 341860352 | bytes 25413872 | solution.py:99
  278.8 7.4 %conditional.3 = (f32[2,258,1024]{2,1,0:T(8,128)}) conditional(s32[]{:T(128)} %convert_element_type.75, f32[2,258,1024]{2,1,0:T(8,128)} %get-tuple-element.461, (s32[]{:T(128)}, s32[]{:T(128)}, f32[2,258,1024]{2,1,0:T(8,128)}, s32[]{:T(128)}, pred[]{:T(512)}, /*index=5*/bf16[8192,1024]{1,0:T(8,128)(2,1)}, bf16[258,128]{1,0:T(8,128)(2,1)}, ...), branch_computations={%region_1.1_spmd, %region_2.4_spmd} | conditional | flops 341860352 | bytes 25413872 | solution.py:99
  286.3 7.4 %conditional.3 = (f32[2,258,1024]{2,1,0:T(8,128)}) conditional(s32[]{:T(128)} %convert_element_type.75, f32[2,258,1024]{2,1,0:T(8,128)} %get-tuple-element.461, (s32[]{:T(128)}, s32[]{:T(128)}, f32[2,258,1024]{2,1,0:T(8,128)}, s32[]{:T(128)}, pred[]{:T(512)}, /*index=5*/bf16[8192,1024]{1,0:T(8,128)(2,1)}, bf16[258,128]{1,0:T(8,128)(2,1)}, ...), branch_computations={%region_1.1_spmd, %region_2.4_spmd} | conditional | flops 341860352 | bytes 25413872 | solution.py:99
  293.7 7.4 %conditional.3 = (f32[2,258,1024]{2,1,0:T(8,128)}) conditional(s32[]{:T(128)} %convert_element_type.75, f32[2,258,1024]{2,1,0:T(8,128)} %get-tuple-element.461, (s32[]{:T(128)}, s32[]{:T(128)}, f32[2,258,1024]{2,1,0:T(8,128)}, s32[]{:T(128)}, pred[]{:T(512)}, /*index=5*/bf16[8192,1024]{1,0:T(8,128)(2,1)}, bf16[258,128]{1,0:T(8,128)(2,1)}, ...), branch_computations={%region_1.1_spmd, %region_2.4_spmd} | conditional | flops 341860352 | bytes 25413872 | solution.py:99
  301.1 7.4 %conditional.3 = (f32[2,258,1024]{2,1,0:T(8,128)}) conditional(s32[]{:T(128)} %convert_element_type.75, f32[2,258,1024]{2,1,0:T(8,128)} %get-tuple-element.461, (s32[]{:T(128)}, s32[]{:T(128)}, f32[2,258,1024]{2,1,0:T(8,128)}, s32[]{:T(128)}, pred[]{:T(512)}, /*index=5*/bf16[8192,1024]{1,0:T(8,128)(2,1)}, bf16[258,128]{1,0:T(8,128)(2,1)}, ...), branch_computations={%region_1.1_spmd, %region_2.4_spmd} | conditional | flops 341860352 | bytes 25413872 | solution.py:99
  308.5 7.4 %conditional.3 = (f32[2,258,1024]{2,1,0:T(8,128)}) conditional(s32[]{:T(128)} %convert_element_type.75, f32[2,258,1024]{2,1,0:T(8,128)} %get-tuple-element.461, (s32[]{:T(128)}, s32[]{:T(128)}, f32[2,258,1024]{2,1,0:T(8,128)}, s32[]{:T(128)}, pred[]{:T(512)}, /*index=5*/bf16[8192,1024]{1,0:T(8,128)(2,1)}, bf16[258,128]{1,0:T(8,128)(2,1)}, ...), branch_computations={%region_1.1_spmd, %region_2.4_spmd} | conditional | flops 341860352 | bytes 25413872 | solution.py:99
  316.0 7.4 %conditional.3 = (f32[2,258,1024]{2,1,0:T(8,128)}) conditional(s32[]{:T(128)} %convert_element_type.75, f32[2,258,1024]{2,1,0:T(8,128)} %get-tuple-element.461, (s32[]{:T(128)}, s32[]{:T(128)}, f32[2,258,1024]{2,1,0:T(8,128)}, s32[]{:T(128)}, pred[]{:T(512)}, /*index=5*/bf16[8192,1024]{1,0:T(8,128)(2,1)}, bf16[258,128]{1,0:T(8,128)(2,1)}, ...), branch_computations={%region_1.1_spmd, %region_2.4_spmd} | conditional | flops 341860352 | bytes 25413872 | solution.py:99
  323.4 7.4 %conditional.3 = (f32[2,258,1024]{2,1,0:T(8,128)}) conditional(s32[]{:T(128)} %convert_element_type.75, f32[2,258,1024]{2,1,0:T(8,128)} %get-tuple-element.461, (s32[]{:T(128)}, s32[]{:T(128)}, f32[2,258,1024]{2,1,0:T(8,128)}, s32[]{:T(128)}, pred[]{:T(512)}, /*index=5*/bf16[8192,1024]{1,0:T(8,128)(2,1)}, bf16[258,128]{1,0:T(8,128)(2,1)}, ...), branch_computations={%region_1.1_spmd, %region_2.4_spmd} | conditional | flops 341860352 | bytes 25413872 | solution.py:99
  330.8 7.4 %conditional.3 = (f32[2,258,1024]{2,1,0:T(8,128)}) conditional(s32[]{:T(128)} %convert_element_type.75, f32[2,258,1024]{2,1,0:T(8,128)} %get-tuple-element.461, (s32[]{:T(128)}, s32[]{:T(128)}, f32[2,258,1024]{2,1,0:T(8,128)}, s32[]{:T(128)}, pred[]{:T(512)}, /*index=5*/bf16[8192,1024]{1,0:T(8,128)(2,1)}, bf16[258,128]{1,0:T(8,128)(2,1)}, ...), branch_computations={%region_1.1_spmd, %region_2.4_spmd} | conditional | flops 341860352 | bytes 25413872 | solution.py:99
  338.3 7.4 %conditional.3 = (f32[2,258,1024]{2,1,0:T(8,128)}) conditional(s32[]{:T(128)} %convert_element_type.75, f32[2,258,1024]{2,1,0:T(8,128)} %get-tuple-element.461, (s32[]{:T(128)}, s32[]{:T(128)}, f32[2,258,1024]{2,1,0:T(8,128)}, s32[]{:T(128)}, pred[]{:T(512)}, /*index=5*/bf16[8192,1024]{1,0:T(8,128)(2,1)}, bf16[258,128]{1,0:T(8,128)(2,1)}, ...), branch_computations={%region_1.1_spmd, %region_2.4_spmd} | conditional | flops 341860352 | bytes 25413872 | solution.py:99
  345.7 7.4 %conditional.3 = (f32[2,258,1024]{2,1,0:T(8,128)}) conditional(s32[]{:T(128)} %convert_element_type.75, f32[2,258,1024]{2,1,0:T(8,128)} %get-tuple-element.461, (s32[]{:T(128)}, s32[]{:T(128)}, f32[2,258,1024]{2,1,0:T(8,128)}, s32[]{:T(128)}, pred[]{:T(512)}, /*index=5*/bf16[8192,1024]{1,0:T(8,128)(2,1)}, bf16[258,128]{1,0:T(8,128)(2,1)}, ...), branch_computations={%region_1.1_spmd, %region_2.4_spmd} | conditional | flops 341860352 | bytes 25413872 | solution.py:99
  353.1 7.4 %conditional.3 = (f32[2,258,1024]{2,1,0:T(8,128)}) conditional(s32[]{:T(128)} %convert_element_type.75, f32[2,258,1024]{2,1,0:T(8,128)} %get-tuple-element.461, (s32[]{:T(128)}, s32[]{:T(128)}, f32[2,258,1024]{2,1,0:T(8,128)}, s32[]{:T(128)}, pred[]{:T(512)}, /*index=5*/bf16[8192,1024]{1,0:T(8,128)(2,1)}, bf16[258,128]{1,0:T(8,128)(2,1)}, ...), branch_computations={%region_1.1_spmd, %region_2.4_spmd} | conditional | flops 341860352 | bytes 25413872 | solution.py:99
  360.5 7.4 %conditional.3 = (f32[2,258,1024]{2,1,0:T(8,128)}) conditional(s32[]{:T(128)} %convert_element_type.75, f32[2,258,1024]{2,1,0:T(8,128)} %get-tuple-element.461, (s32[]{:T(128)}, s32[]{:T(128)}, f32[2,258,1024]{2,1,0:T(8,128)}, s32[]{:T(128)}, pred[]{:T(512)}, /*index=5*/bf16[8192,1024]{1,0:T(8,128)(2,1)}, bf16[258,128]{1,0:T(8,128)(2,1)}, ...), branch_computations={%region_1.1_spmd, %region_2.4_spmd} | conditional | flops 341860352 | bytes 25413872 | solution.py:99
  368.0 7.4 %conditional.3 = (f32[2,258,1024]{2,1,0:T(8,128)}) conditional(s32[]{:T(128)} %convert_element_type.75, f32[2,258,1024]{2,1,0:T(8,128)} %get-tuple-element.461, (s32[]{:T(128)}, s32[]{:T(128)}, f32[2,258,1024]{2,1,0:T(8,128)}, s32[]{:T(128)}, pred[]{:T(512)}, /*index=5*/bf16[8192,1024]{1,0:T(8,128)(2,1)}, bf16[258,128]{1,0:T(8,128)(2,1)}, ...), branch_computations={%region_1.1_spmd, %region_2.4_spmd} | conditional | flops 341860352 | bytes 25413872 | solution.py:99
  375.4 7.4 %conditional.3 = (f32[2,258,1024]{2,1,0:T(8,128)}) conditional(s32[]{:T(128)} %convert_element_type.75, f32[2,258,1024]{2,1,0:T(8,128)} %get-tuple-element.461, (s32[]{:T(128)}, s32[]{:T(128)}, f32[2,258,1024]{2,1,0:T(8,128)}, s32[]{:T(128)}, pred[]{:T(512)}, /*index=5*/bf16[8192,1024]{1,0:T(8,128)(2,1)}, bf16[258,128]{1,0:T(8,128)(2,1)}, ...), branch_computations={%region_1.1_spmd, %region_2.4_spmd} | conditional | flops 341860352 | bytes 25413872 | solution.py:99
  382.8 7.4 %conditional.3 = (f32[2,258,1024]{2,1,0:T(8,128)}) conditional(s32[]{:T(128)} %convert_element_type.75, f32[2,258,1024]{2,1,0:T(8,128)} %get-tuple-element.461, (s32[]{:T(128)}, s32[]{:T(128)}, f32[2,258,1024]{2,1,0:T(8,128)}, s32[]{:T(128)}, pred[]{:T(512)}, /*index=5*/bf16[8192,1024]{1,0:T(8,128)(2,1)}, bf16[258,128]{1,0:T(8,128)(2,1)}, ...), branch_computations={%region_1.1_spmd, %region_2.4_spmd} | conditional | flops 341860352 | bytes 25413872 | solution.py:99
  390.2 7.4 %conditional.3 = (f32[2,258,1024]{2,1,0:T(8,128)}) conditional(s32[]{:T(128)} %convert_element_type.75, f32[2,258,1024]{2,1,0:T(8,128)} %get-tuple-element.461, (s32[]{:T(128)}, s32[]{:T(128)}, f32[2,258,1024]{2,1,0:T(8,128)}, s32[]{:T(128)}, pred[]{:T(512)}, /*index=5*/bf16[8192,1024]{1,0:T(8,128)(2,1)}, bf16[258,128]{1,0:T(8,128)(2,1)}, ...), branch_computations={%region_1.1_spmd, %region_2.4_spmd} | conditional | flops 341860352 | bytes 25413872 | solution.py:99
  397.7 7.4 %conditional.3 = (f32[2,258,1024]{2,1,0:T(8,128)}) conditional(s32[]{:T(128)} %convert_element_type.75, f32[2,258,1024]{2,1,0:T(8,128)} %get-tuple-element.461, (s32[]{:T(128)}, s32[]{:T(128)}, f32[2,258,1024]{2,1,0:T(8,128)}, s32[]{:T(128)}, pred[]{:T(512)}, /*index=5*/bf16[8192,1024]{1,0:T(8,128)(2,1)}, bf16[258,128]{1,0:T(8,128)(2,1)}, ...), branch_computations={%region_1.1_spmd, %region_2.4_spmd} | conditional | flops 341860352 | bytes 25413872 | solution.py:99
  405.1 7.4 %conditional.3 = (f32[2,258,1024]{2,1,0:T(8,128)}) conditional(s32[]{:T(128)} %convert_element_type.75, f32[2,258,1024]{2,1,0:T(8,128)} %get-tuple-element.461, (s32[]{:T(128)}, s32[]{:T(128)}, f32[2,258,1024]{2,1,0:T(8,128)}, s32[]{:T(128)}, pred[]{:T(512)}, /*index=5*/bf16[8192,1024]{1,0:T(8,128)(2,1)}, bf16[258,128]{1,0:T(8,128)(2,1)}, ...), branch_computations={%region_1.1_spmd, %region_2.4_spmd} | conditional | flops 341860352 | bytes 25413872 | solution.py:99
  412.5 7.4 %conditional.3 = (f32[2,258,1024]{2,1,0:T(8,128)}) conditional(s32[]{:T(128)} %convert_element_type.75, f32[2,258,1024]{2,1,0:T(8,128)} %get-tuple-element.461, (s32[]{:T(128)}, s32[]{:T(128)}, f32[2,258,1024]{2,1,0:T(8,128)}, s32[]{:T(128)}, pred[]{:T(512)}, /*index=5*/bf16[8192,1024]{1,0:T(8,128)(2,1)}, bf16[258,128]{1,0:T(8,128)(2,1)}, ...), branch_computations={%region_1.1_spmd, %region_2.4_spmd} | conditional | flops 341860352 | bytes 25413872 | solution.py:99
  420.0 7.4 %conditional.3 = (f32[2,258,1024]{2,1,0:T(8,128)}) conditional(s32[]{:T(128)} %convert_element_type.75, f32[2,258,1024]{2,1,0:T(8,128)} %get-tuple-element.461, (s32[]{:T(128)}, s32[]{:T(128)}, f32[2,258,1024]{2,1,0:T(8,128)}, s32[]{:T(128)}, pred[]{:T(512)}, /*index=5*/bf16[8192,1024]{1,0:T(8,128)(2,1)}, bf16[258,128]{1,0:T(8,128)(2,1)}, ...), branch_computations={%region_1.1_spmd, %region_2.4_spmd} | conditional | flops 341860352 | bytes 25413872 | solution.py:99
  427.4 7.4 %conditional.3 = (f32[2,258,1024]{2,1,0:T(8,128)}) conditional(s32[]{:T(128)} %convert_element_type.75, f32[2,258,1024]{2,1,0:T(8,128)} %get-tuple-element.461, (s32[]{:T(128)}, s32[]{:T(128)}, f32[2,258,1024]{2,1,0:T(8,128)}, s32[]{:T(128)}, pred[]{:T(512)}, /*index=5*/bf16[8192,1024]{1,0:T(8,128)(2,1)}, bf16[258,128]{1,0:T(8,128)(2,1)}, ...), branch_computations={%region_1.1_spmd, %region_2.4_spmd} | conditional | flops 341860352 | bytes 25413872 | solution.py:99
  434.8 7.4 %conditional.3 = (f32[2,258,1024]{2,1,0:T(8,128)}) conditional(s32[]{:T(128)} %convert_element_type.75, f32[2,258,1024]{2,1,0:T(8,128)} %get-tuple-element.461, (s32[]{:T(128)}, s32[]{:T(128)}, f32[2,258,1024]{2,1,0:T(8,128)}, s32[]{:T(128)}, pred[]{:T(512)}, /*index=5*/bf16[8192,1024]{1,0:T(8,128)(2,1)}, bf16[258,128]{1,0:T(8,128)(2,1)}, ...), branch_computations={%region_1.1_spmd, %region_2.4_spmd} | conditional | flops 341860352 | bytes 25413872 | solution.py:99
  442.2 7.4 %conditional.3 = (f32[2,258,1024]{2,1,0:T(8,128)}) conditional(s32[]{:T(128)} %convert_element_type.75, f32[2,258,1024]{2,1,0:T(8,128)} %get-tuple-element.461, (s32[]{:T(128)}, s32[]{:T(128)}, f32[2,258,1024]{2,1,0:T(8,128)}, s32[]{:T(128)}, pred[]{:T(512)}, /*index=5*/bf16[8192,1024]{1,0:T(8,128)(2,1)}, bf16[258,128]{1,0:T(8,128)(2,1)}, ...), branch_computations={%region_1.1_spmd, %region_2.4_spmd} | conditional | flops 341860352 | bytes 25413872 | solution.py:99
  449.7 7.4 %conditional.3 = (f32[2,258,1024]{2,1,0:T(8,128)}) conditional(s32[]{:T(128)} %convert_element_type.75, f32[2,258,1024]{2,1,0:T(8,128)} %get-tuple-element.461, (s32[]{:T(128)}, s32[]{:T(128)}, f32[2,258,1024]{2,1,0:T(8,128)}, s32[]{:T(128)}, pred[]{:T(512)}, /*index=5*/bf16[8192,1024]{1,0:T(8,128)(2,1)}, bf16[258,128]{1,0:T(8,128)(2,1)}, ...), branch_computations={%region_1.1_spmd, %region_2.4_spmd} | conditional | flops 341860352 | bytes 25413872 | solution.py:99
  457.1 7.4 %conditional.3 = (f32[2,258,1024]{2,1,0:T(8,128)}) conditional(s32[]{:T(128)} %convert_element_type.75, f32[2,258,1024]{2,1,0:T(8,128)} %get-tuple-element.461, (s32[]{:T(128)}, s32[]{:T(128)}, f32[2,258,1024]{2,1,0:T(8,128)}, s32[]{:T(128)}, pred[]{:T(512)}, /*index=5*/bf16[8192,1024]{1,0:T(8,128)(2,1)}, bf16[258,128]{1,0:T(8,128)(2,1)}, ...), branch_computations={%region_1.1_spmd, %region_2.4_spmd} | conditional | flops 341860352 | bytes 25413872 | solution.py:99
  464.5 7.4 %conditional.3 = (f32[2,258,1024]{2,1,0:T(8,128)}) conditional(s32[]{:T(128)} %convert_element_type.75, f32[2,258,1024]{2,1,0:T(8,128)} %get-tuple-element.461, (s32[]{:T(128)}, s32[]{:T(128)}, f32[2,258,1024]{2,1,0:T(8,128)}, s32[]{:T(128)}, pred[]{:T(512)}, /*index=5*/bf16[8192,1024]{1,0:T(8,128)(2,1)}, bf16[258,128]{1,0:T(8,128)(2,1)}, ...), branch_computations={%region_1.1_spmd, %region_2.4_spmd} | conditional | flops 341860352 | bytes 25413872 | solution.py:99
  471.9 7.4 %conditional.3 = (f32[2,258,1024]{2,1,0:T(8,128)}) conditional(s32[]{:T(128)} %convert_element_type.75, f32[2,258,1024]{2,1,0:T(8,128)} %get-tuple-element.461, (s32[]{:T(128)}, s32[]{:T(128)}, f32[2,258,1024]{2,1,0:T(8,128)}, s32[]{:T(128)}, pred[]{:T(512)}, /*index=5*/bf16[8192,1024]{1,0:T(8,128)(2,1)}, bf16[258,128]{1,0:T(8,128)(2,1)}, ...), branch_computations={%region_1.1_spmd, %region_2.4_spmd} | conditional | flops 341860352 | bytes 25413872 | solution.py:99
  479.4 7.4 %conditional.3 = (f32[2,258,1024]{2,1,0:T(8,128)}) conditional(s32[]{:T(128)} %convert_element_type.75, f32[2,258,1024]{2,1,0:T(8,128)} %get-tuple-element.461, (s32[]{:T(128)}, s32[]{:T(128)}, f32[2,258,1024]{2,1,0:T(8,128)}, s32[]{:T(128)}, pred[]{:T(512)}, /*index=5*/bf16[8192,1024]{1,0:T(8,128)(2,1)}, bf16[258,128]{1,0:T(8,128)(2,1)}, ...), branch_computations={%region_1.1_spmd, %region_2.4_spmd} | conditional | flops 341860352 | bytes 25413872 | solution.py:99
  486.8 7.4 %conditional.3 = (f32[2,258,1024]{2,1,0:T(8,128)}) conditional(s32[]{:T(128)} %convert_element_type.75, f32[2,258,1024]{2,1,0:T(8,128)} %get-tuple-element.461, (s32[]{:T(128)}, s32[]{:T(128)}, f32[2,258,1024]{2,1,0:T(8,128)}, s32[]{:T(128)}, pred[]{:T(512)}, /*index=5*/bf16[8192,1024]{1,0:T(8,128)(2,1)}, bf16[258,128]{1,0:T(8,128)(2,1)}, ...), branch_computations={%region_1.1_spmd, %region_2.4_spmd} | conditional | flops 341860352 | bytes 25413872 | solution.py:99
  494.2 7.4 %conditional.3 = (f32[2,258,1024]{2,1,0:T(8,128)}) conditional(s32[]{:T(128)} %convert_element_type.75, f32[2,258,1024]{2,1,0:T(8,128)} %get-tuple-element.461, (s32[]{:T(128)}, s32[]{:T(128)}, f32[2,258,1024]{2,1,0:T(8,128)}, s32[]{:T(128)}, pred[]{:T(512)}, /*index=5*/bf16[8192,1024]{1,0:T(8,128)(2,1)}, bf16[258,128]{1,0:T(8,128)(2,1)}, ...), branch_computations={%region_1.1_spmd, %region_2.4_spmd} | conditional | flops 341860352 | bytes 25413872 | solution.py:99
  501.7 7.4 %conditional.3 = (f32[2,258,1024]{2,1,0:T(8,128)}) conditional(s32[]{:T(128)} %convert_element_type.75, f32[2,258,1024]{2,1,0:T(8,128)} %get-tuple-element.461, (s32[]{:T(128)}, s32[]{:T(128)}, f32[2,258,1024]{2,1,0:T(8,128)}, s32[]{:T(128)}, pred[]{:T(512)}, /*index=5*/bf16[8192,1024]{1,0:T(8,128)(2,1)}, bf16[258,128]{1,0:T(8,128)(2,1)}, ...), branch_computations={%region_1.1_spmd, %region_2.4_spmd} | conditional | flops 341860352 | bytes 25413872 | solution.py:99
  509.1 7.4 %conditional.3 = (f32[2,258,1024]{2,1,0:T(8,128)}) conditional(s32[]{:T(128)} %convert_element_type.75, f32[2,258,1024]{2,1,0:T(8,128)} %get-tuple-element.461, (s32[]{:T(128)}, s32[]{:T(128)}, f32[2,258,1024]{2,1,0:T(8,128)}, s32[]{:T(128)}, pred[]{:T(512)}, /*index=5*/bf16[8192,1024]{1,0:T(8,128)(2,1)}, bf16[258,128]{1,0:T(8,128)(2,1)}, ...), branch_computations={%region_1.1_spmd, %region_2.4_spmd} | conditional | flops 341860352 | bytes 25413872 | solution.py:99
  516.5 7.4 %conditional.3 = (f32[2,258,1024]{2,1,0:T(8,128)}) conditional(s32[]{:T(128)} %convert_element_type.75, f32[2,258,1024]{2,1,0:T(8,128)} %get-tuple-element.461, (s32[]{:T(128)}, s32[]{:T(128)}, f32[2,258,1024]{2,1,0:T(8,128)}, s32[]{:T(128)}, pred[]{:T(512)}, /*index=5*/bf16[8192,1024]{1,0:T(8,128)(2,1)}, bf16[258,128]{1,0:T(8,128)(2,1)}, ...), branch_computations={%region_1.1_spmd, %region_2.4_spmd} | conditional | flops 341860352 | bytes 25413872 | solution.py:99
  561.1 7.4 %conditional.3 = (f32[2,258,1024]{2,1,0:T(8,128)}) conditional(s32[]{:T(128)} %convert_element_type.75, f32[2,258,1024]{2,1,0:T(8,128)} %get-tuple-element.461, (s32[]{:T(128)}, s32[]{:T(128)}, f32[2,258,1024]{2,1,0:T(8,128)}, s32[]{:T(128)}, pred[]{:T(512)}, /*index=5*/bf16[8192,1024]{1,0:T(8,128)(2,1)}, bf16[258,128]{1,0:T(8,128)(2,1)}, ...), branch_computations={%region_1.1_spmd, %region_2.4_spmd} | conditional | flops 341860352 | bytes 25413872 | solution.py:99
  613.1 7.4 %conditional.3 = (f32[2,258,1024]{2,1,0:T(8,128)}) conditional(s32[]{:T(128)} %convert_element_type.75, f32[2,258,1024]{2,1,0:T(8,128)} %get-tuple-element.461, (s32[]{:T(128)}, s32[]{:T(128)}, f32[2,258,1024]{2,1,0:T(8,128)}, s32[]{:T(128)}, pred[]{:T(512)}, /*index=5*/bf16[8192,1024]{1,0:T(8,128)(2,1)}, bf16[258,128]{1,0:T(8,128)(2,1)}, ...), branch_computations={%region_1.1_spmd, %region_2.4_spmd} | conditional | flops 341860352 | bytes 25413872 | solution.py:99
  691.9 40.1 %reduce-scatter.2.cloned.1.call-done = bf16[256,1024]{1,0:T(8,128)(2,1)} async-done(((bf16[256,4096]{1,0:T(8,128)(2,1)}), bf16[256,1024]{1,0:T(8,128)(2,1)}) %reduce-scatter.2.cloned.1.call-update) | async-done | bytes 524304 | tf_op jit(solution)/shard_map/reduce_scatter | solution.py:107
  (490 shorter events, 636.9 us)
Async XLA Ops:
  6.5 193.3 %all-gather.2.cloned.1.call-start = ((), (), s32[]{:S(2)}) async-start(), calls=%async_computation.1 | async-start | bytes 17301504 | tf_op jit(solution)/shard_map/all_gather | solution.py:76
  7.3 724.8 %reduce-scatter.2.cloned.1.call-start = ((), (), s32[]{:S(2)}) async-start(), calls=%async_computation.2 | async-start | bytes 2621440 | tf_op jit(solution)/shard_map/reduce_scatter | solution.py:107
  679.9 4.9 copy-start
Sparse Core Ops, SparseCore 0:
  9.0 190.8 all-gather.1
  692.1 39.9 reduce-scatter.1
where the time goes:
time: 746 us; the launch traced here: 739 us
  other arithmetic  237 us (32%)
  waiting for transfers between devices  230 us (31%)
  matrix products  186 us (25%)
  local copies, waits for them, and re-layouts  68.5 us (9%)
  between operations  13.5 us (2%)
    all_gather x1, waiting for transfers between devices, per_device(): shard_rows = lax.all_gather(gated_value, 'ctx', axis=0, tiled=True)  189 us
    dot_general x129, matrix products, dot_plain(): return jnp.dot(left, right, preferred_element_type=jnp.float32)  174 us
    squeeze x64, other arithmetic, include(): low_part = lax.cond(source <= my_index, add_low, keep_low, inner[0])  120 us
    another operation x65, other arithmetic, include(): return jnp.stack([low_part, high_part])  97 us
    slice x65, local copies, waits for them, and re-layouts, filter_spectrum(): rolled = jnp.concatenate([jnp.zeros_like(window[:SPAN]), window[:SPAN]], 0)  66.8 us
    reduce_scatter x1, waiting for transfers between devices, per_device(): lax.psum_scatter(partial_sum.astype(jnp.bfloat16), 'ch', scatter_dimensio...  40.1 us
    concatenate x64, other arithmetic, complex_times(): jnp.concatenate([filt_real * src_real - filt_imag * src_imag, filt_real *...  15.8 us
  transfers between devices with their start and end apart: 2, of which 2 were waited for; matrix products, arithmetic and copies ran while one was open for 0% of the time, Pallas kernels for 0%

commit v1 on v0

v1 whole, which is shorter than its diff:
```python
import functools

import jax
import jax.numpy as jnp
import numpy as np
from jax import lax
from jax.experimental import pallas as pl
from jax.experimental.pallas import tpu as pltpu
from jax.sharding import PartitionSpec as P

SPAN = 128
BLOCKS = 64
HALF = BLOCKS // 2
LENGTH = SPAN * BLOCKS
GROUP = 32
SUB = 16
F32 = jnp.float32
BF16 = jnp.bfloat16


def tables():
    first = np.arange(BLOCKS)[:, None] + 0.25
    natural = np.arange(BLOCKS)[None, :]
    stored = np.concatenate([np.arange(HALF), BLOCKS - 1 - np.arange(HALF)])[None, :]

    def stage_a(order):
        angle = 2 * np.pi * first * order / BLOCKS
        return np.concatenate([np.cos(angle), -np.sin(angle)], 0)

    def stage_a_back(order):
        angle = (2 * np.pi * first * order / BLOCKS).T
        return np.concatenate([np.cos(angle), -np.sin(angle)], 1) / LENGTH

    twist = 2 * np.pi * first * np.arange(SPAN)[None, :] / LENGTH
    angle = 2 * np.pi * np.arange(SPAN)[:, None] * np.arange(SPAN)[None, :] / SPAN
    cos, sin = np.cos(angle), np.sin(angle)
    forth = np.block([[cos, -sin], [sin, cos]])
    back = np.block([[cos, sin], [-sin, cos]])
    rows = np.arange(HALF * SUB)
    swap = np.zeros((HALF * SUB, HALF * SUB))
    swap[(rows % SUB) * HALF + rows // SUB, rows] = 1.0
    bf = lambda a: jnp.asarray(a.astype(np.float32)).astype(BF16)
    return dict(
        a_filter=bf(stage_a(natural)),
        a_value=bf(stage_a(stored)),
        a_back=bf(stage_a_back(stored)),
        twist=jnp.asarray(np.concatenate([np.cos(twist), -np.sin(twist)], 1).astype(np.float32)),
        forth=bf(forth),
        back=bf(back),
        swap=bf(swap),
        unswap=bf(swap.T),
    )


def dot(left, right):
    return jnp.dot(left, right, preferred_element_type=F32)


def stage_a_rows(swapped, a_table, twist, mid_ref):
    t_re = jnp.concatenate([twist[:, :SPAN]] * 2, 1)
    t_im = jnp.concatenate([twist[:, SPAN:]] * 2, 1)
    for c in range(SUB):
        block = swapped[c * HALF : (c + 1) * HALF, :]
        rows = jnp.concatenate([block[:, : 2 * SPAN], block[:, 2 * SPAN :]], 0)
        spec = dot(a_table, rows)
        re, im = spec[:BLOCKS], spec[BLOCKS:]
        out_re = (re * t_re - im * t_im).astype(BF16)
        out_im = (re * t_im + im * t_re).astype(BF16)
        for g in range(2):
            at = (g * SUB + c) * BLOCKS
            mid_ref[at : at + BLOCKS, :SPAN] = out_re[:, g * SPAN : (g + 1) * SPAN]
            mid_ref[at : at + BLOCKS, SPAN:] = out_im[:, g * SPAN : (g + 1) * SPAN]


CHUNK = 512


def filter_kernel(which, h_ref, a_ref, twist_ref, forth_ref, swap_ref, out_ref, gather_ref, mid_ref):
    offset = (which[0] % 4) * GROUP
    rows = lax.broadcasted_iota(jnp.int32, (GROUP, SPAN), 0)
    lanes = lax.broadcasted_iota(jnp.int32, (GROUP, SPAN), 1)
    pick = jnp.where(lanes == rows + offset, 1.0, 0.0).astype(BF16)
    for a in range(HALF):
        for half in range(2):
            at = (half * HALF + a) * SPAN
            turned = lax.dot_general(
                pick, h_ref[at : at + SPAN, :], (((1,), (1,)), ((), ())), preferred_element_type=F32
            ).astype(BF16)
            for g in range(2):
                lane = (half * 2 + g) * SPAN
                gather_ref[a * SUB : (a + 1) * SUB, lane : lane + SPAN] = turned[g * SUB : (g + 1) * SUB]
    swapped = dot(swap_ref[...], gather_ref[...]).astype(BF16)
    stage_a_rows(swapped, a_ref[...], twist_ref[...], mid_ref)
    for k in range(GROUP * BLOCKS // CHUNK):
        part = slice(k * CHUNK, (k + 1) * CHUNK)
        out_ref[part, :] = dot(mid_ref[part, :], forth_ref[...]).astype(out_ref.dtype)


def conv_kernel(
    x_ref, spec_ref, a_ref, a_back_ref, twist_ref, forth_ref, back_ref, swap_ref, unswap_ref, out_ref, mid_ref, turn_ref
):
    pieces = []
    for half in range(2):
        for g in range(2):
            piece = x_ref[:, g * SUB : (g + 1) * SUB, half * SPAN : (half + 1) * SPAN]
            pieces.append(piece.reshape(HALF * SUB, SPAN))
    swapped = dot(swap_ref[...], jnp.concatenate(pieces, 1)).astype(BF16)
    twist = twist_ref[...]
    stage_a_rows(swapped, a_ref[...], twist, mid_ref)
    t_re = jnp.concatenate([twist[:, :SPAN]] * (CHUNK // BLOCKS), 0)
    t_im = jnp.concatenate([twist[:, SPAN:]] * (CHUNK // BLOCKS), 0)
    for k in range(GROUP * BLOCKS // CHUNK):
        part = slice(k * CHUNK, (k + 1) * CHUNK)
        spec = dot(mid_ref[part, :], forth_ref[...])
        x_re, x_im = spec[:, :SPAN], spec[:, SPAN:]
        h = spec_ref[part, :].astype(F32)
        h_re, h_im = h[:, :SPAN], h[:, SPAN:]
        prod = jnp.concatenate([x_re * h_re - x_im * h_im, x_re * h_im + x_im * h_re], 1).astype(BF16)
        turn = dot(prod, back_ref[...])
        re, im = turn[:, :SPAN], turn[:, SPAN:]
        mid_ref[part, :SPAN] = (re * t_re + im * t_im).astype(BF16)
        mid_ref[part, SPAN:] = (im * t_re - re * t_im).astype(BF16)
    for c in range(SUB):
        sides = []
        for g in range(2):
            at = (g * SUB + c) * BLOCKS
            sides.append(
                jnp.concatenate([mid_ref[at : at + BLOCKS, :SPAN], mid_ref[at : at + BLOCKS, SPAN:]], 0)
            )
        y = dot(a_back_ref[...], jnp.concatenate(sides, 1)).astype(BF16)
        turn_ref[c * HALF : (c + 1) * HALF, : 2 * SPAN] = y[:HALF]
        turn_ref[c * HALF : (c + 1) * HALF, 2 * SPAN :] = y[HALF:]
    result = dot(unswap_ref[...], turn_ref[...]).astype(BF16)
    for half in range(2):
        for g in range(2):
            lane = (half * 2 + g) * SPAN
            out_ref[:, g * SUB : (g + 1) * SUB, half * SPAN : (half + 1) * SPAN] = result[:, lane : lane + SPAN].reshape(
                HALF, SUB, SPAN
            )


def full(shape):
    return pl.BlockSpec(shape, lambda *_: (0,) * len(shape))


def filter_spectrum(which, long_filter, t):
    return pl.pallas_call(
        filter_kernel,
        out_shape=jax.ShapeDtypeStruct((GROUP * BLOCKS, 2 * SPAN), BF16),
        grid_spec=pltpu.PrefetchScalarGridSpec(
            num_scalar_prefetch=1,
            grid=(1,),
            in_specs=[
                pl.BlockSpec((LENGTH, SPAN), lambda i, w: (0, w[0] // 4)),
                full((2 * BLOCKS, BLOCKS)),
                full((BLOCKS, 2 * SPAN)),
                full((2 * SPAN, 2 * SPAN)),
                full((HALF * SUB, HALF * SUB)),
            ],
            out_specs=full((GROUP * BLOCKS, 2 * SPAN)),
            scratch_shapes=[
                pltpu.VMEM((HALF * SUB, 4 * SPAN), BF16),
                pltpu.VMEM((GROUP * BLOCKS, 2 * SPAN), BF16),
            ],
        ),
        compiler_params=pltpu.CompilerParams(vmem_limit_bytes=32 << 20),
        name="filter_spectrum",
    )(which, long_filter, t["a_filter"], t["twist"], t["forth"], t["swap"])


def convolve(x, spec, t):
    return pl.pallas_call(
        conv_kernel,
        out_shape=jax.ShapeDtypeStruct((HALF, GROUP, 2 * SPAN), BF16),
        scratch_shapes=[
            pltpu.VMEM((GROUP * BLOCKS, 2 * SPAN), BF16),
            pltpu.VMEM((HALF * SUB, 4 * SPAN), BF16),
        ],
        compiler_params=pltpu.CompilerParams(vmem_limit_bytes=32 << 20),
        name="convolve",
    )(x, spec, t["a_value"], t["a_back"], t["twist"], t["forth"], t["back"], t["swap"], t["unswap"])


def gate_kernel(y_ref, gate_ref, out_ref):
    turned = jnp.transpose(y_ref[...], (1, 0))
    out_ref[...] = (gate_ref[...].astype(F32) * turned.astype(F32)).astype(BF16)


def gate_mix(y, gate):
    return pl.pallas_call(
        gate_kernel,
        out_shape=jax.ShapeDtypeStruct(gate.shape, BF16),
        compiler_params=pltpu.CompilerParams(vmem_limit_bytes=32 << 20),
        name="gate_mix",
    )(y, gate)


def project_kernel(order, mix_ref, w_ref, out_ref):
    out_ref[0] = dot(mix_ref[...], w_ref[...]).astype(BF16)


def project(order, mix, weight):
    tokens, inner = mix.shape
    chunks = order.shape[0]
    cols = weight.shape[1] // 4
    return pl.pallas_call(
        project_kernel,
        out_shape=jax.ShapeDtypeStruct((chunks, tokens, cols), BF16),
        grid_spec=pltpu.PrefetchScalarGridSpec(
            num_scalar_prefetch=1,
            grid=(chunks,),
            in_specs=[
                pl.BlockSpec((tokens, inner), lambda j, o: (0, 0)),
                pl.BlockSpec((inner, cols), lambda j, o: (0, o[j])),
            ],
            out_specs=pl.BlockSpec((1, tokens, cols), lambda j, o: (j, 0, 0)),
        ),
        compiler_params=pltpu.CompilerParams(vmem_limit_bytes=32 << 20),
        name="project",
    )(order, mix, weight)


CORE_PAIR = [(0, 1), (1, 0), (2, 3), (3, 2)]
CHIP_PAIR = [(0, 2), (2, 0), (1, 3), (3, 1)]


def per_device(query_gate, gated_value, long_filter, out_weight):
    t = tables()
    me = lax.axis_index("ctx")
    mine = lax.axis_index("ch")
    tokens, width = gated_value.shape
    turned = gated_value.T.reshape(HALF, GROUP, tokens)
    x = lax.all_to_all(turned, "ctx", 0, 0, tiled=True)
    spec = filter_spectrum(me.reshape(1), long_filter, t)
    y = convolve(x, spec, t)
    y = lax.all_to_all(y, "ctx", 0, 0, tiled=True).reshape(width, tokens)
    mix = gate_mix(y, query_gate)
    away = project(jnp.stack([mine ^ 3, mine ^ 2]), mix, out_weight)
    home = project(jnp.stack([mine ^ 1, mine]), mix, out_weight)
    away_in = lax.ppermute(away[0], "ch", CORE_PAIR)
    away_sum = (away[1].astype(F32) + away_in.astype(F32)).astype(BF16)
    far = lax.ppermute(away_sum, "ch", CHIP_PAIR)
    near = lax.ppermute(home[0], "ch", CORE_PAIR)
    return (home[1].astype(F32) + near.astype(F32) + far.astype(F32)).astype(BF16)


def solution(mesh):
    placed = (P("ctx", "ch"), P("ctx", "ch"), P(None, "ch"), P("ch", None))
    return jax.shard_map(
        per_device, mesh=mesh, in_specs=placed, out_specs=P("ctx", "ch"), check_vma=False
    )
```

time: 746 us -> 75 us (0.10)
  other arithmetic: 237 us -> 1.41 us
  waiting for transfers between devices: 230 us -> 21 us
  matrix products: 186 us -> 0 us
  local copies, waits for them, and re-layouts: 68.5 us -> 18.3 us
  starting transfers between devices: 0.04 us -> 23.5 us
  between operations: 13.5 us -> 0.22 us
  Pallas kernels: 0 us -> 9.87 us
    all_gather x1 -> x0, waiting for transfers between devices: 189 us -> none  [per_device(): shard_rows = lax.all_gather(gated_value, 'ctx', axis=0, tiled=True)]
    dot_general x132 -> x0, matrix products: 186 us -> none  [the longest x129 174 us: dot_plain(): return jnp.dot(left, right, preferred_element_type=jnp.float32)]
    squeeze x64 -> x0, other arithmetic: 120 us -> none  [include(): low_part = lax.cond(source <= my_index, add_low, keep_low, inner[0])]
    another operation x67 -> x2, other arithmetic: 97.9 us -> 0.15 us  [the longest x1 0.08 us: per_device(): away = project(jnp.stack([mine ^ 3, mine ^ 2]), mix, out_weight)]
    slice x65 -> x0, local copies, waits for them, and re-layouts: 66.8 us -> none  [filter_spectrum(): rolled = jnp.concatenate([jnp.zeros_like(window[:SPAN]), window[:SPAN]], 0)]
    reduce_scatter x1 -> x0, waiting for transfers between devices: 40.1 us -> none  [per_device(): lax.psum_scatter(partial_sum.astype(jnp.bfloat16), 'ch', scatter_dimensio...]
    all_to_all x0 -> x2, starting transfers between devices: none -> 17.5 us  [the longest x1 9.73 us: per_device(): x = lax.all_to_all(turned, 'ctx', 0, 0, tiled=True)]
    concatenate x66 -> x0, other arithmetic: 17.2 us -> none  [the longest x64 15.8 us: complex_times(): jnp.concatenate([filt_real * src_real - filt_imag * src_imag, filt_real *...]
  transfers between devices with their start and end apart: 2 -> 5, of which waited for: 2 -> 2; matrix products, arithmetic and copies ran while one was open for 0% -> 1% of each run, Pallas kernels for 0% -> 6%
where the time goes in v1:
time: 75 us; the launch traced here: 74.4 us
  starting transfers between devices  23.5 us (31%)
  waiting for transfers between devices  21 us (28%)
  local copies, waits for them, and re-layouts  18.3 us (24%)
  Pallas kernels  9.87 us (13%)
  other arithmetic  1.41 us (2%)
    unnamed x30, local copies, waits for them, and re-layouts  16.1 us
    ppermute x1, waiting for transfers between devices, per_device(): far = lax.ppermute(away_sum, 'ch', CHIP_PAIR)  11.9 us
    all_to_all x1, starting transfers between devices, per_device(): x = lax.all_to_all(turned, 'ctx', 0, 0, tiled=True)  9.73 us
    all_to_all x1, waiting for transfers between devices, per_device(): y = lax.all_to_all(y, 'ctx', 0, 0, tiled=True).reshape(width, tokens)  9.15 us
    all_to_all x1, starting transfers between devices, per_device(): y = lax.all_to_all(y, 'ctx', 0, 0, tiled=True).reshape(width, tokens)  7.74 us
    pallas_call x2, Pallas kernels, project(): pl.pallas_call(project_kernel, out_shape=jax.ShapeDtypeStruct((chunks, to...  4.58 us
    ppermute x1, starting transfers between devices, per_device(): away_in = lax.ppermute(away[0], 'ch', CORE_PAIR)  3.23 us
    pallas_call x1, Pallas kernels, convolve(): pl.pallas_call(conv_kernel, out_shape=jax.ShapeDtypeStruct((HALF, GROUP,...  2.84 us
  transfers between devices with their start and end apart: 5, of which 2 were waited for; matrix products, arithmetic and copies ran while one was open for 1% of the time, Pallas kernels for 6%

profile of v1, /device:TPU:1, one launch (start us, length us, event | category | flops | bytes accessed | tf_op | source)
XLA Modules:
  0.0 74.4 jit_solution(7568564534768435626)
XLA Ops:
  0.0 0.0 copy-start.10
  0.0 0.0 copy-start.6
  0.0 0.0 copy-start.4
  0.0 0.0 copy-start.12
  0.0 0.0 copy-start.14
  0.0 0.0 copy-start.11
  0.0 0.0 copy-start.8
  0.1 0.0 copy-start.7
  0.1 2.2 %copy.13 = bf16[1024,256]{1,0:T(8,128)(2,1)} copy(bf16[1024,256]{0,1:T(8,128)(2,1)} %bitcast.23) | data formatting | bytes 1048576 | tf_op jit(solution)/shard_map/transpose | solution.py:232
  2.2 9.7 %all-to-all-start = ((bf16[32,32,256]{2,1,0:T(8,128)(2,1)}), bf16[32,32,256]{2,1,0:T(8,128)(2,1)S(1)}, u32[]{:S(2)}, u32[]{:S(2)}) async-start(bf16[32,32,256]{2,1,0:T(8,128)(2,1)} %bitcast.3), calls=%async_computation | async-start | bytes 1048576 | tf_op jit(solution)/shard_map/all_to_all | solution.py:233
  12.0 0.0 copy-start.2
  12.0 5.8 %copy-done.2 = bf16[8192,1024]{1,0:T(8,128)(2,1)S(1)} copy-done((bf16[8192,1024]{1,0:T(8,128)(2,1)S(1)}, bf16[8192,1024]{1,0:T(8,128)(2,1)}, u32[]{:S(2)}) %copy-start.2) | copy-done | bytes 16777240
  17.8 0.0 copy-start.3
  17.8 1.0 %copy-done.3 = bf16[512,512]{1,0:T(8,128)(2,1)S(1)} copy-done((bf16[512,512]{1,0:T(8,128)(2,1)S(1)}, bf16[512,512]{1,0:T(8,128)(2,1)}, u32[]{:S(2)}) %copy-start.3) | copy-done | bytes 524312
  18.8 0.0 copy-start.5
  18.8 0.9 %copy-done.5 = bf16[256,256]{1,0:T(8,128)(2,1)S(1)} copy-done((bf16[256,256]{1,0:T(8,128)(2,1)S(1)}, bf16[256,256]{1,0:T(8,128)(2,1)}, u32[]{:S(2)}) %copy-start.5) | copy-done | bytes 131096
  19.7 0.0 copy-start.9
  19.7 0.8 %copy-done.9 = f32[64,256]{1,0:T(8,128)S(1)} copy-done((f32[64,256]{1,0:T(8,128)S(1)}, f32[64,256]{1,0:T(8,128)}, u32[]{:S(2)}) %copy-start.9) | copy-done | bytes 65560
  20.5 0.8 %copy-done.13 = bf16[128,64]{1,0:T(8,128)(2,1)S(1)} copy-done((bf16[128,64]{1,0:T(8,128)(2,1)S(1)}, bf16[128,64]{1,0:T(8,128)(2,1)}, u32[]{:S(2)}) %copy-start.13) | copy-done | bytes 16408
  21.3 2.2 %filter_spectrum.1.spec_ref = bf16[2048,256]{1,0:T(8,128)(2,1)S(1)} custom-call(s32[1]{0:T(128)} %bitcast.4.which, bf16[8192,1024]{1,0:T(8,128)(2,1)S(1)} %copy-done.2, bf16[128,64]{1,0:T(8,128)(2,1)S(1)} %copy-done.13, f32[64,256]{1,0:T(8,128)S(1)} %copy-done.9, bf16[256,256]{1,0:T(8,128)(2,1)S(1)} %copy-done.5, bf16[512,512]{1,0:T(8,128)(2,1)S(1)} %copy-done.3), custom_call_target="tpu_custom_call" | custom-call | tf_op jit(solution)/shard_map/filter_spectrum/pallas_call | solution.py:147
  23.6 0.0 all-to-all-done.x_ref
  23.6 0.0 copy-done.10
  23.6 0.0 copy-done.6
  23.6 0.0 copy-done.4
  23.6 0.0 copy-done.12
  23.6 0.0 copy-done.14
  23.6 0.0 copy-done.11
  23.6 0.0 copy-done.8
  23.6 2.8 %convolve.1 = bf16[32,32,256]{2,1,0:T(8,128)(2,1)} custom-call(bf16[32,32,256]{2,1,0:T(8,128)(2,1)S(1)} %all-to-all-done.x_ref, bf16[2048,256]{1,0:T(8,128)(2,1)S(1)} %filter_spectrum.1.spec_ref, bf16[128,64]{1,0:T(8,128)(2,1)S(1)} %copy-done.12, bf16[64,128]{1,0:T(8,128)(2,1)S(1)} %copy-done.14, f32[64,256]{1,0:T(8,128)S(1)} %copy-done.10, ...), custom_call_target="tpu_custom_call" | custom-call | tf_op jit(solution)/shard_map/convolve/pallas_call | solution.py:172
  26.5 7.7 %all-to-all-start.1 = ((bf16[32,32,256]{2,1,0:T(8,128)(2,1)}), bf16[32,32,256]{2,1,0:T(8,128)(2,1)S(1)}, u32[]{:S(2)}, u32[]{:S(2)}) async-start(bf16[32,32,256]{2,1,0:T(8,128)(2,1)} %convolve.1), calls=%async_computation.1 | async-start | bytes 1048576 | tf_op jit(solution)/shard_map/all_to_all | solution.py:236
  34.2 0.1 pad_add_fusion.1.order
  34.3 9.1 %all-to-all-done.1 = bf16[32,32,256]{2,1,0:T(8,128)(2,1)S(1)} async-done(((bf16[32,32,256]{2,1,0:T(8,128)(2,1)}), bf16[32,32,256]{2,1,0:T(8,128)(2,1)S(1)}, u32[]{:S(2)}, u32[]{:S(2)}) %all-to-all-start.1) | async-done | bytes 524320 | tf_op jit(solution)/shard_map/all_to_all | solution.py:236
  43.4 0.0 copy-done.7
  43.4 0.2 gate_mix.1.mix_ref
  43.7 0.0 copy-start
  43.7 3.4 %copy-done = bf16[1024,4096]{1,0:T(8,128)(2,1)S(1)} copy-done((bf16[1024,4096]{1,0:T(8,128)(2,1)S(1)}, bf16[1024,4096]{1,0:T(8,128)(2,1)}, u32[]{:S(2)}) %copy-start) | copy-done | bytes 8388632
  47.1 2.3 %project.3 = bf16[2,256,1024]{2,1,0:T(8,128)(2,1)S(1)} custom-call(s32[2]{0:T(128)S(1)} %pad_add_fusion.1.order, bf16[256,1024]{1,0:T(8,128)(2,1)S(1)} %gate_mix.1.mix_ref, bf16[1024,4096]{1,0:T(8,128)(2,1)S(1)} %copy-done), custom_call_target="tpu_custom_call" | custom-call | tf_op jit(solution)/shard_map/project/pallas_call | solution.py:206
  49.4 3.2 %collective-permute-start.1 = (bf16[256,1024]{1,0:T(8,128)(2,1)S(1)}, bf16[256,1024]{1,0:T(8,128)(2,1)S(1)}, u32[]{:S(2)}, u32[]{:S(2)}) collective-permute-start(bf16[256,1024]{1,0:T(8,128)(2,1)S(1)} %slice_bitcast_fusion), channel_id=1, source_target_pairs={{0,1},{1,0},{2,3},{3,2},{4,5},{5,4},{6,7},{7,6},{8,9},{9,8},{10,11... | collective-permute-start | bytes 1572872 | tf_op jit(solution)/shard_map/ppermute | solution.py:240
  52.6 0.1 pad_add_fusion.order
  52.7 3.4 %copy-done.1 = bf16[1024,4096]{1,0:T(8,128)(2,1)S(1)} copy-done((bf16[1024,4096]{1,0:T(8,128)(2,1)S(1)}, bf16[1024,4096]{1,0:T(8,128)(2,1)}, u32[]{:S(2)}) %copy-start.1) | copy-done | bytes 8388632
  56.1 2.3 %project.2 = bf16[2,256,1024]{2,1,0:T(8,128)(2,1)S(1)} custom-call(s32[2]{0:T(128)S(1)} %pad_add_fusion.order, bf16[256,1024]{1,0:T(8,128)(2,1)S(1)} %gate_mix.1.mix_ref, bf16[1024,4096]{1,0:T(8,128)(2,1)S(1)} %copy-done.1), custom_call_target="tpu_custom_call" | custom-call | tf_op jit(solution)/shard_map/project/pallas_call | solution.py:206
  58.4 0.1 collective-permute-start
  58.5 0.0 collective-permute-done.1
  58.5 0.2 fusion
  58.7 2.7 %collective-permute-start.2 = (bf16[256,1024]{1,0:T(8,128)(2,1)S(1)}, bf16[256,1024]{1,0:T(8,128)(2,1)S(1)}, u32[]{:S(2)}, u32[]{:S(2)}) collective-permute-start(bf16[256,1024]{1,0:T(8,128)(2,1)S(1)} %fusion), channel_id=1, source_target_pairs={{0,2},{2,0},{1,3},{3,1},{4,6},{6,4},{5,7},{7,5},{8,10},{10,8},{9,1... | collective-permute-start | bytes 1572872 | tf_op jit(solution)/shard_map/ppermute | solution.py:242
  61.4 0.0 collective-permute-done
  61.4 11.9 %collective-permute-done.2 = bf16[256,1024]{1,0:T(8,128)(2,1)S(1)} collective-permute-done((bf16[256,1024]{1,0:T(8,128)(2,1)S(1)}, bf16[256,1024]{1,0:T(8,128)(2,1)S(1)}, u32[]{:S(2)}, u32[]{:S(2)}) %collective-permute-start.2) | collective-permute-done | bytes 524320 | tf_op jit(solution)/shard_map/ppermute | solution.py:242
  73.3 1.1 %fusion.2 = bf16[256,1024]{1,0:T(8,128)(2,1)} fusion(bf16[256,1024]{1,0:T(8,128)(2,1)S(1)} %collective-permute-done.2, bf16[256,1024]{1,0:T(8,128)(2,1)S(1)} %collective-permute-done, bf16[2,256,1024]{2,1,0:T(8,128)(2,1)S(1)} %project.2), kind=kLoop, calls=%fused_computation.4 | loop fusion | flops 1572864 | bytes 2097152 | tf_op jit(solution)/shard_map/convert_element_type | solution.py:244
  (4 shorter events, 0.1 us)
Async XLA Ops:
  0.0 23.6 %copy-start.10 = (f32[64,256]{1,0:T(8,128)S(1)}, f32[64,256]{1,0:T(8,128)}, u32[]{:S(2)}) copy-start(f32[64,256]{1,0:T(8,128)} %constant.34.clone.twist_ref) | copy-start | bytes 196612
  0.0 23.6 %copy-start.6 = (bf16[256,256]{1,0:T(8,128)(2,1)S(1)}, bf16[256,256]{1,0:T(8,128)(2,1)}, u32[]{:S(2)}) copy-start(bf16[256,256]{1,0:T(8,128)(2,1)} %constant.40.forth_ref) | copy-start | bytes 393220
  0.0 23.6 %copy-start.4 = (bf16[512,512]{1,0:T(8,128)(2,1)S(1)}, bf16[512,512]{1,0:T(8,128)(2,1)}, u32[]{:S(2)}) copy-start(bf16[512,512]{1,0:T(8,128)(2,1)} %constant.41.swap_ref) | copy-start | bytes 1572868
  0.0 23.6 %copy-start.12 = (bf16[128,64]{1,0:T(8,128)(2,1)S(1)}, bf16[128,64]{1,0:T(8,128)(2,1)}, u32[]{:S(2)}) copy-start(bf16[128,64]{1,0:T(8,128)(2,1)} %constant.42.a_ref) | copy-start | bytes 49156
  0.0 23.6 %copy-start.14 = (bf16[64,128]{1,0:T(8,128)(2,1)S(1)}, bf16[64,128]{1,0:T(8,128)(2,1)}, u32[]{:S(2)}) copy-start(bf16[64,128]{1,0:T(8,128)(2,1)} %constant.43.a_back_ref) | copy-start | bytes 49156
  0.0 23.6 %copy-start.11 = (bf16[256,256]{1,0:T(8,128)(2,1)S(1)}, bf16[256,256]{1,0:T(8,128)(2,1)}, u32[]{:S(2)}) copy-start(bf16[256,256]{1,0:T(8,128)(2,1)} %constant.44.back_ref) | copy-start | bytes 393220
  0.0 23.6 %copy-start.8 = (bf16[512,512]{1,0:T(8,128)(2,1)S(1)}, bf16[512,512]{1,0:T(8,128)(2,1)}, u32[]{:S(2)}) copy-start(bf16[512,512]{1,0:T(8,128)(2,1)} %constant.45.unswap_ref) | copy-start | bytes 1572868
  0.1 43.4 %copy-start.7 = (bf16[256,1024]{1,0:T(8,128)(2,1)S(1)}, bf16[256,1024]{1,0:T(8,128)(2,1)}, u32[]{:S(2)}) copy-start(bf16[256,1024]{1,0:T(8,128)(2,1)} %gate_ref.1) | copy-start | bytes 1572868
  2.2 21.3 %all-to-all-start = ((bf16[32,32,256]{2,1,0:T(8,128)(2,1)}), bf16[32,32,256]{2,1,0:T(8,128)(2,1)S(1)}, u32[]{:S(2)}, u32[]{:S(2)}) async-start(bf16[32,32,256]{2,1,0:T(8,128)(2,1)} %bitcast.3), calls=%async_computation | async-start | bytes 1048576 | tf_op jit(solution)/shard_map/all_to_all | solution.py:233
  12.0 5.8 %copy-start.2 = (bf16[8192,1024]{1,0:T(8,128)(2,1)S(1)}, bf16[8192,1024]{1,0:T(8,128)(2,1)}, u32[]{:S(2)}) copy-start(bf16[8192,1024]{1,0:T(8,128)(2,1)} %h_ref.1) | copy-start | bytes 50331652
  17.8 1.0 %copy-start.3 = (bf16[512,512]{1,0:T(8,128)(2,1)S(1)}, bf16[512,512]{1,0:T(8,128)(2,1)}, u32[]{:S(2)}) copy-start(bf16[512,512]{1,0:T(8,128)(2,1)} %constant.41.swap_ref) | copy-start | bytes 1572868
  18.8 0.9 %copy-start.5 = (bf16[256,256]{1,0:T(8,128)(2,1)S(1)}, bf16[256,256]{1,0:T(8,128)(2,1)}, u32[]{:S(2)}) copy-start(bf16[256,256]{1,0:T(8,128)(2,1)} %constant.40.forth_ref) | copy-start | bytes 393220
  19.7 0.8 %copy-start.9 = (f32[64,256]{1,0:T(8,128)S(1)}, f32[64,256]{1,0:T(8,128)}, u32[]{:S(2)}) copy-start(f32[64,256]{1,0:T(8,128)} %constant.34.clone.twist_ref) | copy-start | bytes 196612
  20.5 0.8 %copy-start.13 = (bf16[128,64]{1,0:T(8,128)(2,1)S(1)}, bf16[128,64]{1,0:T(8,128)(2,1)}, u32[]{:S(2)}) copy-start(bf16[128,64]{1,0:T(8,128)(2,1)} %constant.39.a_ref) | copy-start | bytes 49156
  26.5 17.0 %all-to-all-start.1 = ((bf16[32,32,256]{2,1,0:T(8,128)(2,1)}), bf16[32,32,256]{2,1,0:T(8,128)(2,1)S(1)}, u32[]{:S(2)}, u32[]{:S(2)}) async-start(bf16[32,32,256]{2,1,0:T(8,128)(2,1)} %convolve.1), calls=%async_computation.1 | async-start | bytes 1048576 | tf_op jit(solution)/shard_map/all_to_all | solution.py:236
  43.7 3.4 %copy-start = (bf16[1024,4096]{1,0:T(8,128)(2,1)S(1)}, bf16[1024,4096]{1,0:T(8,128)(2,1)}, u32[]{:S(2)}) copy-start(bf16[1024,4096]{1,0:T(8,128)(2,1)} %w_ref.3) | copy-start | bytes 25165828
  49.4 9.1 %collective-permute-start.1 = (bf16[256,1024]{1,0:T(8,128)(2,1)S(1)}, bf16[256,1024]{1,0:T(8,128)(2,1)S(1)}, u32[]{:S(2)}, u32[]{:S(2)}) collective-permute-start(bf16[256,1024]{1,0:T(8,128)(2,1)S(1)} %slice_bitcast_fusion), channel_id=1, source_target_pairs={{0,1},{1,0},{2,3},{3,2},{4,5},{5,4},{6,7},{7,6},{8,9},{9,8},{10,11... | collective-permute-start | bytes 1572872 | tf_op jit(solution)/shard_map/ppermute | solution.py:240
  52.7 3.4 %copy-start.1 = (bf16[1024,4096]{1,0:T(8,128)(2,1)S(1)}, bf16[1024,4096]{1,0:T(8,128)(2,1)}, u32[]{:S(2)}) copy-start(bf16[1024,4096]{1,0:T(8,128)(2,1)} %w_ref.3) | copy-start | bytes 25165828
  58.4 3.0 %collective-permute-start = (bf16[256,1024]{1,0:T(8,128)(2,1)S(1)}, bf16[256,1024]{1,0:T(8,128)(2,1)S(1)}, u32[]{:S(2)}, u32[]{:S(2)}) collective-permute-start(bf16[256,1024]{1,0:T(8,128)(2,1)S(1)} %slice_bitcast_fusion.2), channel_id=1, source_target_pairs={{0,1},{1,0},{2,3},{3,2},{4,5},{5,4},{6,7},{7,6},{8,9},{9,8},{10,11... | collective-permute-start | bytes 1572872 | tf_op jit(solution)/shard_map/ppermute | solution.py:243
  58.7 14.6 %collective-permute-start.2 = (bf16[256,1024]{1,0:T(8,128)(2,1)S(1)}, bf16[256,1024]{1,0:T(8,128)(2,1)S(1)}, u32[]{:S(2)}, u32[]{:S(2)}) collective-permute-start(bf16[256,1024]{1,0:T(8,128)(2,1)S(1)} %fusion), channel_id=1, source_target_pairs={{0,2},{2,0},{1,3},{3,1},{4,6},{6,4},{5,7},{7,5},{8,10},{10,8},{9,1... | collective-permute-start | bytes 1572872 | tf_op jit(solution)/shard_map/ppermute | solution.py:242

commit v2 on v1

--- a/solution.py
+++ b/solution.py
@@ -75,20 +75,43 @@
 CHUNK = 512
 
 
-def filter_kernel(which, h_ref, a_ref, twist_ref, forth_ref, swap_ref, out_ref, gather_ref, mid_ref):
+SLABS = 8
+
+
+def filter_kernel(
+    which, h_hbm, a_hbm, twist_hbm, forth_hbm, swap_hbm, out_ref,
+    slab_ref, a_ref, twist_ref, forth_ref, swap_ref, gather_ref, mid_ref, slab_sem, table_sem,
+):
+    lane_block = pl.multiple_of((which[0] // 4) * SPAN, SPAN)
+    piece = LENGTH // SLABS
+    slabs = [
+        pltpu.make_async_copy(
+            h_hbm.at[pl.ds(k * piece, piece), pl.ds(lane_block, SPAN)],
+            slab_ref.at[pl.ds(k * piece, piece), :],
+            slab_sem.at[k],
+        )
+        for k in range(SLABS)
+    ]
+    pairs = [(a_hbm, a_ref), (twist_hbm, twist_ref), (forth_hbm, forth_ref), (swap_hbm, swap_ref)]
+    loads = [pltpu.make_async_copy(s, d, table_sem.at[k]) for k, (s, d) in enumerate(pairs)]
+    for copy in slabs + loads:
+        copy.start()
     offset = (which[0] % 4) * GROUP
     rows = lax.broadcasted_iota(jnp.int32, (GROUP, SPAN), 0)
     lanes = lax.broadcasted_iota(jnp.int32, (GROUP, SPAN), 1)
     pick = jnp.where(lanes == rows + offset, 1.0, 0.0).astype(BF16)
-    for a in range(HALF):
-        for half in range(2):
-            at = (half * HALF + a) * SPAN
-            turned = lax.dot_general(
-                pick, h_ref[at : at + SPAN, :], (((1,), (1,)), ((), ())), preferred_element_type=F32
-            ).astype(BF16)
-            for g in range(2):
-                lane = (half * 2 + g) * SPAN
-                gather_ref[a * SUB : (a + 1) * SUB, lane : lane + SPAN] = turned[g * SUB : (g + 1) * SUB]
+    for block in range(BLOCKS):
+        if block % (BLOCKS // SLABS) == 0:
+            slabs[block // (BLOCKS // SLABS)].wait()
+        half, a = divmod(block, HALF)
+        turned = lax.dot_general(
+            pick, slab_ref[block * SPAN : (block + 1) * SPAN, :], (((1,), (1,)), ((), ())), preferred_element_type=F32
+        ).astype(BF16)
+        for g in range(2):
+            lane = (half * 2 + g) * SPAN
+            gather_ref[a * SUB : (a + 1) * SUB, lane : lane + SPAN] = turned[g * SUB : (g + 1) * SUB]
+    for copy in loads:
+        copy.wait()
     swapped = dot(swap_ref[...], gather_ref[...]).astype(BF16)
     stage_a_rows(swapped, a_ref[...], twist_ref[...], mid_ref)
     for k in range(GROUP * BLOCKS // CHUNK):
@@ -139,33 +162,30 @@
             )
 
 
-def full(shape):
-    return pl.BlockSpec(shape, lambda *_: (0,) * len(shape))
+def in_hbm(*arrays):
+    return tuple(pltpu.with_memory_space_constraint(a, pltpu.HBM) for a in arrays)
 
 
 def filter_spectrum(which, long_filter, t):
     return pl.pallas_call(
         filter_kernel,
         out_shape=jax.ShapeDtypeStruct((GROUP * BLOCKS, 2 * SPAN), BF16),
-        grid_spec=pltpu.PrefetchScalarGridSpec(
-            num_scalar_prefetch=1,
-            grid=(1,),
-            in_specs=[
-                pl.BlockSpec((LENGTH, SPAN), lambda i, w: (0, w[0] // 4)),
-                full((2 * BLOCKS, BLOCKS)),
-                full((BLOCKS, 2 * SPAN)),
-                full((2 * SPAN, 2 * SPAN)),
-                full((HALF * SUB, HALF * SUB)),
-            ],
-            out_specs=full((GROUP * BLOCKS, 2 * SPAN)),
-            scratch_shapes=[
-                pltpu.VMEM((HALF * SUB, 4 * SPAN), BF16),
-                pltpu.VMEM((GROUP * BLOCKS, 2 * SPAN), BF16),
-            ],
-        ),
+        in_specs=[pl.BlockSpec(memory_space=pltpu.SMEM)] + [pl.BlockSpec(memory_space=pltpu.HBM)] * 5,
+        out_specs=pl.BlockSpec(memory_space=pltpu.VMEM),
+        scratch_shapes=[
+            pltpu.VMEM((LENGTH, SPAN), BF16),
+            pltpu.VMEM((2 * BLOCKS, BLOCKS), BF16),
+            pltpu.VMEM((BLOCKS, 2 * SPAN), F32),
+            pltpu.VMEM((2 * SPAN, 2 * SPAN), BF16),
+            pltpu.VMEM((HALF * SUB, HALF * SUB), BF16),
+            pltpu.VMEM((HALF * SUB, 4 * SPAN), BF16),
+            pltpu.VMEM((GROUP * BLOCKS, 2 * SPAN), BF16),
+            pltpu.SemaphoreType.DMA((SLABS,)),
+            pltpu.SemaphoreType.DMA((4,)),
+        ],
         compiler_params=pltpu.CompilerParams(vmem_limit_bytes=32 << 20),
         name="filter_spectrum",
-    )(which, long_filter, t["a_filter"], t["twist"], t["forth"], t["swap"])
+    )(which, *in_hbm(long_filter, t["a_filter"], t["twist"], t["forth"], t["swap"]))
 
 
 def convolve(x, spec, t):
@@ -181,43 +201,101 @@
     )(x, spec, t["a_value"], t["a_back"], t["twist"], t["forth"], t["back"], t["swap"], t["unswap"])
 
 
-def gate_kernel(y_ref, gate_ref, out_ref):
+def turn_kernel(v_hbm, out_ref, in_ref, sem):
+    width = v_hbm.shape[1] // 4
+    copies = [
+        pltpu.make_async_copy(v_hbm.at[:, pl.ds(k * width, width)], in_ref.at[k], sem.at[k]) for k in range(4)
+    ]
+    for copy in copies:
+        copy.start()
+    for k in range(4):
+        copies[k].wait()
+        out_ref[k * width : (k + 1) * width, :] = jnp.transpose(in_ref[k], (1, 0))
+
+
+def turn(v):
+    tokens, width = v.shape
+    return pl.pallas_call(
+        turn_kernel,
+        out_shape=jax.ShapeDtypeStruct((width, tokens), BF16),
+        in_specs=[pl.BlockSpec(memory_space=pltpu.HBM)],
+        out_specs=pl.BlockSpec(memory_space=pltpu.VMEM),
+        scratch_shapes=[pltpu.VMEM((4, tokens, width // 4), BF16), pltpu.SemaphoreType.DMA((4,))],
+        compiler_params=pltpu.CompilerParams(vmem_limit_bytes=16 << 20),
+        name="turn",
+    )(*in_hbm(v))
+
+
+PARTS = 4
+
+
+def weight_copies(chunk, w_hbm, w_ref, sem):
+    inner, cols = w_ref.shape
+    rows = inner // PARTS
+    start = pl.multiple_of(chunk * cols, cols)
+    return [
+        pltpu.make_async_copy(
+            w_hbm.at[pl.ds(k * rows, rows), pl.ds(start, cols)], w_ref.at[pl.ds(k * rows, rows), :], sem.at[k]
+        )
+        for k in range(PARTS)
+    ]
+
+
+def product(mix_ref, w_ref, copies):
+    rows = w_ref.shape[0] // PARTS
+    total = None
+    for k in range(PARTS):
+        copies[k].wait()
+        part = dot(mix_ref[:, k * rows : (k + 1) * rows], w_ref[k * rows : (k + 1) * rows, :])
+        total = part if total is None else total + part
+    return total
+
+
+def gate_kernel(chunks, y_ref, gate_ref, w_hbm, mix_ref, out_ref, w_ref, sem):
+    copies = weight_copies(chunks[0], w_hbm, w_ref, sem)
+    for copy in copies:
+        copy.start()
     turned = jnp.transpose(y_ref[...], (1, 0))
-    out_ref[...] = (gate_ref[...].astype(F32) * turned.astype(F32)).astype(BF16)
-
-
-def gate_mix(y, gate):
+    mix_ref[...] = (gate_ref[...].astype(F32) * turned.astype(F32)).astype(BF16)
+    out_ref[...] = product(mix_ref, w_ref, copies).astype(BF16)
+
+
+def gate_project(chunks, y, gate, w):
+    tokens, inner, cols = gate.shape[0], w.shape[0], w.shape[1] // 4
+    vmem = pl.BlockSpec(memory_space=pltpu.VMEM)
     return pl.pallas_call(
         gate_kernel,
-        out_shape=jax.ShapeDtypeStruct(gate.shape, BF16),
+        out_shape=(jax.ShapeDtypeStruct(gate.shape, BF16), jax.ShapeDtypeStruct((tokens, cols), BF16)),
+        in_specs=[pl.BlockSpec(memory_space=pltpu.SMEM), vmem, vmem, pl.BlockSpec(memory_space=pltpu.HBM)],
+        out_specs=(vmem, vmem),
+        scratch_shapes=[pltpu.VMEM((inner, cols), BF16), pltpu.SemaphoreType.DMA((PARTS,))],
         compiler_params=pltpu.CompilerParams(vmem_limit_bytes=32 << 20),
-        name="gate_mix",
-    )(y, gate)
-
-
-def project_kernel(order, mix_ref, w_ref, out_ref):
-    out_ref[0] = dot(mix_ref[...], w_ref[...]).astype(BF16)
-
-
-def project(order, mix, weight):
-    tokens, inner = mix.shape
-    chunks = order.shape[0]
-    cols = weight.shape[1] // 4
-    return pl.pallas_call(
-        project_kernel,
-        out_shape=jax.ShapeDtypeStruct((chunks, tokens, cols), BF16),
-        grid_spec=pltpu.PrefetchScalarGridSpec(
-            num_scalar_prefetch=1,
-            grid=(chunks,),
-            in_specs=[
-                pl.BlockSpec((tokens, inner), lambda j, o: (0, 0)),
-                pl.BlockSpec((inner, cols), lambda j, o: (0, o[j])),
-            ],
-            out_specs=pl.BlockSpec((1, tokens, cols), lambda j, o: (j, 0, 0)),
-        ),
+        name="gate_project",
+    )(chunks, y, gate, *in_hbm(w))
+
+
+def project(chunks, mix, w, dtypes):
+    tokens, inner, cols = mix.shape[0], w.shape[0], w.shape[1] // 4
+    count = len(dtypes)
+    vmem = pl.BlockSpec(memory_space=pltpu.VMEM)
+
+    def kernel(chunks, mix_ref, w_hbm, *refs):
+        out_refs, (w_ref, sem) = refs[:count], refs[count:]
+        copies = [weight_copies(chunks[j], w_hbm, w_ref.at[j], sem.at[j]) for j in range(count)]
+        for copy in sum(copies, []):
+            copy.start()
+        for j in range(count):
+            out_refs[j][...] = product(mix_ref, w_ref.at[j], copies[j]).astype(dtypes[j])
+
+    return pl.pallas_call(
+        kernel,
+        out_shape=tuple(jax.ShapeDtypeStruct((tokens, cols), d) for d in dtypes),
+        in_specs=[pl.BlockSpec(memory_space=pltpu.SMEM), vmem, pl.BlockSpec(memory_space=pltpu.HBM)],
+        out_specs=(vmem,) * count,
+        scratch_shapes=[pltpu.VMEM((count, inner, cols), BF16), pltpu.SemaphoreType.DMA((count, PARTS))],
         compiler_params=pltpu.CompilerParams(vmem_limit_bytes=32 << 20),
         name="project",
-    )(order, mix, weight)
+    )(chunks, mix, *in_hbm(w))
 
 
 CORE_PAIR = [(0, 1), (1, 0), (2, 3), (3, 2)]
@@ -229,19 +307,20 @@
     me = lax.axis_index("ctx")
     mine = lax.axis_index("ch")
     tokens, width = gated_value.shape
-    turned = gated_value.T.reshape(HALF, GROUP, tokens)
+    turned = turn(gated_value).reshape(HALF, GROUP, tokens)
     x = lax.all_to_all(turned, "ctx", 0, 0, tiled=True)
     spec = filter_spectrum(me.reshape(1), long_filter, t)
     y = convolve(x, spec, t)
     y = lax.all_to_all(y, "ctx", 0, 0, tiled=True).reshape(width, tokens)
-    mix = gate_mix(y, query_gate)
-    away = project(jnp.stack([mine ^ 3, mine ^ 2]), mix, out_weight)
-    home = project(jnp.stack([mine ^ 1, mine]), mix, out_weight)
-    away_in = lax.ppermute(away[0], "ch", CORE_PAIR)
-    away_sum = (away[1].astype(F32) + away_in.astype(F32)).astype(BF16)
+    order = jnp.arange(3, -1, -1, dtype=jnp.int32) ^ mine
+    mix, away_pair = gate_project(order[:1], y, query_gate, out_weight)
+    away_in = lax.ppermute(away_pair, "ch", CORE_PAIR)
+    (away_own,) = project(order[1:2], mix, out_weight, (F32,))
+    away_sum = (away_own + away_in.astype(F32)).astype(BF16)
     far = lax.ppermute(away_sum, "ch", CHIP_PAIR)
-    near = lax.ppermute(home[0], "ch", CORE_PAIR)
-    return (home[1].astype(F32) + near.astype(F32) + far.astype(F32)).astype(BF16)
+    home_pair, home_own = project(order[2:], mix, out_weight, (BF16, F32))
+    near = lax.ppermute(home_pair, "ch", CORE_PAIR)
+    return (home_own + near.astype(F32) + far.astype(F32)).astype(BF16)
 
 
 def solution(mesh):

time: 75 us -> 67.1 us (0.89)
  local copies, waits for them, and re-layouts: 18.3 us -> 0.77 us
  Pallas kernels: 9.87 us -> 18.1 us
  waiting for transfers between devices: 21 us -> 26.1 us
  starting transfers between devices: 23.5 us -> 20.4 us
    unnamed x30 -> x16, local copies, waits for them, and re-layouts: 16.1 us -> 0.04 us
    pallas_call x3 -> x4, Pallas kernels: 4.79 us -> 11.1 us  [the longest x2 6.24 us: project(): pl.pallas_call(kernel, out_shape=tuple((jax.ShapeDtypeStruct((tokens, col...]
    all_to_all x1, waiting for transfers between devices: 0.01 us -> 5.94 us  [per_device(): x = lax.all_to_all(turned, 'ctx', 0, 0, tiled=True)]
    all_to_all x1, starting transfers between devices: 7.74 us -> 4.35 us  [per_device(): y = lax.all_to_all(y, 'ctx', 0, 0, tiled=True).reshape(width, tokens)]
    transpose x1 -> x0, local copies, waits for them, and re-layouts: 2.17 us -> none  [per_device(): turned = gated_value.T.reshape(HALF, GROUP, tokens)]
    pallas_call x1, Pallas kernels: 2.25 us -> 4.18 us  [filter_spectrum(): pl.pallas_call(filter_kernel, out_shape=jax.ShapeDtypeStruct((GROUP * BLO...]
    all_to_all x1, waiting for transfers between devices: 9.15 us -> 8.23 us  [per_device(): y = lax.all_to_all(y, 'ctx', 0, 0, tiled=True).reshape(width, tokens)]
  transfers between devices with their start and end apart: 5 -> 5, of which waited for: 2 -> 3; matrix products, arithmetic and copies ran while one was open for 1% -> 1% of each run, Pallas kernels for 6% -> 16%
where the time goes in v2:
time: 67.1 us; the launch traced here: 66.7 us
  waiting for transfers between devices  26.1 us (39%)
  starting transfers between devices  20.4 us (30%)
  Pallas kernels  18.1 us (27%)
  other arithmetic  1.2 us (2%)
  local copies, waits for them, and re-layouts  0.77 us (1%)
    ppermute x1, waiting for transfers between devices, per_device(): far = lax.ppermute(away_sum, 'ch', CHIP_PAIR)  11.9 us
    all_to_all x1, starting transfers between devices, per_device(): x = lax.all_to_all(turned, 'ctx', 0, 0, tiled=True)  9.74 us
    all_to_all x1, waiting for transfers between devices, per_device(): y = lax.all_to_all(y, 'ctx', 0, 0, tiled=True).reshape(width, tokens)  8.23 us
    pallas_call x2, Pallas kernels, project(): pl.pallas_call(kernel, out_shape=tuple((jax.ShapeDtypeStruct((tokens, col...  6.24 us
    all_to_all x1, waiting for transfers between devices, per_device(): x = lax.all_to_all(turned, 'ctx', 0, 0, tiled=True)  5.94 us
    all_to_all x1, starting transfers between devices, per_device(): y = lax.all_to_all(y, 'ctx', 0, 0, tiled=True).reshape(width, tokens)  4.35 us
    pallas_call x1, Pallas kernels, filter_spectrum(): pl.pallas_call(filter_kernel, out_shape=jax.ShapeDtypeStruct((GROUP * BLO...  4.18 us
    ppermute x1, starting transfers between devices, per_device(): away_in = lax.ppermute(away_pair, 'ch', CORE_PAIR)  3.55 us
  transfers between devices with their start and end apart: 5, of which 3 were waited for; matrix products, arithmetic and copies ran while one was open for 1% of the time, Pallas kernels for 16%

profile of v2, /device:TPU:1, one launch (start us, length us, event | category | flops | bytes accessed | tf_op | source)
XLA Modules:
  0.0 66.7 jit_solution(4379555640788510530)
XLA Ops:
  0.0 0.0 copy-start
  0.0 0.0 copy-start.1
  0.0 0.0 copy-start.4
  0.0 0.0 copy-start.3
  0.0 0.0 copy-start.5
  0.0 0.0 copy-start.7
  0.0 0.0 copy-start.6
  0.1 0.0 copy-start.2
  0.1 2.2 %turn.1 = bf16[1024,256]{1,0:T(8,128)(2,1)} custom-call(bf16[256,1024]{1,0:T(8,128)(2,1)} %v_hbm.1), custom_call_target="tpu_custom_call" | custom-call | tf_op jit(solution)/shard_map/turn/pallas_call | solution.py:218
  2.3 9.7 %all-to-all-start = ((bf16[32,32,256]{2,1,0:T(8,128)(2,1)}), bf16[32,32,256]{2,1,0:T(8,128)(2,1)S(1)}, u32[]{:S(2)}, u32[]{:S(2)}) async-start(bf16[32,32,256]{2,1,0:T(8,128)(2,1)} %bitcast), calls=%async_computation | async-start | bytes 1048576 | tf_op jit(solution)/shard_map/all_to_all | solution.py:311
  12.0 4.2 %filter_spectrum.1.spec_ref = bf16[2048,256]{1,0:T(8,128)(2,1)S(1)} custom-call(s32[1]{0:T(128)} %bitcast.1.which, bf16[8192,1024]{1,0:T(8,128)(2,1)} %h_hbm.1, bf16[128,64]{1,0:T(8,128)(2,1)} %constant.37.a_hbm, f32[64,256]{1,0:T(8,128)} %constant.32.clone.twist_hbm.twist_ref, bf16[256,256]{1,0:T(8,128)(2,1)} %constant.38.forth_hbm.forth_ref, ...), custom_call_target="tpu_custom_call" | custom-call | tf_op jit(solution)/shard_map/filter_spectrum/pallas_call | solution.py:170
  16.2 5.9 %all-to-all-done.x_ref = bf16[32,32,256]{2,1,0:T(8,128)(2,1)S(1)} async-done(((bf16[32,32,256]{2,1,0:T(8,128)(2,1)}), bf16[32,32,256]{2,1,0:T(8,128)(2,1)S(1)}, u32[]{:S(2)}, u32[]{:S(2)}) %all-to-all-start) | async-done | bytes 524320 | tf_op jit(solution)/shard_map/all_to_all | solution.py:311
  22.2 0.0 copy-done
  22.2 0.0 copy-done.1
  22.2 0.0 copy-done.4
  22.2 0.0 copy-done.3
  22.2 0.0 copy-done.5
  22.2 0.0 copy-done.7
  22.2 0.0 copy-done.6
  22.2 2.8 %convolve.1 = bf16[32,32,256]{2,1,0:T(8,128)(2,1)} custom-call(bf16[32,32,256]{2,1,0:T(8,128)(2,1)S(1)} %all-to-all-done.x_ref, bf16[2048,256]{1,0:T(8,128)(2,1)S(1)} %filter_spectrum.1.spec_ref, bf16[128,64]{1,0:T(8,128)(2,1)S(1)} %copy-done.6, bf16[64,128]{1,0:T(8,128)(2,1)S(1)} %copy-done.7, f32[64,256]{1,0:T(8,128)S(1)} %copy-done.4, ...), custom_call_target="tpu_custom_call" | custom-call | tf_op jit(solution)/shard_map/convolve/pallas_call | solution.py:192
  25.1 4.3 %all-to-all-start.1 = ((bf16[32,32,256]{2,1,0:T(8,128)(2,1)}), bf16[32,32,256]{2,1,0:T(8,128)(2,1)S(1)}, u32[]{:S(2)}, u32[]{:S(2)}) async-start(bf16[32,32,256]{2,1,0:T(8,128)(2,1)} %convolve.1), calls=%async_computation.1 | async-start | bytes 1048576 | tf_op jit(solution)/shard_map/all_to_all | solution.py:314
  29.4 0.7 fusion
  30.1 8.2 %all-to-all-done.1 = bf16[32,32,256]{2,1,0:T(8,128)(2,1)S(1)} async-done(((bf16[32,32,256]{2,1,0:T(8,128)(2,1)}), bf16[32,32,256]{2,1,0:T(8,128)(2,1)S(1)}, u32[]{:S(2)}, u32[]{:S(2)}) %all-to-all-start.1) | async-done | bytes 524320 | tf_op jit(solution)/shard_map/all_to_all | solution.py:314
  38.3 0.0 copy-done.2
  38.3 2.6 %gate_project.1 = (bf16[256,1024]{1,0:T(8,128)(2,1)S(1)}, bf16[256,1024]{1,0:T(8,128)(2,1)S(1)}) custom-call(s32[1]{0:T(128)} %get-tuple-element.13.chunks, bf16[1024,256]{1,0:T(8,128)(2,1)S(1)} %bitcast.3, bf16[256,1024]{1,0:T(8,128)(2,1)S(1)} %copy-done.2, bf16[1024,4096]{1,0:T(8,128)(2,1)} %w_hbm.5), custom_call_target="tpu_custom_call" | custom-call | tf_op jit(solution)/shard_map/gate_project/pallas_call | solution.py:266
  40.9 3.5 %collective-permute-start.1 = (bf16[256,1024]{1,0:T(8,128)(2,1)S(1)}, bf16[256,1024]{1,0:T(8,128)(2,1)S(1)}, u32[]{:S(2)}, u32[]{:S(2)}) collective-permute-start(bf16[256,1024]{1,0:T(8,128)(2,1)S(1)} %get-tuple-element.12), channel_id=1, source_target_pairs={{0,1},{1,0},{2,3},{3,2},{4,5},{5,4},{6,7},{7,6},{8,9},{9,8},{10,11... | collective-permute-start | bytes 1572872 | tf_op jit(solution)/shard_map/ppermute | solution.py:317
  44.5 0.1 slice.9.chunks
  44.6 2.7 %project.3 = f32[256,1024]{1,0:T(8,128)S(1)} custom-call(s32[1]{0:T(128)} %get-tuple-element.14.chunks, bf16[256,1024]{1,0:T(8,128)(2,1)S(1)} %get-tuple-element.9.mix_ref, bf16[1024,4096]{1,0:T(8,128)(2,1)} %w_hbm.5), custom_call_target="tpu_custom_call" | custom-call | tf_op jit(solution)/shard_map/project/pallas_call | solution.py:290
  47.3 3.5 %project.2 = (bf16[256,1024]{1,0:T(8,128)(2,1)S(1)}, f32[256,1024]{1,0:T(8,128)S(1)}) custom-call(s32[2]{0:T(128)S(1)} %slice.9.chunks, bf16[256,1024]{1,0:T(8,128)(2,1)S(1)} %get-tuple-element.9.mix_ref, bf16[1024,4096]{1,0:T(8,128)(2,1)} %w_hbm.5), custom_call_target="tpu_custom_call" | custom-call | tf_op jit(solution)/shard_map/project/pallas_call | solution.py:290
  50.8 0.1 collective-permute-start
  50.9 0.0 collective-permute-done.1
  50.9 0.1 add_convert_fusion.1
  51.1 2.7 %collective-permute-start.2 = (bf16[256,1024]{1,0:T(8,128)(2,1)S(1)}, bf16[256,1024]{1,0:T(8,128)(2,1)S(1)}, u32[]{:S(2)}, u32[]{:S(2)}) collective-permute-start(bf16[256,1024]{1,0:T(8,128)(2,1)S(1)} %add_convert_fusion.1), channel_id=1, source_target_pairs={{0,2},{2,0},{1,3},{3,1},{4,6},{6,4},{5,7},{7,5},{8,10},{10,8},{9,1... | collective-permute-start | bytes 1572872 | tf_op jit(solution)/shard_map/ppermute | solution.py:320
  53.8 0.0 collective-permute-done
  53.8 11.9 %collective-permute-done.2 = bf16[256,1024]{1,0:T(8,128)(2,1)S(1)} collective-permute-done((bf16[256,1024]{1,0:T(8,128)(2,1)S(1)}, bf16[256,1024]{1,0:T(8,128)(2,1)S(1)}, u32[]{:S(2)}, u32[]{:S(2)}) %collective-permute-start.2) | collective-permute-done | bytes 524320 | tf_op jit(solution)/shard_map/ppermute | solution.py:320
  65.7 1.0 %add_convert_fusion = bf16[256,1024]{1,0:T(8,128)(2,1)} fusion(bf16[256,1024]{1,0:T(8,128)(2,1)S(1)} %collective-permute-done.2, f32[256,1024]{1,0:T(8,128)S(1)} %get-tuple-element.10, bf16[256,1024]{1,0:T(8,128)(2,1)S(1)} %collective-permute-done), kind=kLoop, calls=%fused_computation | loop fusion | flops 1310720 | bytes 2621440 | tf_op jit(solution)/shard_map/convert_element_type | solution.py:323
  (1 shorter events, 0.0 us)
Async XLA Ops:
  0.0 22.2 %copy-start = (bf16[512,512]{1,0:T(8,128)(2,1)S(1)}, bf16[512,512]{1,0:T(8,128)(2,1)}, u32[]{:S(2)}) copy-start(bf16[512,512]{1,0:T(8,128)(2,1)} %constant.39.swap_hbm.swap_ref) | copy-start | bytes 1572868
  0.0 22.2 %copy-start.1 = (bf16[256,256]{1,0:T(8,128)(2,1)S(1)}, bf16[256,256]{1,0:T(8,128)(2,1)}, u32[]{:S(2)}) copy-start(bf16[256,256]{1,0:T(8,128)(2,1)} %constant.38.forth_hbm.forth_ref) | copy-start | bytes 393220
  0.0 22.2 %copy-start.4 = (f32[64,256]{1,0:T(8,128)S(1)}, f32[64,256]{1,0:T(8,128)}, u32[]{:S(2)}) copy-start(f32[64,256]{1,0:T(8,128)} %constant.32.clone.twist_hbm.twist_ref) | copy-start | bytes 196612
  0.0 22.2 %copy-start.3 = (bf16[512,512]{1,0:T(8,128)(2,1)S(1)}, bf16[512,512]{1,0:T(8,128)(2,1)}, u32[]{:S(2)}) copy-start(bf16[512,512]{1,0:T(8,128)(2,1)} %constant.43.unswap_ref) | copy-start | bytes 1572868
  0.0 22.2 %copy-start.5 = (bf16[256,256]{1,0:T(8,128)(2,1)S(1)}, bf16[256,256]{1,0:T(8,128)(2,1)}, u32[]{:S(2)}) copy-start(bf16[256,256]{1,0:T(8,128)(2,1)} %constant.42.back_ref) | copy-start | bytes 393220
  0.0 22.2 %copy-start.7 = (bf16[64,128]{1,0:T(8,128)(2,1)S(1)}, bf16[64,128]{1,0:T(8,128)(2,1)}, u32[]{:S(2)}) copy-start(bf16[64,128]{1,0:T(8,128)(2,1)} %constant.41.a_back_ref) | copy-start | bytes 49156
  0.0 22.2 %copy-start.6 = (bf16[128,64]{1,0:T(8,128)(2,1)S(1)}, bf16[128,64]{1,0:T(8,128)(2,1)}, u32[]{:S(2)}) copy-start(bf16[128,64]{1,0:T(8,128)(2,1)} %constant.40.a_ref) | copy-start | bytes 49156
  0.1 38.3 %copy-start.2 = (bf16[256,1024]{1,0:T(8,128)(2,1)S(1)}, bf16[256,1024]{1,0:T(8,128)(2,1)}, u32[]{:S(2)}) copy-start(bf16[256,1024]{1,0:T(8,128)(2,1)} %gate_ref.1) | copy-start | bytes 1572868
  2.3 19.9 %all-to-all-start = ((bf16[32,32,256]{2,1,0:T(8,128)(2,1)}), bf16[32,32,256]{2,1,0:T(8,128)(2,1)S(1)}, u32[]{:S(2)}, u32[]{:S(2)}) async-start(bf16[32,32,256]{2,1,0:T(8,128)(2,1)} %bitcast), calls=%async_computation | async-start | bytes 1048576 | tf_op jit(solution)/shard_map/all_to_all | solution.py:311
  25.1 13.3 %all-to-all-start.1 = ((bf16[32,32,256]{2,1,0:T(8,128)(2,1)}), bf16[32,32,256]{2,1,0:T(8,128)(2,1)S(1)}, u32[]{:S(2)}, u32[]{:S(2)}) async-start(bf16[32,32,256]{2,1,0:T(8,128)(2,1)} %convolve.1), calls=%async_computation.1 | async-start | bytes 1048576 | tf_op jit(solution)/shard_map/all_to_all | solution.py:314
  40.9 10.0 %collective-permute-start.1 = (bf16[256,1024]{1,0:T(8,128)(2,1)S(1)}, bf16[256,1024]{1,0:T(8,128)(2,1)S(1)}, u32[]{:S(2)}, u32[]{:S(2)}) collective-permute-start(bf16[256,1024]{1,0:T(8,128)(2,1)S(1)} %get-tuple-element.12), channel_id=1, source_target_pairs={{0,1},{1,0},{2,3},{3,2},{4,5},{5,4},{6,7},{7,6},{8,9},{9,8},{10,11... | collective-permute-start | bytes 1572872 | tf_op jit(solution)/shard_map/ppermute | solution.py:317
  50.8 3.0 %collective-permute-start = (bf16[256,1024]{1,0:T(8,128)(2,1)S(1)}, bf16[256,1024]{1,0:T(8,128)(2,1)S(1)}, u32[]{:S(2)}, u32[]{:S(2)}) collective-permute-start(bf16[256,1024]{1,0:T(8,128)(2,1)S(1)} %get-tuple-element.11), channel_id=1, source_target_pairs={{0,1},{1,0},{2,3},{3,2},{4,5},{5,4},{6,7},{7,6},{8,9},{9,8},{10,11... | collective-permute-start | bytes 1572872 | tf_op jit(solution)/shard_map/ppermute | solution.py:322
  51.1 14.6 %collective-permute-start.2 = (bf16[256,1024]{1,0:T(8,128)(2,1)S(1)}, bf16[256,1024]{1,0:T(8,128)(2,1)S(1)}, u32[]{:S(2)}, u32[]{:S(2)}) collective-permute-start(bf16[256,1024]{1,0:T(8,128)(2,1)S(1)} %add_convert_fusion.1), channel_id=1, source_target_pairs={{0,2},{2,0},{1,3},{3,1},{4,6},{6,4},{5,7},{7,5},{8,10},{10,8},{9,1... | collective-permute-start | bytes 1572872 | tf_op jit(solution)/shard_map/ppermute | solution.py:320

commit v3 on v2

--- a/solution.py
+++ b/solution.py
@@ -120,8 +120,12 @@
 
 
 def conv_kernel(
-    x_ref, spec_ref, a_ref, a_back_ref, twist_ref, forth_ref, back_ref, swap_ref, unswap_ref, out_ref, mid_ref, turn_ref
+    chunks, x_ref, spec_ref, a_ref, a_back_ref, twist_ref, forth_ref, back_ref, swap_ref, unswap_ref, w_hbm,
+    out_ref, w_ref, mid_ref, turn_ref, sem,
 ):
+    copies = weight_copies(chunks[0], w_hbm, w_ref, sem)
+    for copy in copies:
+        copy.start()
     pieces = []
     for half in range(2):
         for g in range(2):
@@ -160,6 +164,8 @@
             out_ref[:, g * SUB : (g + 1) * SUB, half * SPAN : (half + 1) * SPAN] = result[:, lane : lane + SPAN].reshape(
                 HALF, SUB, SPAN
             )
+    for copy in copies:
+        copy.wait()
 
 
 def in_hbm(*arrays):
@@ -188,17 +194,24 @@
     )(which, *in_hbm(long_filter, t["a_filter"], t["twist"], t["forth"], t["swap"]))
 
 
-def convolve(x, spec, t):
+def convolve(chunks, x, spec, w, t):
+    inner, cols = w.shape[0], w.shape[1] // 4
+    vmem = pl.BlockSpec(memory_space=pltpu.VMEM)
     return pl.pallas_call(
         conv_kernel,
-        out_shape=jax.ShapeDtypeStruct((HALF, GROUP, 2 * SPAN), BF16),
+        out_shape=(pltpu.VMEM((HALF, GROUP, 2 * SPAN), BF16), pltpu.VMEM((inner, cols), BF16)),
+        in_specs=[pl.BlockSpec(memory_space=pltpu.SMEM)] + [vmem] * 9 + [pl.BlockSpec(memory_space=pltpu.HBM)],
+        out_specs=(vmem, vmem),
         scratch_shapes=[
             pltpu.VMEM((GROUP * BLOCKS, 2 * SPAN), BF16),
             pltpu.VMEM((HALF * SUB, 4 * SPAN), BF16),
+            pltpu.SemaphoreType.DMA((PARTS,)),
         ],
         compiler_params=pltpu.CompilerParams(vmem_limit_bytes=32 << 20),
         name="convolve",
-    )(x, spec, t["a_value"], t["a_back"], t["twist"], t["forth"], t["back"], t["swap"], t["unswap"])
+    )(
+        chunks, x, spec, t["a_value"], t["a_back"], t["twist"], t["forth"], t["back"], t["swap"], t["unswap"], *in_hbm(w)
+    )
 
 
 def turn_kernel(v_hbm, out_ref, in_ref, sem):
@@ -217,7 +230,7 @@
     tokens, width = v.shape
     return pl.pallas_call(
         turn_kernel,
-        out_shape=jax.ShapeDtypeStruct((width, tokens), BF16),
+        out_shape=pltpu.VMEM((width, tokens), BF16),
         in_specs=[pl.BlockSpec(memory_space=pltpu.HBM)],
         out_specs=pl.BlockSpec(memory_space=pltpu.VMEM),
         scratch_shapes=[pltpu.VMEM((4, tokens, width // 4), BF16), pltpu.SemaphoreType.DMA((4,))],
@@ -251,27 +264,21 @@
     return total
 
 
-def gate_kernel(chunks, y_ref, gate_ref, w_hbm, mix_ref, out_ref, w_ref, sem):
-    copies = weight_copies(chunks[0], w_hbm, w_ref, sem)
-    for copy in copies:
-        copy.start()
+def gate_kernel(y_ref, gate_ref, w_ref, mix_ref, out_ref):
     turned = jnp.transpose(y_ref[...], (1, 0))
-    mix_ref[...] = (gate_ref[...].astype(F32) * turned.astype(F32)).astype(BF16)
-    out_ref[...] = product(mix_ref, w_ref, copies).astype(BF16)
-
-
-def gate_project(chunks, y, gate, w):
-    tokens, inner, cols = gate.shape[0], w.shape[0], w.shape[1] // 4
-    vmem = pl.BlockSpec(memory_space=pltpu.VMEM)
+    mix = (gate_ref[...].astype(F32) * turned.astype(F32)).astype(BF16)
+    mix_ref[...] = mix
+    out_ref[...] = dot(mix, w_ref[...]).astype(BF16)
+
+
+def gate_project(y, gate, w):
+    tokens, cols = gate.shape[0], w.shape[1]
     return pl.pallas_call(
         gate_kernel,
         out_shape=(jax.ShapeDtypeStruct(gate.shape, BF16), jax.ShapeDtypeStruct((tokens, cols), BF16)),
-        in_specs=[pl.BlockSpec(memory_space=pltpu.SMEM), vmem, vmem, pl.BlockSpec(memory_space=pltpu.HBM)],
-        out_specs=(vmem, vmem),
-        scratch_shapes=[pltpu.VMEM((inner, cols), BF16), pltpu.SemaphoreType.DMA((PARTS,))],
         compiler_params=pltpu.CompilerParams(vmem_limit_bytes=32 << 20),
         name="gate_project",
-    )(chunks, y, gate, *in_hbm(w))
+    )(y, gate, w)
 
 
 def project(chunks, mix, w, dtypes):
@@ -310,13 +317,14 @@
     turned = turn(gated_value).reshape(HALF, GROUP, tokens)
     x = lax.all_to_all(turned, "ctx", 0, 0, tiled=True)
     spec = filter_spectrum(me.reshape(1), long_filter, t)
-    y = convolve(x, spec, t)
+    order = jnp.arange(3, -1, -1, dtype=jnp.int32) ^ mine
+    y, w_first = convolve(order[:1], x, spec, out_weight, t)
     y = lax.all_to_all(y, "ctx", 0, 0, tiled=True).reshape(width, tokens)
-    order = jnp.arange(3, -1, -1, dtype=jnp.int32) ^ mine
-    mix, away_pair = gate_project(order[:1], y, query_gate, out_weight)
+    mix, away_pair = gate_project(y, query_gate, w_first)
     away_in = lax.ppermute(away_pair, "ch", CORE_PAIR)
     (away_own,) = project(order[1:2], mix, out_weight, (F32,))
     away_sum = (away_own + away_in.astype(F32)).astype(BF16)
+    mix, away_sum = lax.optimization_barrier((mix, away_sum))
     far = lax.ppermute(away_sum, "ch", CHIP_PAIR)
     home_pair, home_own = project(order[2:], mix, out_weight, (BF16, F32))
     near = lax.ppermute(home_pair, "ch", CORE_PAIR)

time: 67.1 us -> 61.8 us (0.921)
  blocking collectives: 0 us -> 13.1 us
  waiting for transfers between devices: 26.1 us -> 13.7 us
  starting transfers between devices: 20.4 us -> 16.4 us
  Pallas kernels: 18.1 us -> 16.3 us
    all_to_all x0 -> x1, blocking collectives: none -> 13.1 us  [per_device(): y = lax.all_to_all(y, 'ctx', 0, 0, tiled=True).reshape(width, tokens)]
    all_to_all x1 -> x0, waiting for transfers between devices: 8.23 us -> none  [per_device(): y = lax.all_to_all(y, 'ctx', 0, 0, tiled=True).reshape(width, tokens)]
    all_to_all x1 -> x0, starting transfers between devices: 4.35 us -> none  [per_device(): y = lax.all_to_all(y, 'ctx', 0, 0, tiled=True).reshape(width, tokens)]
    ppermute x1, waiting for transfers between devices: 11.9 us -> 8.55 us  [per_device(): far = lax.ppermute(away_sum, 'ch', CHIP_PAIR)]
    pallas_call x1, Pallas kernels: 2.61 us -> 0.74 us  [gate_project(): pl.pallas_call(gate_kernel, out_shape=(jax.ShapeDtypeStruct(gate.shape, B...]
    all_to_all x1, waiting for transfers between devices: 5.94 us -> 5.13 us  [per_device(): x = lax.all_to_all(turned, 'ctx', 0, 0, tiled=True)]
  transfers between devices with their start and end apart: 5 -> 4, of which waited for: 3 -> 2; matrix products, arithmetic and copies ran while one was open for 1% -> 1% of each run, Pallas kernels for 16% -> 17%
where the time goes in v3:
time: 61.8 us; the launch traced here: 61.5 us
  starting transfers between devices  16.4 us (27%)
  Pallas kernels  16.3 us (26%)
  waiting for transfers between devices  13.7 us (22%)
  blocking collectives  13.1 us (21%)
  other arithmetic  1.2 us (2%)
  local copies, waits for them, and re-layouts  0.73 us (1%)
    all_to_all x1, blocking collectives, per_device(): y = lax.all_to_all(y, 'ctx', 0, 0, tiled=True).reshape(width, tokens)  13.1 us
    all_to_all x1, starting transfers between devices, per_device(): x = lax.all_to_all(turned, 'ctx', 0, 0, tiled=True)  9.74 us
    ppermute x1, waiting for transfers between devices, per_device(): far = lax.ppermute(away_sum, 'ch', CHIP_PAIR)  8.55 us
    pallas_call x2, Pallas kernels, project(): pl.pallas_call(kernel, out_shape=tuple((jax.ShapeDtypeStruct((tokens, col...  6.18 us
    all_to_all x1, waiting for transfers between devices, per_device(): x = lax.all_to_all(turned, 'ctx', 0, 0, tiled=True)  5.13 us
    pallas_call x1, Pallas kernels, filter_spectrum(): pl.pallas_call(filter_kernel, out_shape=jax.ShapeDtypeStruct((GROUP * BLO...  4.27 us
    ppermute x1, starting transfers between devices, per_device(): away_in = lax.ppermute(away_pair, 'ch', CORE_PAIR)  3.54 us
    pallas_call x1, Pallas kernels, convolve(): pl.pallas_call(conv_kernel, out_shape=(pltpu.VMEM((HALF, GROUP, 2 * SPAN)...  3.03 us
  transfers between devices with their start and end apart: 4, of which 2 were waited for; matrix products, arithmetic and copies ran while one was open for 1% of the time, Pallas kernels for 17%

profile of v3, /device:TPU:1, one launch (start us, length us, event | category | flops | bytes accessed | tf_op | source)
XLA Modules:
  0.0 61.5 jit_solution(9969505085068343979)
XLA Ops:
  0.0 2.1 %turn.1 = bf16[1024,256]{1,0:T(8,128)(2,1)} custom-call(bf16[256,1024]{1,0:T(8,128)(2,1)} %v_hbm.1), custom_call_target="tpu_custom_call" | custom-call | tf_op jit(solution)/shard_map/turn/pallas_call | solution.py:231
  2.1 9.7 %all-to-all-start = ((bf16[32,32,256]{2,1,0:T(8,128)(2,1)}), bf16[32,32,256]{2,1,0:T(8,128)(2,1)S(1)}, u32[]{:S(2)}, u32[]{:S(2)}) async-start(bf16[32,32,256]{2,1,0:T(8,128)(2,1)} %bitcast), calls=%async_computation | async-start | bytes 1048576 | tf_op jit(solution)/shard_map/all_to_all | solution.py:318
  11.8 0.0 copy-start
  11.9 0.0 copy-start.1
  11.9 0.0 copy-start.2
  11.9 0.0 copy-start.4
  11.9 0.0 copy-start.5
  11.9 0.0 copy-start.6
  11.9 0.0 copy-start.7
  11.9 4.3 %filter_spectrum.1.spec_ref = bf16[2048,256]{1,0:T(8,128)(2,1)S(1)} custom-call(s32[1]{0:T(128)} %bitcast.1.which, bf16[8192,1024]{1,0:T(8,128)(2,1)} %h_hbm.1, bf16[128,64]{1,0:T(8,128)(2,1)} %constant.37.a_hbm, f32[64,256]{1,0:T(8,128)} %constant.32.clone.twist_hbm.twist_ref, bf16[256,256]{1,0:T(8,128)(2,1)} %constant.38.forth_hbm.forth_ref, ...), custom_call_target="tpu_custom_call" | custom-call | tf_op jit(solution)/shard_map/filter_spectrum/pallas_call | solution.py:176
  16.2 0.0 copy-start.3
  16.2 0.6 fusion
  16.8 5.1 %all-to-all-done.x_ref = bf16[32,32,256]{2,1,0:T(8,128)(2,1)S(1)} async-done(((bf16[32,32,256]{2,1,0:T(8,128)(2,1)}), bf16[32,32,256]{2,1,0:T(8,128)(2,1)S(1)}, u32[]{:S(2)}, u32[]{:S(2)}) %all-to-all-start) | async-done | bytes 524320 | tf_op jit(solution)/shard_map/all_to_all | solution.py:318
  22.0 0.0 copy-done
  22.0 0.0 copy-done.1
  22.0 0.0 copy-done.2
  22.0 0.0 copy-done.4
  22.0 0.0 copy-done.5
  22.0 0.0 copy-done.6
  22.0 0.0 copy-done.7
  22.0 3.0 %convolve.1 = (bf16[32,32,256]{2,1,0:T(8,128)(2,1)S(1)}, bf16[1024,1024]{1,0:T(8,128)(2,1)S(1)}) custom-call(s32[1]{0:T(128)} %get-tuple-element.22.chunks, bf16[32,32,256]{2,1,0:T(8,128)(2,1)S(1)} %all-to-all-done.x_ref, bf16[2048,256]{1,0:T(8,128)(2,1)S(1)} %filter_spectrum.1.spec_ref, bf16[128,64]{1,0:T(8,128)(2,1)S(1)} %copy-done.6, ...), custom_call_target="tpu_custom_call" | custom-call | tf_op jit(solution)/shard_map/convolve/pallas_call | solution.py:200
  25.1 13.1 %all_to_all.10 = bf16[32,32,256]{2,1,0:T(8,128)(2,1)S(1)} all-to-all(bf16[32,32,256]{2,1,0:T(8,128)(2,1)S(1)} %get-tuple-element.13), channel_id=1, replica_groups=mesh['ctx'=32,'ch'=4] {'ctx'}, dimensions={0} | all-to-all | bytes 1048576 | tf_op jit(solution)/shard_map/all_to_all | solution.py:322
  38.1 0.0 copy-done.3
  38.1 0.7 %gate_project.1 = (bf16[256,1024]{1,0:T(8,128)(2,1)S(1)}, bf16[256,1024]{1,0:T(8,128)(2,1)S(1)}) custom-call(bf16[1024,256]{1,0:T(8,128)(2,1)S(1)} %bitcast.3, bf16[256,1024]{1,0:T(8,128)(2,1)S(1)} %copy-done.3, bf16[1024,1024]{1,0:T(8,128)(2,1)S(1)} %get-tuple-element.14.w_ref), custom_call_target="tpu_custom_call" | custom-call | tf_op jit(solution)/shard_map/gate_project/pallas_call | solution.py:276
  38.9 3.5 %collective-permute-start = (bf16[256,1024]{1,0:T(8,128)(2,1)S(1)}, bf16[256,1024]{1,0:T(8,128)(2,1)S(1)}, u32[]{:S(2)}, u32[]{:S(2)}) collective-permute-start(bf16[256,1024]{1,0:T(8,128)(2,1)S(1)} %get-tuple-element.16), channel_id=1, source_target_pairs={{0,1},{1,0},{2,3},{3,2},{4,5},{5,4},{6,7},{7,6},{8,9},{9,8},{10,11... | collective-permute-start | bytes 1572872 | tf_op jit(solution)/shard_map/ppermute | solution.py:324
  42.4 0.1 slice.9.chunks
  42.5 2.7 %project.2 = f32[256,1024]{1,0:T(8,128)S(1)} custom-call(s32[1]{0:T(128)} %get-tuple-element.21.chunks, bf16[256,1024]{1,0:T(8,128)(2,1)S(1)} %get-tuple-element.17.mix_ref, bf16[1024,4096]{1,0:T(8,128)(2,1)} %w_hbm.5), custom_call_target="tpu_custom_call" | custom-call | tf_op jit(solution)/shard_map/project/pallas_call | solution.py:297
  45.2 0.0 collective-permute-done
  45.2 0.1 add_convert_fusion.1
  45.3 2.7 %collective-permute-start.2 = (bf16[256,1024]{1,0:T(8,128)(2,1)S(1)}, bf16[256,1024]{1,0:T(8,128)(2,1)S(1)}, u32[]{:S(2)}, u32[]{:S(2)}) collective-permute-start(bf16[256,1024]{1,0:T(8,128)(2,1)S(1)} %add_convert_fusion.1), channel_id=1, source_target_pairs={{0,2},{2,0},{1,3},{3,1},{4,6},{6,4},{5,7},{7,5},{8,10},{10,8},{9,1... | collective-permute-start | bytes 1572872 | tf_op jit(solution)/shard_map/ppermute | solution.py:328
  48.0 3.5 %project.3 = (bf16[256,1024]{1,0:T(8,128)(2,1)S(1)}, f32[256,1024]{1,0:T(8,128)S(1)}) custom-call(s32[2]{0:T(128)S(1)} %slice.9.chunks, bf16[256,1024]{1,0:T(8,128)(2,1)S(1)} %get-tuple-element.17.mix_ref, bf16[1024,4096]{1,0:T(8,128)(2,1)} %w_hbm.5), custom_call_target="tpu_custom_call" | custom-call | tf_op jit(solution)/shard_map/project/pallas_call | solution.py:297
  51.5 0.4 collective-permute-start.1
  51.9 8.6 %collective-permute-done.2 = bf16[256,1024]{1,0:T(8,128)(2,1)S(1)} collective-permute-done((bf16[256,1024]{1,0:T(8,128)(2,1)S(1)}, bf16[256,1024]{1,0:T(8,128)(2,1)S(1)}, u32[]{:S(2)}, u32[]{:S(2)}) %collective-permute-start.2) | collective-permute-done | bytes 524320 | tf_op jit(solution)/shard_map/ppermute | solution.py:328
  60.5 0.0 collective-permute-done.1
  60.5 1.0 %add_convert_fusion = bf16[256,1024]{1,0:T(8,128)(2,1)} fusion(bf16[256,1024]{1,0:T(8,128)(2,1)S(1)} %collective-permute-done.2, f32[256,1024]{1,0:T(8,128)S(1)} %get-tuple-element.18, bf16[256,1024]{1,0:T(8,128)(2,1)S(1)} %collective-permute-done.1), kind=kLoop, calls=%fused_computation | loop fusion | flops 1310720 | bytes 2621440 | tf_op jit(solution)/shard_map/convert_element_type | solution.py:331
  (1 shorter events, 0.0 us)
Async XLA Ops:
  2.1 19.9 %all-to-all-start = ((bf16[32,32,256]{2,1,0:T(8,128)(2,1)}), bf16[32,32,256]{2,1,0:T(8,128)(2,1)S(1)}, u32[]{:S(2)}, u32[]{:S(2)}) async-start(bf16[32,32,256]{2,1,0:T(8,128)(2,1)} %bitcast), calls=%async_computation | async-start | bytes 1048576 | tf_op jit(solution)/shard_map/all_to_all | solution.py:318
  11.8 10.1 %copy-start = (bf16[512,512]{1,0:T(8,128)(2,1)S(1)}, bf16[512,512]{1,0:T(8,128)(2,1)}, u32[]{:S(2)}) copy-start(bf16[512,512]{1,0:T(8,128)(2,1)} %constant.39.swap_hbm.swap_ref) | copy-start | bytes 1572868
  11.9 10.1 %copy-start.1 = (bf16[256,256]{1,0:T(8,128)(2,1)S(1)}, bf16[256,256]{1,0:T(8,128)(2,1)}, u32[]{:S(2)}) copy-start(bf16[256,256]{1,0:T(8,128)(2,1)} %constant.38.forth_hbm.forth_ref) | copy-start | bytes 393220
  11.9 10.1 %copy-start.2 = (bf16[512,512]{1,0:T(8,128)(2,1)S(1)}, bf16[512,512]{1,0:T(8,128)(2,1)}, u32[]{:S(2)}) copy-start(bf16[512,512]{1,0:T(8,128)(2,1)} %constant.43.unswap_ref) | copy-start | bytes 1572868
  11.9 10.1 %copy-start.4 = (f32[64,256]{1,0:T(8,128)S(1)}, f32[64,256]{1,0:T(8,128)}, u32[]{:S(2)}) copy-start(f32[64,256]{1,0:T(8,128)} %constant.32.clone.twist_hbm.twist_ref) | copy-start | bytes 196612
  11.9 10.1 %copy-start.5 = (bf16[256,256]{1,0:T(8,128)(2,1)S(1)}, bf16[256,256]{1,0:T(8,128)(2,1)}, u32[]{:S(2)}) copy-start(bf16[256,256]{1,0:T(8,128)(2,1)} %constant.42.back_ref) | copy-start | bytes 393220
  11.9 10.1 %copy-start.6 = (bf16[128,64]{1,0:T(8,128)(2,1)S(1)}, bf16[128,64]{1,0:T(8,128)(2,1)}, u32[]{:S(2)}) copy-start(bf16[128,64]{1,0:T(8,128)(2,1)} %constant.40.a_ref) | copy-start | bytes 49156
  11.9 10.1 %copy-start.7 = (bf16[64,128]{1,0:T(8,128)(2,1)S(1)}, bf16[64,128]{1,0:T(8,128)(2,1)}, u32[]{:S(2)}) copy-start(bf16[64,128]{1,0:T(8,128)(2,1)} %constant.41.a_back_ref) | copy-start | bytes 49156
  16.2 21.9 %copy-start.3 = (bf16[256,1024]{1,0:T(8,128)(2,1)S(1)}, bf16[256,1024]{1,0:T(8,128)(2,1)}, u32[]{:S(2)}) copy-start(bf16[256,1024]{1,0:T(8,128)(2,1)} %gate_ref.1) | copy-start | bytes 1572868
  38.9 6.3 %collective-permute-start = (bf16[256,1024]{1,0:T(8,128)(2,1)S(1)}, bf16[256,1024]{1,0:T(8,128)(2,1)S(1)}, u32[]{:S(2)}, u32[]{:S(2)}) collective-permute-start(bf16[256,1024]{1,0:T(8,128)(2,1)S(1)} %get-tuple-element.16), channel_id=1, source_target_pairs={{0,1},{1,0},{2,3},{3,2},{4,5},{5,4},{6,7},{7,6},{8,9},{9,8},{10,11... | collective-permute-start | bytes 1572872 | tf_op jit(solution)/shard_map/ppermute | solution.py:324
  45.3 15.1 %collective-permute-start.2 = (bf16[256,1024]{1,0:T(8,128)(2,1)S(1)}, bf16[256,1024]{1,0:T(8,128)(2,1)S(1)}, u32[]{:S(2)}, u32[]{:S(2)}) collective-permute-start(bf16[256,1024]{1,0:T(8,128)(2,1)S(1)} %add_convert_fusion.1), channel_id=1, source_target_pairs={{0,2},{2,0},{1,3},{3,1},{4,6},{6,4},{5,7},{7,5},{8,10},{10,8},{9,1... | collective-permute-start | bytes 1572872 | tf_op jit(solution)/shard_map/ppermute | solution.py:328
  51.5 8.9 %collective-permute-start.1 = (bf16[256,1024]{1,0:T(8,128)(2,1)S(1)}, bf16[256,1024]{1,0:T(8,128)(2,1)S(1)}, u32[]{:S(2)}, u32[]{:S(2)}) collective-permute-start(bf16[256,1024]{1,0:T(8,128)(2,1)S(1)} %get-tuple-element.19), channel_id=1, source_target_pairs={{0,1},{1,0},{2,3},{3,2},{4,5},{5,4},{6,7},{7,6},{8,9},{9,8},{10,11... | collective-permute-start | bytes 1572872 | tf_op jit(solution)/shard_map/ppermute | solution.py:330

commit v4 on v3

--- a/solution.py
+++ b/solution.py
@@ -120,10 +120,10 @@
 
 
 def conv_kernel(
-    chunks, x_ref, spec_ref, a_ref, a_back_ref, twist_ref, forth_ref, back_ref, swap_ref, unswap_ref, w_hbm,
-    out_ref, w_ref, mid_ref, turn_ref, sem,
+    starts, x_ref, spec_ref, a_ref, a_back_ref, twist_ref, forth_ref, back_ref, swap_ref, unswap_ref, w_hbm,
+    out_ref, w_pair_ref, w_own_ref, mid_ref, turn_ref, sem,
 ):
-    copies = weight_copies(chunks[0], w_hbm, w_ref, sem)
+    copies = weight_copies(starts[0], w_hbm, w_pair_ref, sem.at[0]) + weight_copies(starts[1], w_hbm, w_own_ref, sem.at[1])
     for copy in copies:
         copy.start()
     pieces = []
@@ -168,6 +168,10 @@
         copy.wait()
 
 
+def cost(flops, moved):
+    return pl.CostEstimate(flops=flops, transcendentals=0, bytes_accessed=moved)
+
+
 def in_hbm(*arrays):
     return tuple(pltpu.with_memory_space_constraint(a, pltpu.HBM) for a in arrays)
 
@@ -194,46 +198,66 @@
     )(which, *in_hbm(long_filter, t["a_filter"], t["twist"], t["forth"], t["swap"]))
 
 
-def convolve(chunks, x, spec, w, t):
-    inner, cols = w.shape[0], w.shape[1] // 4
+def convolve(starts, x, spec, w, t):
+    inner, cols = w.shape[0], w.shape[1] // 8
     vmem = pl.BlockSpec(memory_space=pltpu.VMEM)
     return pl.pallas_call(
         conv_kernel,
-        out_shape=(pltpu.VMEM((HALF, GROUP, 2 * SPAN), BF16), pltpu.VMEM((inner, cols), BF16)),
+        out_shape=(
+            jax.ShapeDtypeStruct((HALF, GROUP, 2 * SPAN), BF16),
+            jax.ShapeDtypeStruct((inner, cols), BF16),
+            jax.ShapeDtypeStruct((inner, cols), BF16),
+        ),
         in_specs=[pl.BlockSpec(memory_space=pltpu.SMEM)] + [vmem] * 9 + [pl.BlockSpec(memory_space=pltpu.HBM)],
-        out_specs=(vmem, vmem),
+        out_specs=(vmem, vmem, vmem),
         scratch_shapes=[
             pltpu.VMEM((GROUP * BLOCKS, 2 * SPAN), BF16),
             pltpu.VMEM((HALF * SUB, 4 * SPAN), BF16),
-            pltpu.SemaphoreType.DMA((PARTS,)),
+            pltpu.SemaphoreType.DMA((2, PARTS)),
         ],
         compiler_params=pltpu.CompilerParams(vmem_limit_bytes=32 << 20),
         name="convolve",
     )(
-        chunks, x, spec, t["a_value"], t["a_back"], t["twist"], t["forth"], t["back"], t["swap"], t["unswap"], *in_hbm(w)
+        starts, x, spec, t["a_value"], t["a_back"], t["twist"], t["forth"], t["back"], t["swap"], t["unswap"], *in_hbm(w)
     )
 
 
-def turn_kernel(v_hbm, out_ref, in_ref, sem):
-    width = v_hbm.shape[1] // 4
-    copies = [
-        pltpu.make_async_copy(v_hbm.at[:, pl.ds(k * width, width)], in_ref.at[k], sem.at[k]) for k in range(4)
+TURN = 4
+
+
+def turn_kernel(v_hbm, out_hbm, in_ref, turned_ref, in_sem, out_sem):
+    width = v_hbm.shape[1] // TURN
+    loads = [
+        pltpu.make_async_copy(v_hbm.at[:, pl.ds(k * width, width)], in_ref.at[k], in_sem.at[k]) for k in range(TURN)
     ]
-    for copy in copies:
-        copy.start()
-    for k in range(4):
-        copies[k].wait()
-        out_ref[k * width : (k + 1) * width, :] = jnp.transpose(in_ref[k], (1, 0))
+    stores = [
+        pltpu.make_async_copy(turned_ref.at[k], out_hbm.at[pl.ds(k * width, width), :], out_sem.at[k])
+        for k in range(TURN)
+    ]
+    for load in loads:
+        load.start()
+    for k in range(TURN):
+        loads[k].wait()
+        turned_ref[k] = jnp.transpose(in_ref[k], (1, 0))
+        stores[k].start()
+    for store in stores:
+        store.wait()
 
 
 def turn(v):
     tokens, width = v.shape
+    hbm = pl.BlockSpec(memory_space=pltpu.HBM)
     return pl.pallas_call(
         turn_kernel,
-        out_shape=pltpu.VMEM((width, tokens), BF16),
-        in_specs=[pl.BlockSpec(memory_space=pltpu.HBM)],
-        out_specs=pl.BlockSpec(memory_space=pltpu.VMEM),
-        scratch_shapes=[pltpu.VMEM((4, tokens, width // 4), BF16), pltpu.SemaphoreType.DMA((4,))],
+        out_shape=jax.ShapeDtypeStruct((width, tokens), BF16),
+        in_specs=[hbm],
+        out_specs=hbm,
+        scratch_shapes=[
+            pltpu.VMEM((TURN, tokens, width // TURN), BF16),
+            pltpu.VMEM((TURN, width // TURN, tokens), BF16),
+            pltpu.SemaphoreType.DMA((TURN,)),
+            pltpu.SemaphoreType.DMA((TURN,)),
+        ],
         compiler_params=pltpu.CompilerParams(vmem_limit_bytes=16 << 20),
         name="turn",
     )(*in_hbm(v))
@@ -242,10 +266,10 @@
 PARTS = 4
 
 
-def weight_copies(chunk, w_hbm, w_ref, sem):
+def weight_copies(start, w_hbm, w_ref, sem):
     inner, cols = w_ref.shape
     rows = inner // PARTS
-    start = pl.multiple_of(chunk * cols, cols)
+    start = pl.multiple_of(start, cols)
     return [
         pltpu.make_async_copy(
             w_hbm.at[pl.ds(k * rows, rows), pl.ds(start, cols)], w_ref.at[pl.ds(k * rows, rows), :], sem.at[k]
@@ -281,31 +305,82 @@
     )(y, gate, w)
 
 
-def project(chunks, mix, w, dtypes):
-    tokens, inner, cols = mix.shape[0], w.shape[0], w.shape[1] // 4
-    count = len(dtypes)
+def resident_kernel(mix_ref, w_ref, out_ref):
+    out_ref[...] = dot(mix_ref[...], w_ref[...])
+
+
+def project_resident(mix, w):
+    return pl.pallas_call(
+        resident_kernel,
+        out_shape=jax.ShapeDtypeStruct((mix.shape[0], w.shape[1]), F32),
+        compiler_params=pltpu.CompilerParams(vmem_limit_bytes=32 << 20),
+        cost_estimate=cost(2 * mix.shape[0] * w.shape[0] * w.shape[1], 0),
+        name="project_resident",
+    )(mix, w)
+
+
+def project(starts, cols, mix, w, pieces):
+    tokens, inner = mix.shape[0], w.shape[0]
+    rows = tokens // pieces
     vmem = pl.BlockSpec(memory_space=pltpu.VMEM)
 
-    def kernel(chunks, mix_ref, w_hbm, *refs):
-        out_refs, (w_ref, sem) = refs[:count], refs[count:]
-        copies = [weight_copies(chunks[j], w_hbm, w_ref.at[j], sem.at[j]) for j in range(count)]
-        for copy in sum(copies, []):
+    def kernel(starts, mix_ref, w_hbm, *refs):
+        piece_refs, (own_ref, w_ref, sem) = refs[:pieces], refs[pieces:]
+        copies = [weight_copies(starts[j], w_hbm, w_ref.at[j], sem.at[j]) for j in range(2)]
+        for copy in copies[0] + copies[1]:
             copy.start()
-        for j in range(count):
-            out_refs[j][...] = product(mix_ref, w_ref.at[j], copies[j]).astype(dtypes[j])
-
-    return pl.pallas_call(
+        pair = product(mix_ref, w_ref.at[0], copies[0]).astype(BF16)
+        for k in range(pieces):
+            piece_refs[k][...] = pair[k * rows : (k + 1) * rows]
+        own_ref[...] = product(mix_ref, w_ref.at[1], copies[1])
+
+    out = pl.pallas_call(
         kernel,
-        out_shape=tuple(jax.ShapeDtypeStruct((tokens, cols), d) for d in dtypes),
+        out_shape=(jax.ShapeDtypeStruct((rows, cols), BF16),) * pieces + (jax.ShapeDtypeStruct((tokens, cols), F32),),
         in_specs=[pl.BlockSpec(memory_space=pltpu.SMEM), vmem, pl.BlockSpec(memory_space=pltpu.HBM)],
-        out_specs=(vmem,) * count,
-        scratch_shapes=[pltpu.VMEM((count, inner, cols), BF16), pltpu.SemaphoreType.DMA((count, PARTS))],
+        out_specs=(vmem,) * (pieces + 1),
+        scratch_shapes=[pltpu.VMEM((2, inner, cols), BF16), pltpu.SemaphoreType.DMA((2, PARTS))],
         compiler_params=pltpu.CompilerParams(vmem_limit_bytes=32 << 20),
+        cost_estimate=cost(4 * tokens * inner * cols, 4 * inner * cols),
         name="project",
-    )(chunks, mix, *in_hbm(w))
+    )(starts, mix, *in_hbm(w))
+    return out[:pieces], out[pieces]
+
+
+def finish(home, near, far_a, far_b):
+    tokens, cols = home.shape
+    rows = tokens // len(near)
+
+    def kernel(home_ref, *refs):
+        near_refs, (far_a_ref, far_b_ref, out_hbm, sum_ref, sem) = refs[: len(near)], refs[len(near) :]
+        copies = []
+        for k, near_ref in enumerate(near_refs):
+            part = slice(k * rows, (k + 1) * rows)
+            far = jnp.concatenate([far_a_ref[part, :], far_b_ref[part, :]], 1)
+            total = home_ref[part, :] + near_ref[...].astype(F32) + far.astype(F32)
+            sum_ref[part, :] = total.astype(BF16)
+            copy = pltpu.make_async_copy(
+                sum_ref.at[pl.ds(k * rows, rows), :], out_hbm.at[pl.ds(k * rows, rows), :], sem.at[k]
+            )
+            copy.start()
+            copies.append(copy)
+        for copy in copies:
+            copy.wait()
+
+    return pl.pallas_call(
+        kernel,
+        out_shape=jax.ShapeDtypeStruct(home.shape, BF16),
+        in_specs=[pl.BlockSpec(memory_space=pltpu.VMEM)] * (3 + len(near)),
+        out_specs=pl.BlockSpec(memory_space=pltpu.HBM),
+        scratch_shapes=[pltpu.VMEM(home.shape, BF16), pltpu.SemaphoreType.DMA((len(near),))],
+        compiler_params=pltpu.CompilerParams(vmem_limit_bytes=16 << 20),
+        name="finish",
+    )(home, *near, far_a, far_b)
 
 
 CORE_PAIR = [(0, 1), (1, 0), (2, 3), (3, 2)]
+PIECES_B = 4
+PIECES_HOME = 2
 CHIP_PAIR = [(0, 2), (2, 0), (1, 3), (3, 1)]
 
 
@@ -317,18 +392,28 @@
     turned = turn(gated_value).reshape(HALF, GROUP, tokens)
     x = lax.all_to_all(turned, "ctx", 0, 0, tiled=True)
     spec = filter_spectrum(me.reshape(1), long_filter, t)
-    order = jnp.arange(3, -1, -1, dtype=jnp.int32) ^ mine
-    y, w_first = convolve(order[:1], x, spec, out_weight, t)
+    cols = out_weight.shape[1] // 4
+    half = cols // 2
+    first = jnp.stack([mine ^ 3, mine ^ 2]).astype(jnp.int32) * cols
+    home = jnp.stack([mine ^ 1, mine]).astype(jnp.int32) * cols
+    second = first + half
+    y, w_pair, w_own = convolve(first, x, spec, out_weight, t)
     y = lax.all_to_all(y, "ctx", 0, 0, tiled=True).reshape(width, tokens)
-    mix, away_pair = gate_project(y, query_gate, w_first)
-    away_in = lax.ppermute(away_pair, "ch", CORE_PAIR)
-    (away_own,) = project(order[1:2], mix, out_weight, (F32,))
-    away_sum = (away_own + away_in.astype(F32)).astype(BF16)
-    mix, away_sum = lax.optimization_barrier((mix, away_sum))
-    far = lax.ppermute(away_sum, "ch", CHIP_PAIR)
-    home_pair, home_own = project(order[2:], mix, out_weight, (BF16, F32))
-    near = lax.ppermute(home_pair, "ch", CORE_PAIR)
-    return (home_own + near.astype(F32) + far.astype(F32)).astype(BF16)
+    mix, pair_a = gate_project(y, query_gate, w_pair)
+    in_a = lax.ppermute(pair_a, "ch", CORE_PAIR)
+    own_a = project_resident(mix, w_own)
+    sum_a = (own_a + in_a.astype(F32)).astype(BF16)
+    mix, sum_a = lax.optimization_barrier((mix, sum_a))
+    far_a = lax.ppermute(sum_a, "ch", CHIP_PAIR)
+    pair_b, own_b = project(second, half, mix, out_weight, PIECES_B)
+    in_b = [lax.ppermute(piece, "ch", CORE_PAIR) for piece in pair_b]
+    sum_b = (own_b + jnp.concatenate(in_b, 0).astype(F32)).astype(BF16)
+    mix, sum_b = lax.optimization_barrier((mix, sum_b))
+    far_b = lax.ppermute(sum_b, "ch", CHIP_PAIR)
+    mix, far_a = lax.optimization_barrier((mix, far_a))
+    home_pair, home_own = project(home, cols, mix, out_weight, PIECES_HOME)
+    near = [lax.ppermute(piece, "ch", CORE_PAIR) for piece in home_pair]
+    return finish(home_own, near, far_a, far_b)
 
 
 def solution(mesh):

time: 61.8 us -> 65 us (1.052)
  starting transfers between devices: 16.4 us -> 19.2 us
  waiting for transfers between devices: 13.7 us -> 11.7 us
  Pallas kernels: 16.3 us -> 18.1 us
  local copies, waits for them, and re-layouts: 0.73 us -> 2.11 us
  other arithmetic: 1.2 us -> 0.31 us
    ppermute x3 -> x9, starting transfers between devices: 6.62 us -> 9.41 us  [the longest x1 3.57 us: per_device(): in_a = lax.ppermute(pair_a, 'ch', CORE_PAIR)]
    ppermute x3 -> x9, waiting for transfers between devices: 8.56 us -> 5.85 us  [the longest x1 3.38 us: per_device(): far_b = lax.ppermute(sum_b, 'ch', CHIP_PAIR)]
    pallas_call x4 -> x6, Pallas kernels: 11.3 us -> 13.5 us  [the longest x2 6.22 us: project(): pl.pallas_call(kernel, out_shape=(jax.ShapeDtypeStruct((rows, cols), BF16...]
    unnamed x16, local copies, waits for them, and re-layouts: 0.05 us -> 2.11 us
    convert_element_type x2, other arithmetic: 1.19 us -> 0.15 us  [the longest x1 0.08 us: per_device(): sum_b = (own_b + jnp.concatenate(in_b, 0).astype(F32)).astype(BF16)]
    all_to_all x1, waiting for transfers between devices: 5.13 us -> 5.85 us  [per_device(): x = lax.all_to_all(turned, 'ctx', 0, 0, tiled=True)]
    slice x2 -> x0, local copies, waits for them, and re-layouts: 0.68 us -> none  [the longest x1 0.61 us: per_device(): away_own, = project(order[1:2], mix, out_weight, (F32,))]
  transfers between devices with their start and end apart: 4 -> 10, of which waited for: 2 -> 8; matrix products, arithmetic and copies ran while one was open for 1% -> 0% of each run, Pallas kernels for 17% -> 17%
where the time goes in v4:
time: 65 us; the launch traced here: 64.6 us
  starting transfers between devices  19.2 us (30%)
  Pallas kernels  18.1 us (28%)
  blocking collectives  13.1 us (20%)
  waiting for transfers between devices  11.7 us (18%)
  local copies, waits for them, and re-layouts  2.11 us (3%)
    all_to_all x1, blocking collectives, per_device(): y = lax.all_to_all(y, 'ctx', 0, 0, tiled=True).reshape(width, tokens)  13.1 us
    all_to_all x1, starting transfers between devices, per_device(): x = lax.all_to_all(turned, 'ctx', 0, 0, tiled=True)  9.74 us
    pallas_call x2, Pallas kernels, project(): pl.pallas_call(kernel, out_shape=(jax.ShapeDtypeStruct((rows, cols), BF16...  6.22 us
    all_to_all x1, waiting for transfers between devices, per_device(): x = lax.all_to_all(turned, 'ctx', 0, 0, tiled=True)  5.85 us
    pallas_call x1, Pallas kernels, filter_spectrum(): pl.pallas_call(filter_kernel, out_shape=jax.ShapeDtypeStruct((GROUP * BLO...  4.19 us
    pallas_call x1, Pallas kernels, convolve(): pl.pallas_call(conv_kernel, out_shape=(jax.ShapeDtypeStruct((HALF, GROUP,...  3.84 us
    ppermute x1, starting transfers between devices, per_device(): in_a = lax.ppermute(pair_a, 'ch', CORE_PAIR)  3.57 us
    ppermute x1, waiting for transfers between devices, per_device(): far_b = lax.ppermute(sum_b, 'ch', CHIP_PAIR)  3.38 us
  transfers between devices with their start and end apart: 10, of which 8 were waited for; matrix products, arithmetic and copies ran while one was open for 0% of the time, Pallas kernels for 17%

profile of v4, /device:TPU:1, one launch (start us, length us, event | category | flops | bytes accessed | tf_op | source)
XLA Modules:
  0.0 64.6 jit_solution(10730005760617724693)
XLA Ops:
  0.0 0.0 copy-start
  0.0 0.0 copy-start.1
  0.0 0.0 copy-start.4
  0.0 0.0 copy-start.5
  0.0 0.0 copy-start.7
  0.0 0.0 copy-start.6
  0.0 2.1 %turn.1 = bf16[1024,256]{1,0:T(8,128)(2,1)} custom-call(bf16[256,1024]{1,0:T(8,128)(2,1)} %v_hbm.1), custom_call_target="tpu_custom_call" | custom-call | tf_op jit(solution)/shard_map/turn/pallas_call | solution.py:250
  2.1 9.7 %all-to-all-start = ((bf16[32,32,256]{2,1,0:T(8,128)(2,1)}), bf16[32,32,256]{2,1,0:T(8,128)(2,1)S(1)}, u32[]{:S(2)}, u32[]{:S(2)}) async-start(bf16[32,32,256]{2,1,0:T(8,128)(2,1)} %bitcast.4), calls=%async_computation | async-start | bytes 1048576 | tf_op jit(solution)/shard_map/all_to_all | solution.py:393
  11.9 4.2 %filter_spectrum.1.spec_ref = bf16[2048,256]{1,0:T(8,128)(2,1)S(1)} custom-call(s32[1]{0:T(128)} %bitcast.5.which, bf16[8192,1024]{1,0:T(8,128)(2,1)} %h_hbm.1, bf16[128,64]{1,0:T(8,128)(2,1)} %constant.43.a_hbm, f32[64,256]{1,0:T(8,128)} %constant.38.clone.twist_hbm.twist_ref, bf16[256,256]{1,0:T(8,128)(2,1)} %constant.44.forth_hbm.forth_ref, ...), custom_call_target="tpu_custom_call" | custom-call | tf_op jit(solution)/shard_map/filter_spectrum/pallas_call | solution.py:180
  16.1 0.1 broadcast_add_fusion
  16.1 5.8 %all-to-all-done.x_ref = bf16[32,32,256]{2,1,0:T(8,128)(2,1)S(1)} async-done(((bf16[32,32,256]{2,1,0:T(8,128)(2,1)}), bf16[32,32,256]{2,1,0:T(8,128)(2,1)S(1)}, u32[]{:S(2)}, u32[]{:S(2)}) %all-to-all-start) | async-done | bytes 524320 | tf_op jit(solution)/shard_map/all_to_all | solution.py:393
  22.0 0.0 copy-done
  22.0 0.0 copy-done.1
  22.0 0.0 copy-done.4
  22.0 0.0 copy-done.5
  22.0 0.0 copy-done.7
  22.0 0.0 copy-done.6
  22.0 0.0 copy-start.2
  22.0 1.0 %copy-done.2 = bf16[512,512]{1,0:T(8,128)(2,1)S(1)} copy-done((bf16[512,512]{1,0:T(8,128)(2,1)S(1)}, bf16[512,512]{1,0:T(8,128)(2,1)}, u32[]{:S(2)}) %copy-start.2) | copy-done | bytes 524312
  23.1 3.8 %convolve.1 = (bf16[32,32,256]{2,1,0:T(8,128)(2,1)S(1)}, bf16[1024,512]{1,0:T(8,128)(2,1)S(1)}, bf16[1024,512]{1,0:T(8,128)(2,1)S(1)}) custom-call(s32[2]{0:T(128)S(1)} %get-tuple-element.44.starts, bf16[32,32,256]{2,1,0:T(8,128)(2,1)S(1)} %all-to-all-done.x_ref, bf16[2048,256]{1,0:T(8,128)(2,1)S(1)} %filter_spectrum.1.spec_ref, ...), custom_call_target="tpu_custom_call" | custom-call | tf_op jit(solution)/shard_map/convolve/pallas_call | solution.py:204
  26.9 13.1 %all_to_all.10 = bf16[32,32,256]{2,1,0:T(8,128)(2,1)S(1)} all-to-all(bf16[32,32,256]{2,1,0:T(8,128)(2,1)S(1)} %get-tuple-element.24), channel_id=1, replica_groups=mesh['ctx'=32,'ch'=4] {'ctx'}, dimensions={0} | all-to-all | bytes 1048576 | tf_op jit(solution)/shard_map/all_to_all | solution.py:401
  40.0 1.0 %copy-done.3 = bf16[256,1024]{1,0:T(8,128)(2,1)S(1)} copy-done((bf16[256,1024]{1,0:T(8,128)(2,1)S(1)}, bf16[256,1024]{1,0:T(8,128)(2,1)}, u32[]{:S(2)}) %copy-start.3) | copy-done | bytes 524312
  41.0 0.5 gate_project.1
  41.5 3.6 %collective-permute-start = (bf16[256,512]{1,0:T(8,128)(2,1)S(1)}, bf16[256,512]{1,0:T(8,128)(2,1)S(1)}, u32[]{:S(2)}, u32[]{:S(2)}) collective-permute-start(bf16[256,512]{1,0:T(8,128)(2,1)S(1)} %get-tuple-element.28), channel_id=1, source_target_pairs={{0,1},{1,0},{2,3},{3,2},{4,5},{5,4},{6,7},{7,6},{8,9},{9,8},{10,11... | collective-permute-start | bytes 786440 | tf_op jit(solution)/shard_map/ppermute | solution.py:403
  45.1 0.4 project_resident.1
  45.5 0.7 %collective-permute-done = bf16[256,512]{1,0:T(8,128)(2,1)S(1)} collective-permute-done((bf16[256,512]{1,0:T(8,128)(2,1)S(1)}, bf16[256,512]{1,0:T(8,128)(2,1)S(1)}, u32[]{:S(2)}, u32[]{:S(2)}) %collective-permute-start) | collective-permute-done | bytes 262176 | tf_op jit(solution)/shard_map/ppermute | solution.py:403
  46.2 0.1 add_convert_fusion.1
  46.3 2.7 %collective-permute-start.5 = (bf16[256,512]{1,0:T(8,128)(2,1)S(1)}, bf16[256,512]{1,0:T(8,128)(2,1)S(1)}, u32[]{:S(2)}, u32[]{:S(2)}) collective-permute-start(bf16[256,512]{1,0:T(8,128)(2,1)S(1)} %add_convert_fusion.1), channel_id=1, source_target_pairs={{0,2},{2,0},{1,3},{3,1},{4,6},{6,4},{5,7},{7,5},{8,10},{10,8},{9,1... | collective-permute-start | bytes 786440 | tf_op jit(solution)/shard_map/ppermute | solution.py:407
  49.0 2.7 %project.2 = (bf16[64,512]{1,0:T(8,128)(2,1)S(1)}, bf16[64,512]{1,0:T(8,128)(2,1)S(1)}, bf16[64,512]{1,0:T(8,128)(2,1)S(1)}, bf16[64,512]{1,0:T(8,128)(2,1)S(1)}, f32[256,512]{1,0:T(8,128)S(1)}) custom-call(s32[2]{0:T(128)S(1)} %get-tuple-element.43.starts, bf16[256,1024]{1,0:T(8,128)(2,1)S(1)} %get-tuple-element.37.mix_ref, bf16[1024,4096]{1,0:T(8,128)(2,1)} %w_hbm.5), custom_call_target="tpu_custom_call" | custom-call | flops 536870912 | bytes 2097152 | tf_op jit(solution)/shard_map/project/pallas_call | solution.py:337
  51.7 0.7 %collective-permute-start.1 = (bf16[64,512]{1,0:T(8,128)(2,1)S(1)}, bf16[64,512]{1,0:T(8,128)(2,1)S(1)}, u32[]{:S(2)}, u32[]{:S(2)}) collective-permute-start(bf16[64,512]{1,0:T(8,128)(2,1)S(1)} %get-tuple-element.31), channel_id=1, source_target_pairs={{0,1},{1,0},{2,3},{3,2},{4,5},{5,4},{6,7},{7,6},{8,9},{9,8},{10,11... | collective-permute-start | bytes 196616 | tf_op jit(solution)/shard_map/ppermute | solution.py:409
  52.5 0.1 collective-permute-start.2
  52.6 0.4 collective-permute-start.3
  53.0 0.1 collective-permute-start.4
  53.1 0.1 add_multiply_fusion.starts
  53.2 0.2 collective-permute-done.1
  53.4 0.4 collective-permute-done.2
  53.7 0.2 collective-permute-done.3
  53.9 0.4 collective-permute-done.4
  54.2 0.1 add_convert_fusion
  54.3 0.4 collective-permute-start.8
  54.8 0.7 %collective-permute-done.5.refs_2_ = bf16[256,512]{1,0:T(8,128)(2,1)S(1)} collective-permute-done((bf16[256,512]{1,0:T(8,128)(2,1)S(1)}, bf16[256,512]{1,0:T(8,128)(2,1)S(1)}, u32[]{:S(2)}, u32[]{:S(2)}) %collective-permute-start.5) | collective-permute-done | bytes 262176 | tf_op jit(solution)/shard_map/ppermute | solution.py:407
  55.4 3.5 %project.3 = (bf16[128,1024]{1,0:T(8,128)(2,1)S(1)}, bf16[128,1024]{1,0:T(8,128)(2,1)S(1)}, f32[256,1024]{1,0:T(8,128)S(1)}) custom-call(s32[2]{0:T(128)S(1)} %add_multiply_fusion.starts, bf16[256,1024]{1,0:T(8,128)(2,1)S(1)} %get-tuple-element.37.mix_ref, bf16[1024,4096]{1,0:T(8,128)(2,1)} %w_hbm.5), custom_call_target="tpu_custom_call" | custom-call | flops 1073741824 | bytes 4194304 | tf_op jit(solution)/shard_map/project/pallas_call | solution.py:337
  58.9 1.3 %collective-permute-start.6 = (bf16[128,1024]{1,0:T(8,128)(2,1)S(1)}, bf16[128,1024]{1,0:T(8,128)(2,1)S(1)}, u32[]{:S(2)}, u32[]{:S(2)}) collective-permute-start(bf16[128,1024]{1,0:T(8,128)(2,1)S(1)} %get-tuple-element.39), channel_id=1, source_target_pairs={{0,1},{1,0},{2,3},{3,2},{4,5},{5,4},{6,7},{7,6},{8,9},{9,8},{10,11... | collective-permute-start | bytes 786440 | tf_op jit(solution)/shard_map/ppermute | solution.py:415
  60.2 0.1 collective-permute-start.7
  60.3 3.4 %collective-permute-done.8.refs_3_ = bf16[256,512]{1,0:T(8,128)(2,1)S(1)} collective-permute-done((bf16[256,512]{1,0:T(8,128)(2,1)S(1)}, bf16[256,512]{1,0:T(8,128)(2,1)S(1)}, u32[]{:S(2)}, u32[]{:S(2)}) %collective-permute-start.8) | collective-permute-done | bytes 262176 | tf_op jit(solution)/shard_map/ppermute | solution.py:412
  63.7 0.0 collective-permute-done.6.refs_0_
  63.7 0.0 collective-permute-done.7.refs_1_
  63.7 0.9 %finish.1 = bf16[256,1024]{1,0:T(8,128)(2,1)} custom-call(f32[256,1024]{1,0:T(8,128)S(1)} %get-tuple-element.38.home_ref, bf16[128,1024]{1,0:T(8,128)(2,1)S(1)} %collective-permute-done.6.refs_0_, bf16[128,1024]{1,0:T(8,128)(2,1)S(1)} %collective-permute-done.7.refs_1_, bf16[256,512]{1,0:T(8,128)(2,1)S(1)} %collective-permute-done.5.refs_2_, ...), custom_call_target="tpu_custom_call" | custom-call | tf_op jit(solution)/shard_map/finish/pallas_call | solution.py:370
  (1 shorter events, 0.0 us)
Async XLA Ops:
  0.0 22.0 %copy-start = (bf16[512,512]{1,0:T(8,128)(2,1)S(1)}, bf16[512,512]{1,0:T(8,128)(2,1)}, u32[]{:S(2)}) copy-start(bf16[512,512]{1,0:T(8,128)(2,1)} %constant.45.swap_hbm.swap_ref) | copy-start | bytes 1572868
  0.0 22.0 %copy-start.1 = (bf16[256,256]{1,0:T(8,128)(2,1)S(1)}, bf16[256,256]{1,0:T(8,128)(2,1)}, u32[]{:S(2)}) copy-start(bf16[256,256]{1,0:T(8,128)(2,1)} %constant.44.forth_hbm.forth_ref) | copy-start | bytes 393220
  0.0 22.0 %copy-start.4 = (f32[64,256]{1,0:T(8,128)S(1)}, f32[64,256]{1,0:T(8,128)}, u32[]{:S(2)}) copy-start(f32[64,256]{1,0:T(8,128)} %constant.38.clone.twist_hbm.twist_ref) | copy-start | bytes 196612
  0.0 22.0 %copy-start.5 = (bf16[256,256]{1,0:T(8,128)(2,1)S(1)}, bf16[256,256]{1,0:T(8,128)(2,1)}, u32[]{:S(2)}) copy-start(bf16[256,256]{1,0:T(8,128)(2,1)} %constant.48.back_ref) | copy-start | bytes 393220
  0.0 22.0 %copy-start.7 = (bf16[64,128]{1,0:T(8,128)(2,1)S(1)}, bf16[64,128]{1,0:T(8,128)(2,1)}, u32[]{:S(2)}) copy-start(bf16[64,128]{1,0:T(8,128)(2,1)} %constant.47.a_back_ref) | copy-start | bytes 49156
  0.0 22.0 %copy-start.6 = (bf16[128,64]{1,0:T(8,128)(2,1)S(1)}, bf16[128,64]{1,0:T(8,128)(2,1)}, u32[]{:S(2)}) copy-start(bf16[128,64]{1,0:T(8,128)(2,1)} %constant.46.a_ref) | copy-start | bytes 49156
  2.1 19.9 %all-to-all-start = ((bf16[32,32,256]{2,1,0:T(8,128)(2,1)}), bf16[32,32,256]{2,1,0:T(8,128)(2,1)S(1)}, u32[]{:S(2)}, u32[]{:S(2)}) async-start(bf16[32,32,256]{2,1,0:T(8,128)(2,1)} %bitcast.4), calls=%async_computation | async-start | bytes 1048576 | tf_op jit(solution)/shard_map/all_to_all | solution.py:393
  22.0 1.0 %copy-start.2 = (bf16[512,512]{1,0:T(8,128)(2,1)S(1)}, bf16[512,512]{1,0:T(8,128)(2,1)}, u32[]{:S(2)}) copy-start(bf16[512,512]{1,0:T(8,128)(2,1)} %constant.49.unswap_ref) | copy-start | bytes 1572868
  40.0 1.0 %copy-start.3 = (bf16[256,1024]{1,0:T(8,128)(2,1)S(1)}, bf16[256,1024]{1,0:T(8,128)(2,1)}, u32[]{:S(2)}) copy-start(bf16[256,1024]{1,0:T(8,128)(2,1)} %gate_ref.1) | copy-start | bytes 1572868
  41.5 4.7 %collective-permute-start = (bf16[256,512]{1,0:T(8,128)(2,1)S(1)}, bf16[256,512]{1,0:T(8,128)(2,1)S(1)}, u32[]{:S(2)}, u32[]{:S(2)}) collective-permute-start(bf16[256,512]{1,0:T(8,128)(2,1)S(1)} %get-tuple-element.28), channel_id=1, source_target_pairs={{0,1},{1,0},{2,3},{3,2},{4,5},{5,4},{6,7},{7,6},{8,9},{9,8},{10,11... | collective-permute-start | bytes 786440 | tf_op jit(solution)/shard_map/ppermute | solution.py:403
  46.3 9.1 %collective-permute-start.5 = (bf16[256,512]{1,0:T(8,128)(2,1)S(1)}, bf16[256,512]{1,0:T(8,128)(2,1)S(1)}, u32[]{:S(2)}, u32[]{:S(2)}) collective-permute-start(bf16[256,512]{1,0:T(8,128)(2,1)S(1)} %add_convert_fusion.1), channel_id=1, source_target_pairs={{0,2},{2,0},{1,3},{3,1},{4,6},{6,4},{5,7},{7,5},{8,10},{10,8},{9,1... | collective-permute-start | bytes 786440 | tf_op jit(solution)/shard_map/ppermute | solution.py:407
  51.7 1.6 %collective-permute-start.1 = (bf16[64,512]{1,0:T(8,128)(2,1)S(1)}, bf16[64,512]{1,0:T(8,128)(2,1)S(1)}, u32[]{:S(2)}, u32[]{:S(2)}) collective-permute-start(bf16[64,512]{1,0:T(8,128)(2,1)S(1)} %get-tuple-element.31), channel_id=1, source_target_pairs={{0,1},{1,0},{2,3},{3,2},{4,5},{5,4},{6,7},{7,6},{8,9},{9,8},{10,11... | collective-permute-start | bytes 196616 | tf_op jit(solution)/shard_map/ppermute | solution.py:409
  52.5 1.3 %collective-permute-start.2 = (bf16[64,512]{1,0:T(8,128)(2,1)S(1)}, bf16[64,512]{1,0:T(8,128)(2,1)S(1)}, u32[]{:S(2)}, u32[]{:S(2)}) collective-permute-start(bf16[64,512]{1,0:T(8,128)(2,1)S(1)} %get-tuple-element.32), channel_id=1, source_target_pairs={{0,1},{1,0},{2,3},{3,2},{4,5},{5,4},{6,7},{7,6},{8,9},{9,8},{10,11... | collective-permute-start | bytes 196616 | tf_op jit(solution)/shard_map/ppermute | solution.py:409
  52.6 1.3 %collective-permute-start.3 = (bf16[64,512]{1,0:T(8,128)(2,1)S(1)}, bf16[64,512]{1,0:T(8,128)(2,1)S(1)}, u32[]{:S(2)}, u32[]{:S(2)}) collective-permute-start(bf16[64,512]{1,0:T(8,128)(2,1)S(1)} %get-tuple-element.33), channel_id=1, source_target_pairs={{0,1},{1,0},{2,3},{3,2},{4,5},{5,4},{6,7},{7,6},{8,9},{9,8},{10,11... | collective-permute-start | bytes 196616 | tf_op jit(solution)/shard_map/ppermute | solution.py:409
  53.0 1.3 %collective-permute-start.4 = (bf16[64,512]{1,0:T(8,128)(2,1)S(1)}, bf16[64,512]{1,0:T(8,128)(2,1)S(1)}, u32[]{:S(2)}, u32[]{:S(2)}) collective-permute-start(bf16[64,512]{1,0:T(8,128)(2,1)S(1)} %get-tuple-element.34), channel_id=1, source_target_pairs={{0,1},{1,0},{2,3},{3,2},{4,5},{5,4},{6,7},{7,6},{8,9},{9,8},{10,11... | collective-permute-start | bytes 196616 | tf_op jit(solution)/shard_map/ppermute | solution.py:409
  54.3 9.3 %collective-permute-start.8 = (bf16[256,512]{1,0:T(8,128)(2,1)S(1)}, bf16[256,512]{1,0:T(8,128)(2,1)S(1)}, u32[]{:S(2)}, u32[]{:S(2)}) collective-permute-start(bf16[256,512]{1,0:T(8,128)(2,1)S(1)} %add_convert_fusion), channel_id=1, source_target_pairs={{0,2},{2,0},{1,3},{3,1},{4,6},{6,4},{5,7},{7,5},{8,10},{10,8},{9,1... | collective-permute-start | bytes 786440 | tf_op jit(solution)/shard_map/ppermute | solution.py:412
  58.9 4.8 %collective-permute-start.6 = (bf16[128,1024]{1,0:T(8,128)(2,1)S(1)}, bf16[128,1024]{1,0:T(8,128)(2,1)S(1)}, u32[]{:S(2)}, u32[]{:S(2)}) collective-permute-start(bf16[128,1024]{1,0:T(8,128)(2,1)S(1)} %get-tuple-element.39), channel_id=1, source_target_pairs={{0,1},{1,0},{2,3},{3,2},{4,5},{5,4},{6,7},{7,6},{8,9},{9,8},{10,11... | collective-permute-start | bytes 786440 | tf_op jit(solution)/shard_map/ppermute | solution.py:415
  60.2 3.5 %collective-permute-start.7 = (bf16[128,1024]{1,0:T(8,128)(2,1)S(1)}, bf16[128,1024]{1,0:T(8,128)(2,1)S(1)}, u32[]{:S(2)}, u32[]{:S(2)}) collective-permute-start(bf16[128,1024]{1,0:T(8,128)(2,1)S(1)} %get-tuple-element.40), channel_id=1, source_target_pairs={{0,1},{1,0},{2,3},{3,2},{4,5},{5,4},{6,7},{7,6},{8,9},{9,8},{10,11... | collective-permute-start | bytes 786440 | tf_op jit(solution)/shard_map/ppermute | solution.py:415

commit v5 on v3

--- a/solution.py
+++ b/solution.py
@@ -35,10 +35,9 @@
     angle = 2 * np.pi * np.arange(SPAN)[:, None] * np.arange(SPAN)[None, :] / SPAN
     cos, sin = np.cos(angle), np.sin(angle)
     forth = np.block([[cos, -sin], [sin, cos]])
-    back = np.block([[cos, sin], [-sin, cos]])
-    rows = np.arange(HALF * SUB)
-    swap = np.zeros((HALF * SUB, HALF * SUB))
-    swap[(rows % SUB) * HALF + rows // SUB, rows] = 1.0
+    rows = np.arange(SUB * SUB)
+    swap = np.zeros((SUB * SUB, SUB * SUB))
+    swap[(rows % SUB) * SUB + rows // SUB, rows] = 1.0
     bf = lambda a: jnp.asarray(a.astype(np.float32)).astype(BF16)
     return dict(
         a_filter=bf(stage_a(natural)),
@@ -46,22 +45,24 @@
         a_back=bf(stage_a_back(stored)),
         twist=jnp.asarray(np.concatenate([np.cos(twist), -np.sin(twist)], 1).astype(np.float32)),
         forth=bf(forth),
-        back=bf(back),
         swap=bf(swap),
-        unswap=bf(swap.T),
     )
 
 
 def dot(left, right):
     return jnp.dot(left, right, preferred_element_type=F32)
+
+
+def lane_of(half, high, g):
+    return ((half * 2 + high) * 2 + g) * SPAN
 
 
 def stage_a_rows(swapped, a_table, twist, mid_ref):
     t_re = jnp.concatenate([twist[:, :SPAN]] * 2, 1)
     t_im = jnp.concatenate([twist[:, SPAN:]] * 2, 1)
     for c in range(SUB):
-        block = swapped[c * HALF : (c + 1) * HALF, :]
-        rows = jnp.concatenate([block[:, : 2 * SPAN], block[:, 2 * SPAN :]], 0)
+        block = swapped[c * SUB : (c + 1) * SUB, :]
+        rows = jnp.concatenate([block[:, k * 2 * SPAN : (k + 1) * 2 * SPAN] for k in range(4)], 0)
         spec = dot(a_table, rows)
         re, im = spec[:BLOCKS], spec[BLOCKS:]
         out_re = (re * t_re - im * t_im).astype(BF16)
@@ -78,9 +79,26 @@
 SLABS = 8
 
 
+HALF_PARTS = 2
+
+
+def half_copies(side, chunk, w_hbm, w_ref, sem):
+    inner, cols = w_ref.shape
+    rows = inner // HALF_PARTS
+    start = pl.multiple_of(chunk * cols, cols)
+    return [
+        pltpu.make_async_copy(
+            w_hbm.at[pl.ds(side * inner + k * rows, rows), pl.ds(start, cols)],
+            w_ref.at[pl.ds(k * rows, rows), :],
+            sem.at[k],
+        )
+        for k in range(HALF_PARTS)
+    ]
+
+
 def filter_kernel(
-    which, h_hbm, a_hbm, twist_hbm, forth_hbm, swap_hbm, out_ref,
-    slab_ref, a_ref, twist_ref, forth_ref, swap_ref, gather_ref, mid_ref, slab_sem, table_sem,
+    which, h_hbm, w_hbm, a_hbm, twist_hbm, forth_hbm, swap_hbm, out_ref, w_ref,
+    slab_ref, a_ref, twist_ref, forth_ref, swap_ref, gather_ref, mid_ref, slab_sem, w_sem, table_sem,
 ):
     lane_block = pl.multiple_of((which[0] // 4) * SPAN, SPAN)
     piece = LENGTH // SLABS
@@ -94,7 +112,8 @@
     ]
     pairs = [(a_hbm, a_ref), (twist_hbm, twist_ref), (forth_hbm, forth_ref), (swap_hbm, swap_ref)]
     loads = [pltpu.make_async_copy(s, d, table_sem.at[k]) for k, (s, d) in enumerate(pairs)]
-    for copy in slabs + loads:
+    weights = half_copies(0, which[1], w_hbm, w_ref, w_sem)
+    for copy in slabs + loads + weights:
         copy.start()
     offset = (which[0] % 4) * GROUP
     rows = lax.broadcasted_iota(jnp.int32, (GROUP, SPAN), 0)
@@ -103,12 +122,12 @@
     for block in range(BLOCKS):
         if block % (BLOCKS // SLABS) == 0:
             slabs[block // (BLOCKS // SLABS)].wait()
-        half, a = divmod(block, HALF)
+        half, high, a = block // HALF, block // SUB % 2, block % SUB
         turned = lax.dot_general(
             pick, slab_ref[block * SPAN : (block + 1) * SPAN, :], (((1,), (1,)), ((), ())), preferred_element_type=F32
         ).astype(BF16)
         for g in range(2):
-            lane = (half * 2 + g) * SPAN
+            lane = lane_of(half, high, g)
             gather_ref[a * SUB : (a + 1) * SUB, lane : lane + SPAN] = turned[g * SUB : (g + 1) * SUB]
     for copy in loads:
         copy.wait()
@@ -117,20 +136,25 @@
     for k in range(GROUP * BLOCKS // CHUNK):
         part = slice(k * CHUNK, (k + 1) * CHUNK)
         out_ref[part, :] = dot(mid_ref[part, :], forth_ref[...]).astype(out_ref.dtype)
+    for copy in weights:
+        copy.wait()
 
 
 def conv_kernel(
-    chunks, x_ref, spec_ref, a_ref, a_back_ref, twist_ref, forth_ref, back_ref, swap_ref, unswap_ref, w_hbm,
+    chunks, x_ref, spec_ref, a_ref, a_back_ref, twist_ref, forth_ref, swap_ref, w_hbm,
     out_ref, w_ref, mid_ref, turn_ref, sem,
 ):
-    copies = weight_copies(chunks[0], w_hbm, w_ref, sem)
+    copies = half_copies(1, chunks[0], w_hbm, w_ref, sem)
     for copy in copies:
         copy.start()
     pieces = []
     for half in range(2):
-        for g in range(2):
-            piece = x_ref[:, g * SUB : (g + 1) * SUB, half * SPAN : (half + 1) * SPAN]
-            pieces.append(piece.reshape(HALF * SUB, SPAN))
+        for high in range(2):
+            for g in range(2):
+                piece = x_ref[
+                    high * SUB : (high + 1) * SUB, g * SUB : (g + 1) * SUB, half * SPAN : (half + 1) * SPAN
+                ]
+                pieces.append(piece.reshape(SUB * SUB, SPAN))
     swapped = dot(swap_ref[...], jnp.concatenate(pieces, 1)).astype(BF16)
     twist = twist_ref[...]
     stage_a_rows(swapped, a_ref[...], twist, mid_ref)
@@ -143,7 +167,7 @@
         h = spec_ref[part, :].astype(F32)
         h_re, h_im = h[:, :SPAN], h[:, SPAN:]
         prod = jnp.concatenate([x_re * h_re - x_im * h_im, x_re * h_im + x_im * h_re], 1).astype(BF16)
-        turn = dot(prod, back_ref[...])
+        turn = lax.dot_general(prod, forth_ref[...], (((1,), (1,)), ((), ())), preferred_element_type=F32)
         re, im = turn[:, :SPAN], turn[:, SPAN:]
         mid_ref[part, :SPAN] = (re * t_re + im * t_im).astype(BF16)
         mid_ref[part, SPAN:] = (im * t_re - re * t_im).astype(BF16)
@@ -155,15 +179,16 @@
                 jnp.concatenate([mid_ref[at : at + BLOCKS, :SPAN], mid_ref[at : at + BLOCKS, SPAN:]], 0)
             )
         y = dot(a_back_ref[...], jnp.concatenate(sides, 1)).astype(BF16)
-        turn_ref[c * HALF : (c + 1) * HALF, : 2 * SPAN] = y[:HALF]
-        turn_ref[c * HALF : (c + 1) * HALF, 2 * SPAN :] = y[HALF:]
-    result = dot(unswap_ref[...], turn_ref[...]).astype(BF16)
+        for k in range(4):
+            turn_ref[c * SUB : (c + 1) * SUB, k * 2 * SPAN : (k + 1) * 2 * SPAN] = y[k * SUB : (k + 1) * SUB]
+    result = dot(swap_ref[...], turn_ref[...]).astype(BF16)
     for half in range(2):
-        for g in range(2):
-            lane = (half * 2 + g) * SPAN
-            out_ref[:, g * SUB : (g + 1) * SUB, half * SPAN : (half + 1) * SPAN] = result[:, lane : lane + SPAN].reshape(
-                HALF, SUB, SPAN
-            )
+        for high in range(2):
+            for g in range(2):
+                lane = lane_of(half, high, g)
+                out_ref[
+                    high * SUB : (high + 1) * SUB, g * SUB : (g + 1) * SUB, half * SPAN : (half + 1) * SPAN
+                ] = result[:, lane : lane + SPAN].reshape(SUB, SUB, SPAN)
     for copy in copies:
         copy.wait()
 
@@ -172,45 +197,53 @@
     return tuple(pltpu.with_memory_space_constraint(a, pltpu.HBM) for a in arrays)
 
 
-def filter_spectrum(which, long_filter, t):
+def filter_spectrum(which, long_filter, weight, t):
+    half_chunk = (weight.shape[0] // 2, weight.shape[1] // 4)
+    vmem = pl.BlockSpec(memory_space=pltpu.VMEM)
     return pl.pallas_call(
         filter_kernel,
-        out_shape=jax.ShapeDtypeStruct((GROUP * BLOCKS, 2 * SPAN), BF16),
-        in_specs=[pl.BlockSpec(memory_space=pltpu.SMEM)] + [pl.BlockSpec(memory_space=pltpu.HBM)] * 5,
-        out_specs=pl.BlockSpec(memory_space=pltpu.VMEM),
+        out_shape=(
+            jax.ShapeDtypeStruct((GROUP * BLOCKS, 2 * SPAN), BF16),
+            jax.ShapeDtypeStruct(half_chunk, BF16),
+        ),
+        in_specs=[pl.BlockSpec(memory_space=pltpu.SMEM)] + [pl.BlockSpec(memory_space=pltpu.HBM)] * 6,
+        out_specs=(vmem, vmem),
         scratch_shapes=[
             pltpu.VMEM((LENGTH, SPAN), BF16),
             pltpu.VMEM((2 * BLOCKS, BLOCKS), BF16),
             pltpu.VMEM((BLOCKS, 2 * SPAN), F32),
             pltpu.VMEM((2 * SPAN, 2 * SPAN), BF16),
-            pltpu.VMEM((HALF * SUB, HALF * SUB), BF16),
-            pltpu.VMEM((HALF * SUB, 4 * SPAN), BF16),
+            pltpu.VMEM((SUB * SUB, SUB * SUB), BF16),
+            pltpu.VMEM((SUB * SUB, 8 * SPAN), BF16),
             pltpu.VMEM((GROUP * BLOCKS, 2 * SPAN), BF16),
             pltpu.SemaphoreType.DMA((SLABS,)),
+            pltpu.SemaphoreType.DMA((HALF_PARTS,)),
             pltpu.SemaphoreType.DMA((4,)),
         ],
         compiler_params=pltpu.CompilerParams(vmem_limit_bytes=32 << 20),
         name="filter_spectrum",
-    )(which, *in_hbm(long_filter, t["a_filter"], t["twist"], t["forth"], t["swap"]))
+    )(which, *in_hbm(long_filter, weight, t["a_filter"], t["twist"], t["forth"], t["swap"]))
 
 
 def convolve(chunks, x, spec, w, t):
-    inner, cols = w.shape[0], w.shape[1] // 4
     vmem = pl.BlockSpec(memory_space=pltpu.VMEM)
     return pl.pallas_call(
         conv_kernel,
-        out_shape=(pltpu.VMEM((HALF, GROUP, 2 * SPAN), BF16), pltpu.VMEM((inner, cols), BF16)),
-        in_specs=[pl.BlockSpec(memory_space=pltpu.SMEM)] + [vmem] * 9 + [pl.BlockSpec(memory_space=pltpu.HBM)],
+        out_shape=(
+            jax.ShapeDtypeStruct((HALF, GROUP, 2 * SPAN), BF16),
+            jax.ShapeDtypeStruct((w.shape[0] // 2, w.shape[1] // 4), BF16),
+        ),
+        in_specs=[pl.BlockSpec(memory_space=pltpu.SMEM)] + [vmem] * 7 + [pl.BlockSpec(memory_space=pltpu.HBM)],
         out_specs=(vmem, vmem),
         scratch_shapes=[
             pltpu.VMEM((GROUP * BLOCKS, 2 * SPAN), BF16),
-            pltpu.VMEM((HALF * SUB, 4 * SPAN), BF16),
-            pltpu.SemaphoreType.DMA((PARTS,)),
+            pltpu.VMEM((SUB * SUB, 8 * SPAN), BF16),
+            pltpu.SemaphoreType.DMA((HALF_PARTS,)),
         ],
         compiler_params=pltpu.CompilerParams(vmem_limit_bytes=32 << 20),
         name="convolve",
     )(
-        chunks, x, spec, t["a_value"], t["a_back"], t["twist"], t["forth"], t["back"], t["swap"], t["unswap"], *in_hbm(w)
+        chunks, x, spec, t["a_value"], t["a_back"], t["twist"], t["forth"], t["swap"], *in_hbm(w)
     )
 
 
@@ -264,21 +297,22 @@
     return total
 
 
-def gate_kernel(y_ref, gate_ref, w_ref, mix_ref, out_ref):
+def gate_kernel(y_ref, gate_ref, w_top_ref, w_low_ref, mix_ref, out_ref):
     turned = jnp.transpose(y_ref[...], (1, 0))
     mix = (gate_ref[...].astype(F32) * turned.astype(F32)).astype(BF16)
     mix_ref[...] = mix
-    out_ref[...] = dot(mix, w_ref[...]).astype(BF16)
-
-
-def gate_project(y, gate, w):
-    tokens, cols = gate.shape[0], w.shape[1]
+    rows = w_top_ref.shape[0]
+    out_ref[...] = (dot(mix[:, :rows], w_top_ref[...]) + dot(mix[:, rows:], w_low_ref[...])).astype(BF16)
+
+
+def gate_project(y, gate, w_top, w_low):
+    tokens, cols = gate.shape[0], w_top.shape[1]
     return pl.pallas_call(
         gate_kernel,
         out_shape=(jax.ShapeDtypeStruct(gate.shape, BF16), jax.ShapeDtypeStruct((tokens, cols), BF16)),
         compiler_params=pltpu.CompilerParams(vmem_limit_bytes=32 << 20),
         name="gate_project",
-    )(y, gate, w)
+    )(y, gate, w_top, w_low)
 
 
 def project(chunks, mix, w, dtypes):
@@ -316,11 +350,12 @@
     tokens, width = gated_value.shape
     turned = turn(gated_value).reshape(HALF, GROUP, tokens)
     x = lax.all_to_all(turned, "ctx", 0, 0, tiled=True)
-    spec = filter_spectrum(me.reshape(1), long_filter, t)
     order = jnp.arange(3, -1, -1, dtype=jnp.int32) ^ mine
-    y, w_first = convolve(order[:1], x, spec, out_weight, t)
+    which = jnp.stack([me, mine ^ 3]).astype(jnp.int32)
+    spec, w_top = filter_spectrum(which, long_filter, out_weight, t)
+    y, w_low = convolve(order[:1], x, spec, out_weight, t)
     y = lax.all_to_all(y, "ctx", 0, 0, tiled=True).reshape(width, tokens)
-    mix, away_pair = gate_project(y, query_gate, w_first)
+    mix, away_pair = gate_project(y, query_gate, w_top, w_low)
     away_in = lax.ppermute(away_pair, "ch", CORE_PAIR)
     (away_own,) = project(order[1:2], mix, out_weight, (F32,))
     away_sum = (away_own + away_in.astype(F32)).astype(BF16)

time: 61.8 us -> 62.4 us (level)
  Pallas kernels: 16.3 us -> 17.3 us
    pallas_call x2, Pallas kernels: 7.3 us -> 8.22 us  [the longest x1 4.7 us: filter_spectrum(): pl.pallas_call(filter_kernel, out_shape=(jax.ShapeDtypeStruct((GROUP * BL...]
where the time goes in v5:
time: 62.4 us; the launch traced here: 62.1 us
  Pallas kernels  17.3 us (28%)
  starting transfers between devices  16.4 us (26%)
  waiting for transfers between devices  13.3 us (21%)
  blocking collectives  13.1 us (21%)
  other arithmetic  1.27 us (2%)
  local copies, waits for them, and re-layouts  0.74 us (1%)
    all_to_all x1, blocking collectives, per_device(): y = lax.all_to_all(y, 'ctx', 0, 0, tiled=True).reshape(width, tokens)  13.1 us
    all_to_all x1, starting transfers between devices, per_device(): x = lax.all_to_all(turned, 'ctx', 0, 0, tiled=True)  9.74 us
    ppermute x1, waiting for transfers between devices, per_device(): far = lax.ppermute(away_sum, 'ch', CHIP_PAIR)  8.56 us
    pallas_call x2, Pallas kernels, project(): pl.pallas_call(kernel, out_shape=tuple((jax.ShapeDtypeStruct((tokens, col...  6.16 us
    pallas_call x1, Pallas kernels, filter_spectrum(): pl.pallas_call(filter_kernel, out_shape=(jax.ShapeDtypeStruct((GROUP * BL...  4.7 us
    all_to_all x1, waiting for transfers between devices, per_device(): x = lax.all_to_all(turned, 'ctx', 0, 0, tiled=True)  4.69 us
    ppermute x1, starting transfers between devices, per_device(): away_in = lax.ppermute(away_pair, 'ch', CORE_PAIR)  3.55 us
    pallas_call x1, Pallas kernels, convolve(): pl.pallas_call(conv_kernel, out_shape=(jax.ShapeDtypeStruct((HALF, GROUP,...  3.52 us
  transfers between devices with their start and end apart: 4, of which 2 were waited for; matrix products, arithmetic and copies ran while one was open for 1% of the time, Pallas kernels for 17%

profile of v5, /device:TPU:1, one launch (start us, length us, event | category | flops | bytes accessed | tf_op | source)
XLA Modules:
  0.0 62.1 jit_solution(16341011323805036567)
XLA Ops:
  0.0 0.0 copy-start
  0.0 0.0 copy-start.1
  0.0 0.0 copy-start.3
  0.0 0.0 copy-start.5
  0.0 0.0 copy-start.4
  0.0 2.1 %turn.1 = bf16[1024,256]{1,0:T(8,128)(2,1)} custom-call(bf16[256,1024]{1,0:T(8,128)(2,1)} %v_hbm.1), custom_call_target="tpu_custom_call" | custom-call | tf_op jit(solution)/shard_map/turn/pallas_call | solution.py:264
  2.2 9.7 %all-to-all-start = ((bf16[32,32,256]{2,1,0:T(8,128)(2,1)}), bf16[32,32,256]{2,1,0:T(8,128)(2,1)S(1)}, u32[]{:S(2)}, u32[]{:S(2)}) async-start(bf16[32,32,256]{2,1,0:T(8,128)(2,1)} %bitcast), calls=%async_computation | async-start | bytes 1048576 | tf_op jit(solution)/shard_map/all_to_all | solution.py:352
  11.9 0.1 pad_add_fusion.which
  12.0 0.0 copy-start.2
  12.0 4.7 %filter_spectrum.1 = (bf16[2048,256]{1,0:T(8,128)(2,1)S(1)}, bf16[512,1024]{1,0:T(8,128)(2,1)S(1)}) custom-call(s32[2]{0:T(128)S(1)} %pad_add_fusion.which, bf16[8192,1024]{1,0:T(8,128)(2,1)} %h_hbm.1, bf16[1024,4096]{1,0:T(8,128)(2,1)} %w_hbm.7, bf16[128,64]{1,0:T(8,128)(2,1)} %constant.32.a_hbm, f32[64,256]{1,0:T(8,128)} %constant.29.clone.twist_hbm.twist_ref, ...), custom_call_target="tpu_custom_call" | custom-call | tf_op jit(solution)/shard_map/filter_spectrum/pallas_call | solution.py:203
  16.7 0.6 %fusion = (s32[1]{0:T(128)}, s32[1]{0:T(128)}) fusion(s32[4]{0:T(128)S(1)} %add_xor_fusion), kind=kLoop, calls=%fused_computation.4 | loop fusion | bytes 16 | tf_op jit(solution)/shard_map/slice | solution.py:360
  17.4 4.7 %all-to-all-done.x_ref = bf16[32,32,256]{2,1,0:T(8,128)(2,1)S(1)} async-done(((bf16[32,32,256]{2,1,0:T(8,128)(2,1)}), bf16[32,32,256]{2,1,0:T(8,128)(2,1)S(1)}, u32[]{:S(2)}, u32[]{:S(2)}) %all-to-all-start) | async-done | bytes 524320 | tf_op jit(solution)/shard_map/all_to_all | solution.py:352
  22.1 0.0 copy-done
  22.1 0.0 copy-done.1
  22.1 0.0 copy-done.3
  22.1 0.0 copy-done.5
  22.1 0.0 copy-done.4
  22.1 3.5 %convolve.1 = (bf16[32,32,256]{2,1,0:T(8,128)(2,1)S(1)}, bf16[512,1024]{1,0:T(8,128)(2,1)S(1)}) custom-call(s32[1]{0:T(128)} %get-tuple-element.26.chunks, bf16[32,32,256]{2,1,0:T(8,128)(2,1)S(1)} %all-to-all-done.x_ref, bf16[2048,256]{1,0:T(8,128)(2,1)S(1)} %get-tuple-element.15.spec_ref, bf16[128,64]{1,0:T(8,128)(2,1)S(1)} %copy-done.4, ...), custom_call_target="tpu_custom_call" | custom-call | tf_op jit(solution)/shard_map/convolve/pallas_call | solution.py:230
  25.6 13.1 %all_to_all.10 = bf16[32,32,256]{2,1,0:T(8,128)(2,1)S(1)} all-to-all(bf16[32,32,256]{2,1,0:T(8,128)(2,1)S(1)} %get-tuple-element.16), channel_id=1, replica_groups=mesh['ctx'=32,'ch'=4] {'ctx'}, dimensions={0} | all-to-all | bytes 1048576 | tf_op jit(solution)/shard_map/all_to_all | solution.py:357
  38.7 0.0 copy-done.2
  38.7 0.8 %gate_project.1 = (bf16[256,1024]{1,0:T(8,128)(2,1)S(1)}, bf16[256,1024]{1,0:T(8,128)(2,1)S(1)}) custom-call(bf16[1024,256]{1,0:T(8,128)(2,1)S(1)} %bitcast.4, bf16[256,1024]{1,0:T(8,128)(2,1)S(1)} %copy-done.2, bf16[512,1024]{1,0:T(8,128)(2,1)S(1)} %get-tuple-element.17.w_top_ref, bf16[512,1024]{1,0:T(8,128)(2,1)S(1)} %get-tuple-element.18.w_low_ref), custom_call_target="tpu_custom_call" | custom-call | tf_op jit(solution)/shard_map/gate_project/pallas_call | solution.py:310
  39.4 3.5 %collective-permute-start = (bf16[256,1024]{1,0:T(8,128)(2,1)S(1)}, bf16[256,1024]{1,0:T(8,128)(2,1)S(1)}, u32[]{:S(2)}, u32[]{:S(2)}) collective-permute-start(bf16[256,1024]{1,0:T(8,128)(2,1)S(1)} %get-tuple-element.20), channel_id=1, source_target_pairs={{0,1},{1,0},{2,3},{3,2},{4,5},{5,4},{6,7},{7,6},{8,9},{9,8},{10,11... | collective-permute-start | bytes 1572872 | tf_op jit(solution)/shard_map/ppermute | solution.py:359
  43.0 0.1 slice.9.chunks
  43.1 2.7 %project.2 = f32[256,1024]{1,0:T(8,128)S(1)} custom-call(s32[1]{0:T(128)} %get-tuple-element.25.chunks, bf16[256,1024]{1,0:T(8,128)(2,1)S(1)} %get-tuple-element.21.mix_ref, bf16[1024,4096]{1,0:T(8,128)(2,1)} %w_hbm.7), custom_call_target="tpu_custom_call" | custom-call | tf_op jit(solution)/shard_map/project/pallas_call | solution.py:331
  45.7 0.0 collective-permute-done
  45.8 0.1 add_convert_fusion.1
  45.9 2.7 %collective-permute-start.2 = (bf16[256,1024]{1,0:T(8,128)(2,1)S(1)}, bf16[256,1024]{1,0:T(8,128)(2,1)S(1)}, u32[]{:S(2)}, u32[]{:S(2)}) collective-permute-start(bf16[256,1024]{1,0:T(8,128)(2,1)S(1)} %add_convert_fusion.1), channel_id=1, source_target_pairs={{0,2},{2,0},{1,3},{3,1},{4,6},{6,4},{5,7},{7,5},{8,10},{10,8},{9,1... | collective-permute-start | bytes 1572872 | tf_op jit(solution)/shard_map/ppermute | solution.py:363
  48.6 3.5 %project.3 = (bf16[256,1024]{1,0:T(8,128)(2,1)S(1)}, f32[256,1024]{1,0:T(8,128)S(1)}) custom-call(s32[2]{0:T(128)S(1)} %slice.9.chunks, bf16[256,1024]{1,0:T(8,128)(2,1)S(1)} %get-tuple-element.21.mix_ref, bf16[1024,4096]{1,0:T(8,128)(2,1)} %w_hbm.7), custom_call_target="tpu_custom_call" | custom-call | tf_op jit(solution)/shard_map/project/pallas_call | solution.py:331
  52.1 0.4 collective-permute-start.1
  52.5 8.6 %collective-permute-done.2 = bf16[256,1024]{1,0:T(8,128)(2,1)S(1)} collective-permute-done((bf16[256,1024]{1,0:T(8,128)(2,1)S(1)}, bf16[256,1024]{1,0:T(8,128)(2,1)S(1)}, u32[]{:S(2)}, u32[]{:S(2)}) %collective-permute-start.2) | collective-permute-done | bytes 524320 | tf_op jit(solution)/shard_map/ppermute | solution.py:363
  61.0 0.0 collective-permute-done.1
  61.0 1.0 %add_convert_fusion = bf16[256,1024]{1,0:T(8,128)(2,1)} fusion(bf16[256,1024]{1,0:T(8,128)(2,1)S(1)} %collective-permute-done.2, f32[256,1024]{1,0:T(8,128)S(1)} %get-tuple-element.22, bf16[256,1024]{1,0:T(8,128)(2,1)S(1)} %collective-permute-done.1), kind=kLoop, calls=%fused_computation | loop fusion | flops 1310720 | bytes 2621440 | tf_op jit(solution)/shard_map/convert_element_type | solution.py:366
  (1 shorter events, 0.0 us)
Async XLA Ops:
  0.0 22.1 %copy-start = (bf16[256,256]{1,0:T(8,128)(2,1)S(1)}, bf16[256,256]{1,0:T(8,128)(2,1)}, u32[]{:S(2)}) copy-start(bf16[256,256]{1,0:T(8,128)(2,1)} %constant.34.swap_hbm.swap_ref) | copy-start | bytes 393220
  0.0 22.1 %copy-start.1 = (bf16[256,256]{1,0:T(8,128)(2,1)S(1)}, bf16[256,256]{1,0:T(8,128)(2,1)}, u32[]{:S(2)}) copy-start(bf16[256,256]{1,0:T(8,128)(2,1)} %constant.33.forth_hbm.forth_ref) | copy-start | bytes 393220
  0.0 22.1 %copy-start.3 = (f32[64,256]{1,0:T(8,128)S(1)}, f32[64,256]{1,0:T(8,128)}, u32[]{:S(2)}) copy-start(f32[64,256]{1,0:T(8,128)} %constant.29.clone.twist_hbm.twist_ref) | copy-start | bytes 196612
  0.0 22.1 %copy-start.5 = (bf16[64,128]{1,0:T(8,128)(2,1)S(1)}, bf16[64,128]{1,0:T(8,128)(2,1)}, u32[]{:S(2)}) copy-start(bf16[64,128]{1,0:T(8,128)(2,1)} %constant.36.a_back_ref) | copy-start | bytes 49156
  0.0 22.1 %copy-start.4 = (bf16[128,64]{1,0:T(8,128)(2,1)S(1)}, bf16[128,64]{1,0:T(8,128)(2,1)}, u32[]{:S(2)}) copy-start(bf16[128,64]{1,0:T(8,128)(2,1)} %constant.35.a_ref) | copy-start | bytes 49156
  2.2 19.9 %all-to-all-start = ((bf16[32,32,256]{2,1,0:T(8,128)(2,1)}), bf16[32,32,256]{2,1,0:T(8,128)(2,1)S(1)}, u32[]{:S(2)}, u32[]{:S(2)}) async-start(bf16[32,32,256]{2,1,0:T(8,128)(2,1)} %bitcast), calls=%async_computation | async-start | bytes 1048576 | tf_op jit(solution)/shard_map/all_to_all | solution.py:352
  12.0 26.7 %copy-start.2 = (bf16[256,1024]{1,0:T(8,128)(2,1)S(1)}, bf16[256,1024]{1,0:T(8,128)(2,1)}, u32[]{:S(2)}) copy-start(bf16[256,1024]{1,0:T(8,128)(2,1)} %gate_ref.1) | copy-start | bytes 1572868
  39.4 6.3 %collective-permute-start = (bf16[256,1024]{1,0:T(8,128)(2,1)S(1)}, bf16[256,1024]{1,0:T(8,128)(2,1)S(1)}, u32[]{:S(2)}, u32[]{:S(2)}) collective-permute-start(bf16[256,1024]{1,0:T(8,128)(2,1)S(1)} %get-tuple-element.20), channel_id=1, source_target_pairs={{0,1},{1,0},{2,3},{3,2},{4,5},{5,4},{6,7},{7,6},{8,9},{9,8},{10,11... | collective-permute-start | bytes 1572872 | tf_op jit(solution)/shard_map/ppermute | solution.py:359
  45.9 15.1 %collective-permute-start.2 = (bf16[256,1024]{1,0:T(8,128)(2,1)S(1)}, bf16[256,1024]{1,0:T(8,128)(2,1)S(1)}, u32[]{:S(2)}, u32[]{:S(2)}) collective-permute-start(bf16[256,1024]{1,0:T(8,128)(2,1)S(1)} %add_convert_fusion.1), channel_id=1, source_target_pairs={{0,2},{2,0},{1,3},{3,1},{4,6},{6,4},{5,7},{7,5},{8,10},{10,8},{9,1... | collective-permute-start | bytes 1572872 | tf_op jit(solution)/shard_map/ppermute | solution.py:363
  52.1 8.9 %collective-permute-start.1 = (bf16[256,1024]{1,0:T(8,128)(2,1)S(1)}, bf16[256,1024]{1,0:T(8,128)(2,1)S(1)}, u32[]{:S(2)}, u32[]{:S(2)}) collective-permute-start(bf16[256,1024]{1,0:T(8,128)(2,1)S(1)} %get-tuple-element.23), channel_id=1, source_target_pairs={{0,1},{1,0},{2,3},{3,2},{4,5},{5,4},{6,7},{7,6},{8,9},{9,8},{10,11... | collective-permute-start | bytes 1572872 | tf_op jit(solution)/shard_map/ppermute | solution.py:365

commit v6 on v5

--- a/solution.py
+++ b/solution.py
@@ -79,20 +79,20 @@
 SLABS = 8
 
 
-HALF_PARTS = 2
-
-
-def half_copies(side, chunk, w_hbm, w_ref, sem):
-    inner, cols = w_ref.shape
-    rows = inner // HALF_PARTS
+QUARTERS = 4
+EARLY = 3
+
+
+def quarter_copies(first, count, chunk, w_hbm, w_ref, sem):
+    rows, cols = w_ref.shape[0] // count, w_ref.shape[1]
     start = pl.multiple_of(chunk * cols, cols)
     return [
         pltpu.make_async_copy(
-            w_hbm.at[pl.ds(side * inner + k * rows, rows), pl.ds(start, cols)],
+            w_hbm.at[pl.ds((first + k) * rows, rows), pl.ds(start, cols)],
             w_ref.at[pl.ds(k * rows, rows), :],
             sem.at[k],
         )
-        for k in range(HALF_PARTS)
+        for k in range(count)
     ]
 
 
@@ -112,7 +112,7 @@
     ]
     pairs = [(a_hbm, a_ref), (twist_hbm, twist_ref), (forth_hbm, forth_ref), (swap_hbm, swap_ref)]
     loads = [pltpu.make_async_copy(s, d, table_sem.at[k]) for k, (s, d) in enumerate(pairs)]
-    weights = half_copies(0, which[1], w_hbm, w_ref, w_sem)
+    weights = quarter_copies(0, EARLY, which[1], w_hbm, w_ref, w_sem)
     for copy in slabs + loads + weights:
         copy.start()
     offset = (which[0] % 4) * GROUP
@@ -144,7 +144,7 @@
     chunks, x_ref, spec_ref, a_ref, a_back_ref, twist_ref, forth_ref, swap_ref, w_hbm,
     out_ref, w_ref, mid_ref, turn_ref, sem,
 ):
-    copies = half_copies(1, chunks[0], w_hbm, w_ref, sem)
+    copies = quarter_copies(EARLY, QUARTERS - EARLY, chunks[0], w_hbm, w_ref, sem)
     for copy in copies:
         copy.start()
     pieces = []
@@ -171,6 +171,8 @@
         re, im = turn[:, :SPAN], turn[:, SPAN:]
         mid_ref[part, :SPAN] = (re * t_re + im * t_im).astype(BF16)
         mid_ref[part, SPAN:] = (im * t_re - re * t_im).astype(BF16)
+    for copy in copies:
+        copy.wait()
     for c in range(SUB):
         sides = []
         for g in range(2):
@@ -189,8 +191,6 @@
                 out_ref[
                     high * SUB : (high + 1) * SUB, g * SUB : (g + 1) * SUB, half * SPAN : (half + 1) * SPAN
                 ] = result[:, lane : lane + SPAN].reshape(SUB, SUB, SPAN)
-    for copy in copies:
-        copy.wait()
 
 
 def in_hbm(*arrays):
@@ -198,13 +198,13 @@
 
 
 def filter_spectrum(which, long_filter, weight, t):
-    half_chunk = (weight.shape[0] // 2, weight.shape[1] // 4)
+    early_chunk = (weight.shape[0] // QUARTERS * EARLY, weight.shape[1] // 4)
     vmem = pl.BlockSpec(memory_space=pltpu.VMEM)
     return pl.pallas_call(
         filter_kernel,
         out_shape=(
             jax.ShapeDtypeStruct((GROUP * BLOCKS, 2 * SPAN), BF16),
-            jax.ShapeDtypeStruct(half_chunk, BF16),
+            jax.ShapeDtypeStruct(early_chunk, BF16),
         ),
         in_specs=[pl.BlockSpec(memory_space=pltpu.SMEM)] + [pl.BlockSpec(memory_space=pltpu.HBM)] * 6,
         out_specs=(vmem, vmem),
@@ -217,7 +217,7 @@
             pltpu.VMEM((SUB * SUB, 8 * SPAN), BF16),
             pltpu.VMEM((GROUP * BLOCKS, 2 * SPAN), BF16),
             pltpu.SemaphoreType.DMA((SLABS,)),
-            pltpu.SemaphoreType.DMA((HALF_PARTS,)),
+            pltpu.SemaphoreType.DMA((EARLY,)),
             pltpu.SemaphoreType.DMA((4,)),
         ],
         compiler_params=pltpu.CompilerParams(vmem_limit_bytes=32 << 20),
@@ -231,14 +231,14 @@
         conv_kernel,
         out_shape=(
             jax.ShapeDtypeStruct((HALF, GROUP, 2 * SPAN), BF16),
-            jax.ShapeDtypeStruct((w.shape[0] // 2, w.shape[1] // 4), BF16),
+            jax.ShapeDtypeStruct((w.shape[0] // QUARTERS * (QUARTERS - EARLY), w.shape[1] // 4), BF16),
         ),
         in_specs=[pl.BlockSpec(memory_space=pltpu.SMEM)] + [vmem] * 7 + [pl.BlockSpec(memory_space=pltpu.HBM)],
         out_specs=(vmem, vmem),
         scratch_shapes=[
             pltpu.VMEM((GROUP * BLOCKS, 2 * SPAN), BF16),
             pltpu.VMEM((SUB * SUB, 8 * SPAN), BF16),
-            pltpu.SemaphoreType.DMA((HALF_PARTS,)),
+            pltpu.SemaphoreType.DMA((QUARTERS - EARLY,)),
         ],
         compiler_params=pltpu.CompilerParams(vmem_limit_bytes=32 << 20),
         name="convolve",

time: 62.4 us -> 62.2 us (level)
  transfers between devices with their start and end apart: 4 -> 4, of which waited for: 2 -> 2; matrix products, arithmetic and copies ran while one was open for 1% -> 1% of each run, Pallas kernels for 17% -> 18%
where the time goes in v6:
time: 62.2 us; the launch traced here: 61.8 us
  Pallas kernels  17.1 us (27%)
  starting transfers between devices  16.4 us (26%)
  waiting for transfers between devices  13.2 us (21%)
  blocking collectives  13.1 us (21%)
  other arithmetic  1.27 us (2%)
  local copies, waits for them, and re-layouts  0.74 us (1%)
    all_to_all x1, blocking collectives, per_device(): y = lax.all_to_all(y, 'ctx', 0, 0, tiled=True).reshape(width, tokens)  13.1 us
    all_to_all x1, starting transfers between devices, per_device(): x = lax.all_to_all(turned, 'ctx', 0, 0, tiled=True)  9.74 us
    ppermute x1, waiting for transfers between devices, per_device(): far = lax.ppermute(away_sum, 'ch', CHIP_PAIR)  8.55 us
    pallas_call x2, Pallas kernels, project(): pl.pallas_call(kernel, out_shape=tuple((jax.ShapeDtypeStruct((tokens, col...  6.16 us
    pallas_call x1, Pallas kernels, filter_spectrum(): pl.pallas_call(filter_kernel, out_shape=(jax.ShapeDtypeStruct((GROUP * BL...  4.71 us
    all_to_all x1, waiting for transfers between devices, per_device(): x = lax.all_to_all(turned, 'ctx', 0, 0, tiled=True)  4.65 us
    ppermute x1, starting transfers between devices, per_device(): away_in = lax.ppermute(away_pair, 'ch', CORE_PAIR)  3.55 us
    pallas_call x1, Pallas kernels, convolve(): pl.pallas_call(conv_kernel, out_shape=(jax.ShapeDtypeStruct((HALF, GROUP,...  3.37 us
  transfers between devices with their start and end apart: 4, of which 2 were waited for; matrix products, arithmetic and copies ran while one was open for 1% of the time, Pallas kernels for 18%

profile of v6, /device:TPU:1, one launch (start us, length us, event | category | flops | bytes accessed | tf_op | source)
XLA Modules:
  0.0 61.8 jit_solution(14382514657128302432)
XLA Ops:
  0.0 2.1 %turn.1 = bf16[1024,256]{1,0:T(8,128)(2,1)} custom-call(bf16[256,1024]{1,0:T(8,128)(2,1)} %v_hbm.1), custom_call_target="tpu_custom_call" | custom-call | tf_op jit(solution)/shard_map/turn/pallas_call | solution.py:264
  2.1 9.7 %all-to-all-start = ((bf16[32,32,256]{2,1,0:T(8,128)(2,1)}), bf16[32,32,256]{2,1,0:T(8,128)(2,1)S(1)}, u32[]{:S(2)}, u32[]{:S(2)}) async-start(bf16[32,32,256]{2,1,0:T(8,128)(2,1)} %bitcast), calls=%async_computation | async-start | bytes 1048576 | tf_op jit(solution)/shard_map/all_to_all | solution.py:352
  11.8 0.1 pad_add_fusion.which
  11.9 0.0 copy-start
  11.9 0.0 copy-start.1
  11.9 0.0 copy-start.3
  11.9 0.0 copy-start.4
  11.9 0.0 copy-start.5
  11.9 4.7 %filter_spectrum.1 = (bf16[2048,256]{1,0:T(8,128)(2,1)S(1)}, bf16[768,1024]{1,0:T(8,128)(2,1)S(1)}) custom-call(s32[2]{0:T(128)S(1)} %pad_add_fusion.which, bf16[8192,1024]{1,0:T(8,128)(2,1)} %h_hbm.1, bf16[1024,4096]{1,0:T(8,128)(2,1)} %w_hbm.7, bf16[128,64]{1,0:T(8,128)(2,1)} %constant.32.a_hbm, f32[64,256]{1,0:T(8,128)} %constant.29.clone.twist_hbm.twist_ref, ...), custom_call_target="tpu_custom_call" | custom-call | tf_op jit(solution)/shard_map/filter_spectrum/pallas_call | solution.py:203
  16.7 0.6 %fusion = (s32[1]{0:T(128)}, s32[1]{0:T(128)}) fusion(s32[4]{0:T(128)S(1)} %add_xor_fusion), kind=kLoop, calls=%fused_computation.4 | loop fusion | bytes 16 | tf_op jit(solution)/shard_map/slice | solution.py:360
  17.3 4.7 %all-to-all-done.x_ref = bf16[32,32,256]{2,1,0:T(8,128)(2,1)S(1)} async-done(((bf16[32,32,256]{2,1,0:T(8,128)(2,1)}), bf16[32,32,256]{2,1,0:T(8,128)(2,1)S(1)}, u32[]{:S(2)}, u32[]{:S(2)}) %all-to-all-start) | async-done | bytes 524320 | tf_op jit(solution)/shard_map/all_to_all | solution.py:352
  22.0 0.0 copy-start.2
  22.0 0.0 copy-done
  22.0 0.0 copy-done.1
  22.0 0.0 copy-done.3
  22.0 0.0 copy-done.4
  22.0 0.0 copy-done.5
  22.0 3.4 %convolve.1 = (bf16[32,32,256]{2,1,0:T(8,128)(2,1)S(1)}, bf16[256,1024]{1,0:T(8,128)(2,1)S(1)}) custom-call(s32[1]{0:T(128)} %get-tuple-element.26.chunks, bf16[32,32,256]{2,1,0:T(8,128)(2,1)S(1)} %all-to-all-done.x_ref, bf16[2048,256]{1,0:T(8,128)(2,1)S(1)} %get-tuple-element.15.spec_ref, bf16[128,64]{1,0:T(8,128)(2,1)S(1)} %copy-done.4, ...), custom_call_target="tpu_custom_call" | custom-call | tf_op jit(solution)/shard_map/convolve/pallas_call | solution.py:230
  25.4 13.1 %all_to_all.10 = bf16[32,32,256]{2,1,0:T(8,128)(2,1)S(1)} all-to-all(bf16[32,32,256]{2,1,0:T(8,128)(2,1)S(1)} %get-tuple-element.16), channel_id=1, replica_groups=mesh['ctx'=32,'ch'=4] {'ctx'}, dimensions={0} | all-to-all | bytes 1048576 | tf_op jit(solution)/shard_map/all_to_all | solution.py:357
  38.4 0.0 copy-done.2
  38.4 0.8 %gate_project.1 = (bf16[256,1024]{1,0:T(8,128)(2,1)S(1)}, bf16[256,1024]{1,0:T(8,128)(2,1)S(1)}) custom-call(bf16[1024,256]{1,0:T(8,128)(2,1)S(1)} %bitcast.4, bf16[256,1024]{1,0:T(8,128)(2,1)S(1)} %copy-done.2, bf16[768,1024]{1,0:T(8,128)(2,1)S(1)} %get-tuple-element.17.w_top_ref, bf16[256,1024]{1,0:T(8,128)(2,1)S(1)} %get-tuple-element.18.w_low_ref), custom_call_target="tpu_custom_call" | custom-call | tf_op jit(solution)/shard_map/gate_project/pallas_call | solution.py:310
  39.2 3.5 %collective-permute-start = (bf16[256,1024]{1,0:T(8,128)(2,1)S(1)}, bf16[256,1024]{1,0:T(8,128)(2,1)S(1)}, u32[]{:S(2)}, u32[]{:S(2)}) collective-permute-start(bf16[256,1024]{1,0:T(8,128)(2,1)S(1)} %get-tuple-element.20), channel_id=1, source_target_pairs={{0,1},{1,0},{2,3},{3,2},{4,5},{5,4},{6,7},{7,6},{8,9},{9,8},{10,11... | collective-permute-start | bytes 1572872 | tf_op jit(solution)/shard_map/ppermute | solution.py:359
  42.8 0.1 slice.9.chunks
  42.8 2.7 %project.2 = f32[256,1024]{1,0:T(8,128)S(1)} custom-call(s32[1]{0:T(128)} %get-tuple-element.25.chunks, bf16[256,1024]{1,0:T(8,128)(2,1)S(1)} %get-tuple-element.21.mix_ref, bf16[1024,4096]{1,0:T(8,128)(2,1)} %w_hbm.7), custom_call_target="tpu_custom_call" | custom-call | tf_op jit(solution)/shard_map/project/pallas_call | solution.py:331
  45.5 0.0 collective-permute-done
  45.5 0.1 add_convert_fusion.1
  45.7 2.7 %collective-permute-start.2 = (bf16[256,1024]{1,0:T(8,128)(2,1)S(1)}, bf16[256,1024]{1,0:T(8,128)(2,1)S(1)}, u32[]{:S(2)}, u32[]{:S(2)}) collective-permute-start(bf16[256,1024]{1,0:T(8,128)(2,1)S(1)} %add_convert_fusion.1), channel_id=1, source_target_pairs={{0,2},{2,0},{1,3},{3,1},{4,6},{6,4},{5,7},{7,5},{8,10},{10,8},{9,1... | collective-permute-start | bytes 1572872 | tf_op jit(solution)/shard_map/ppermute | solution.py:363
  48.4 3.5 %project.3 = (bf16[256,1024]{1,0:T(8,128)(2,1)S(1)}, f32[256,1024]{1,0:T(8,128)S(1)}) custom-call(s32[2]{0:T(128)S(1)} %slice.9.chunks, bf16[256,1024]{1,0:T(8,128)(2,1)S(1)} %get-tuple-element.21.mix_ref, bf16[1024,4096]{1,0:T(8,128)(2,1)} %w_hbm.7), custom_call_target="tpu_custom_call" | custom-call | tf_op jit(solution)/shard_map/project/pallas_call | solution.py:331
  51.9 0.4 collective-permute-start.1
  52.2 8.6 %collective-permute-done.2 = bf16[256,1024]{1,0:T(8,128)(2,1)S(1)} collective-permute-done((bf16[256,1024]{1,0:T(8,128)(2,1)S(1)}, bf16[256,1024]{1,0:T(8,128)(2,1)S(1)}, u32[]{:S(2)}, u32[]{:S(2)}) %collective-permute-start.2) | collective-permute-done | bytes 524320 | tf_op jit(solution)/shard_map/ppermute | solution.py:363
  60.8 0.0 collective-permute-done.1
  60.8 1.0 %add_convert_fusion = bf16[256,1024]{1,0:T(8,128)(2,1)} fusion(bf16[256,1024]{1,0:T(8,128)(2,1)S(1)} %collective-permute-done.2, f32[256,1024]{1,0:T(8,128)S(1)} %get-tuple-element.22, bf16[256,1024]{1,0:T(8,128)(2,1)S(1)} %collective-permute-done.1), kind=kLoop, calls=%fused_computation | loop fusion | flops 1310720 | bytes 2621440 | tf_op jit(solution)/shard_map/convert_element_type | solution.py:366
  (1 shorter events, 0.0 us)
Async XLA Ops:
  2.1 19.9 %all-to-all-start = ((bf16[32,32,256]{2,1,0:T(8,128)(2,1)}), bf16[32,32,256]{2,1,0:T(8,128)(2,1)S(1)}, u32[]{:S(2)}, u32[]{:S(2)}) async-start(bf16[32,32,256]{2,1,0:T(8,128)(2,1)} %bitcast), calls=%async_computation | async-start | bytes 1048576 | tf_op jit(solution)/shard_map/all_to_all | solution.py:352
  11.9 10.1 %copy-start = (bf16[256,256]{1,0:T(8,128)(2,1)S(1)}, bf16[256,256]{1,0:T(8,128)(2,1)}, u32[]{:S(2)}) copy-start(bf16[256,256]{1,0:T(8,128)(2,1)} %constant.34.swap_hbm.swap_ref) | copy-start | bytes 393220
  11.9 10.1 %copy-start.1 = (bf16[256,256]{1,0:T(8,128)(2,1)S(1)}, bf16[256,256]{1,0:T(8,128)(2,1)}, u32[]{:S(2)}) copy-start(bf16[256,256]{1,0:T(8,128)(2,1)} %constant.33.forth_hbm.forth_ref) | copy-start | bytes 393220
  11.9 10.1 %copy-start.3 = (f32[64,256]{1,0:T(8,128)S(1)}, f32[64,256]{1,0:T(8,128)}, u32[]{:S(2)}) copy-start(f32[64,256]{1,0:T(8,128)} %constant.29.clone.twist_hbm.twist_ref) | copy-start | bytes 196612
  11.9 10.1 %copy-start.4 = (bf16[128,64]{1,0:T(8,128)(2,1)S(1)}, bf16[128,64]{1,0:T(8,128)(2,1)}, u32[]{:S(2)}) copy-start(bf16[128,64]{1,0:T(8,128)(2,1)} %constant.35.a_ref) | copy-start | bytes 49156
  11.9 10.1 %copy-start.5 = (bf16[64,128]{1,0:T(8,128)(2,1)S(1)}, bf16[64,128]{1,0:T(8,128)(2,1)}, u32[]{:S(2)}) copy-start(bf16[64,128]{1,0:T(8,128)(2,1)} %constant.36.a_back_ref) | copy-start | bytes 49156
  22.0 16.5 %copy-start.2 = (bf16[256,1024]{1,0:T(8,128)(2,1)S(1)}, bf16[256,1024]{1,0:T(8,128)(2,1)}, u32[]{:S(2)}) copy-start(bf16[256,1024]{1,0:T(8,128)(2,1)} %gate_ref.1) | copy-start | bytes 1572868
  39.2 6.3 %collective-permute-start = (bf16[256,1024]{1,0:T(8,128)(2,1)S(1)}, bf16[256,1024]{1,0:T(8,128)(2,1)S(1)}, u32[]{:S(2)}, u32[]{:S(2)}) collective-permute-start(bf16[256,1024]{1,0:T(8,128)(2,1)S(1)} %get-tuple-element.20), channel_id=1, source_target_pairs={{0,1},{1,0},{2,3},{3,2},{4,5},{5,4},{6,7},{7,6},{8,9},{9,8},{10,11... | collective-permute-start | bytes 1572872 | tf_op jit(solution)/shard_map/ppermute | solution.py:359
  45.7 15.1 %collective-permute-start.2 = (bf16[256,1024]{1,0:T(8,128)(2,1)S(1)}, bf16[256,1024]{1,0:T(8,128)(2,1)S(1)}, u32[]{:S(2)}, u32[]{:S(2)}) collective-permute-start(bf16[256,1024]{1,0:T(8,128)(2,1)S(1)} %add_convert_fusion.1), channel_id=1, source_target_pairs={{0,2},{2,0},{1,3},{3,1},{4,6},{6,4},{5,7},{7,5},{8,10},{10,8},{9,1... | collective-permute-start | bytes 1572872 | tf_op jit(solution)/shard_map/ppermute | solution.py:363
  51.9 8.9 %collective-permute-start.1 = (bf16[256,1024]{1,0:T(8,128)(2,1)S(1)}, bf16[256,1024]{1,0:T(8,128)(2,1)S(1)}, u32[]{:S(2)}, u32[]{:S(2)}) collective-permute-start(bf16[256,1024]{1,0:T(8,128)(2,1)S(1)} %get-tuple-element.23), channel_id=1, source_target_pairs={{0,1},{1,0},{2,3},{3,2},{4,5},{5,4},{6,7},{7,6},{8,9},{9,8},{10,11... | collective-permute-start | bytes 1572872 | tf_op jit(solution)/shard_map/ppermute | solution.py:365

commit v7 on v3

--- a/solution.py
+++ b/solution.py
@@ -281,24 +281,28 @@
     )(y, gate, w)
 
 
-def project(chunks, mix, w, dtypes):
+def project(chunks, mix, w, targets):
     tokens, inner, cols = mix.shape[0], w.shape[0], w.shape[1] // 4
-    count = len(dtypes)
+    count = 1 + max(j for j, _, _ in targets)
+    pieces = [(j, dtype, k * tokens // n, tokens // n) for j, dtype, n in targets for k in range(n)]
     vmem = pl.BlockSpec(memory_space=pltpu.VMEM)
 
     def kernel(chunks, mix_ref, w_hbm, *refs):
-        out_refs, (w_ref, sem) = refs[:count], refs[count:]
+        out_refs, (w_ref, sem) = refs[: len(pieces)], refs[len(pieces) :]
         copies = [weight_copies(chunks[j], w_hbm, w_ref.at[j], sem.at[j]) for j in range(count)]
         for copy in sum(copies, []):
             copy.start()
         for j in range(count):
-            out_refs[j][...] = product(mix_ref, w_ref.at[j], copies[j]).astype(dtypes[j])
+            out = product(mix_ref, w_ref.at[j], copies[j])
+            for (position, dtype, start, rows), out_ref in zip(pieces, out_refs):
+                if position == j:
+                    out_ref[...] = out[start : start + rows].astype(dtype)
 
     return pl.pallas_call(
         kernel,
-        out_shape=tuple(jax.ShapeDtypeStruct((tokens, cols), d) for d in dtypes),
+        out_shape=tuple(jax.ShapeDtypeStruct((rows, cols), dtype) for _, dtype, _, rows in pieces),
         in_specs=[pl.BlockSpec(memory_space=pltpu.SMEM), vmem, pl.BlockSpec(memory_space=pltpu.HBM)],
-        out_specs=(vmem,) * count,
+        out_specs=(vmem,) * len(pieces),
         scratch_shapes=[pltpu.VMEM((count, inner, cols), BF16), pltpu.SemaphoreType.DMA((count, PARTS))],
         compiler_params=pltpu.CompilerParams(vmem_limit_bytes=32 << 20),
         name="project",
@@ -317,17 +321,16 @@
     turned = turn(gated_value).reshape(HALF, GROUP, tokens)
     x = lax.all_to_all(turned, "ctx", 0, 0, tiled=True)
     spec = filter_spectrum(me.reshape(1), long_filter, t)
-    order = jnp.arange(3, -1, -1, dtype=jnp.int32) ^ mine
-    y, w_first = convolve(order[:1], x, spec, out_weight, t)
+    y, w_first = convolve((mine ^ 3).reshape(1), x, spec, out_weight, t)
     y = lax.all_to_all(y, "ctx", 0, 0, tiled=True).reshape(width, tokens)
     mix, away_pair = gate_project(y, query_gate, w_first)
     away_in = lax.ppermute(away_pair, "ch", CORE_PAIR)
-    (away_own,) = project(order[1:2], mix, out_weight, (F32,))
+    (away_own,) = project((mine ^ 2).reshape(1), mix, out_weight, ((0, F32, 1),))
     away_sum = (away_own + away_in.astype(F32)).astype(BF16)
     mix, away_sum = lax.optimization_barrier((mix, away_sum))
     far = lax.ppermute(away_sum, "ch", CHIP_PAIR)
-    home_pair, home_own = project(order[2:], mix, out_weight, (BF16, F32))
-    near = lax.ppermute(home_pair, "ch", CORE_PAIR)
+    *home_pair, home_own = project(jnp.stack([mine ^ 1, mine]), mix, out_weight, ((0, BF16, 2), (1, F32, 1)))
+    near = jnp.concatenate([lax.ppermute(piece, "ch", CORE_PAIR) for piece in home_pair])
     return (home_own + near.astype(F32) + far.astype(F32)).astype(BF16)
 
 

time: 61.8 us -> 60.6 us (0.981)
  Pallas kernels: 16.3 us -> 15.1 us
  local copies, waits for them, and re-layouts: 0.73 us -> 0.05 us
    ppermute x1, waiting for transfers between devices: 8.55 us -> 6.86 us  [per_device(): far = lax.ppermute(away_sum, 'ch', CHIP_PAIR)]
    ppermute x1 -> x2, waiting for transfers between devices: 0.01 us -> 1.4 us  [per_device(): lax.ppermute(piece, 'ch', CORE_PAIR)]
    slice x2 -> x0, local copies, waits for them, and re-layouts: 0.68 us -> none  [the longest x1 0.61 us: per_device(): away_own, = project(order[1:2], mix, out_weight, (F32,))]
    pallas_call x2, Pallas kernels: 6.18 us -> 5.54 us  [project(): pl.pallas_call(kernel, out_shape=tuple((jax.ShapeDtypeStruct((rows, cols)...]
    all_to_all x1, waiting for transfers between devices: 5.13 us -> 5.75 us  [per_device(): x = lax.all_to_all(turned, 'ctx', 0, 0, tiled=True)]
  transfers between devices with their start and end apart: 4 -> 5, of which waited for: 2 -> 4; matrix products, arithmetic and copies ran while one was open for 1% -> 0% of each run, Pallas kernels for 17% -> 16%
where the time goes in v7:
time: 60.6 us; the launch traced here: 60.3 us
  starting transfers between devices  16.6 us (27%)
  Pallas kernels  15.1 us (25%)
  waiting for transfers between devices  14 us (23%)
  blocking collectives  13.1 us (22%)
  other arithmetic  1.29 us (2%)
    all_to_all x1, blocking collectives, per_device(): y = lax.all_to_all(y, 'ctx', 0, 0, tiled=True).reshape(width, tokens)  13.1 us
    all_to_all x1, starting transfers between devices, per_device(): x = lax.all_to_all(turned, 'ctx', 0, 0, tiled=True)  9.74 us
    ppermute x1, waiting for transfers between devices, per_device(): far = lax.ppermute(away_sum, 'ch', CHIP_PAIR)  6.86 us
    all_to_all x1, waiting for transfers between devices, per_device(): x = lax.all_to_all(turned, 'ctx', 0, 0, tiled=True)  5.75 us
    pallas_call x2, Pallas kernels, project(): pl.pallas_call(kernel, out_shape=tuple((jax.ShapeDtypeStruct((rows, cols)...  5.54 us
    pallas_call x1, Pallas kernels, filter_spectrum(): pl.pallas_call(filter_kernel, out_shape=jax.ShapeDtypeStruct((GROUP * BLO...  4.27 us
    ppermute x1, starting transfers between devices, per_device(): away_in = lax.ppermute(away_pair, 'ch', CORE_PAIR)  3.54 us
    ppermute x1, starting transfers between devices, per_device(): far = lax.ppermute(away_sum, 'ch', CHIP_PAIR)  2.7 us
  transfers between devices with their start and end apart: 5, of which 4 were waited for; matrix products, arithmetic and copies ran while one was open for 0% of the time, Pallas kernels for 16%

profile of v7, /device:TPU:1, one launch (start us, length us, event | category | flops | bytes accessed | tf_op | source)
XLA Modules:
  0.0 60.3 jit_solution(16099934084773906944)
XLA Ops:
  0.0 2.1 %turn.1 = bf16[1024,256]{1,0:T(8,128)(2,1)} custom-call(bf16[256,1024]{1,0:T(8,128)(2,1)} %v_hbm.1), custom_call_target="tpu_custom_call" | custom-call | tf_op jit(solution)/shard_map/turn/pallas_call | solution.py:231
  2.1 9.7 %all-to-all-start = ((bf16[32,32,256]{2,1,0:T(8,128)(2,1)}), bf16[32,32,256]{2,1,0:T(8,128)(2,1)S(1)}, u32[]{:S(2)}, u32[]{:S(2)}) async-start(bf16[32,32,256]{2,1,0:T(8,128)(2,1)} %bitcast.3), calls=%async_computation | async-start | bytes 1048576 | tf_op jit(solution)/shard_map/all_to_all | solution.py:322
  11.8 0.0 copy-start
  11.9 0.0 copy-start.1
  11.9 0.0 copy-start.2
  11.9 0.0 copy-start.4
  11.9 0.0 copy-start.5
  11.9 0.0 copy-start.6
  11.9 0.0 copy-start.7
  11.9 4.3 %filter_spectrum.1.spec_ref = bf16[2048,256]{1,0:T(8,128)(2,1)S(1)} custom-call(s32[1]{0:T(128)} %bitcast.4.which, bf16[8192,1024]{1,0:T(8,128)(2,1)} %h_hbm.1, bf16[128,64]{1,0:T(8,128)(2,1)} %constant.39.a_hbm, f32[64,256]{1,0:T(8,128)} %constant.34.clone.twist_hbm.twist_ref, bf16[256,256]{1,0:T(8,128)(2,1)} %constant.40.forth_hbm.forth_ref, ...), custom_call_target="tpu_custom_call" | custom-call | tf_op jit(solution)/shard_map/filter_spectrum/pallas_call | solution.py:176
  16.2 0.0 copy-start.3
  16.2 5.7 %all-to-all-done.x_ref = bf16[32,32,256]{2,1,0:T(8,128)(2,1)S(1)} async-done(((bf16[32,32,256]{2,1,0:T(8,128)(2,1)}), bf16[32,32,256]{2,1,0:T(8,128)(2,1)S(1)}, u32[]{:S(2)}, u32[]{:S(2)}) %all-to-all-start) | async-done | bytes 524320 | tf_op jit(solution)/shard_map/all_to_all | solution.py:322
  22.0 0.0 copy-done
  22.0 0.0 copy-done.1
  22.0 0.0 copy-done.2
  22.0 0.0 copy-done.4
  22.0 0.0 copy-done.5
  22.0 0.0 copy-done.6
  22.0 0.0 copy-done.7
  22.0 2.5 %convolve.1 = (bf16[32,32,256]{2,1,0:T(8,128)(2,1)S(1)}, bf16[1024,1024]{1,0:T(8,128)(2,1)S(1)}) custom-call(s32[1]{0:T(128)} %bitcast.2.chunks, bf16[32,32,256]{2,1,0:T(8,128)(2,1)S(1)} %all-to-all-done.x_ref, bf16[2048,256]{1,0:T(8,128)(2,1)S(1)} %filter_spectrum.1.spec_ref, bf16[128,64]{1,0:T(8,128)(2,1)S(1)} %copy-done.6, bf16[64,128]{1,0:T(8,128)(2,1)S(1)} %copy-done.7, ...), custom_call_target="tpu_custom_call" | custom-call | tf_op jit(solution)/shard_map/convolve/pallas_call | solution.py:200
  24.5 13.1 %all_to_all.10 = bf16[32,32,256]{2,1,0:T(8,128)(2,1)S(1)} all-to-all(bf16[32,32,256]{2,1,0:T(8,128)(2,1)S(1)} %get-tuple-element.14), channel_id=1, replica_groups=mesh['ctx'=32,'ch'=4] {'ctx'}, dimensions={0} | all-to-all | bytes 1048576 | tf_op jit(solution)/shard_map/all_to_all | solution.py:325
  37.6 0.0 copy-done.3
  37.6 0.7 %gate_project.1 = (bf16[256,1024]{1,0:T(8,128)(2,1)S(1)}, bf16[256,1024]{1,0:T(8,128)(2,1)S(1)}) custom-call(bf16[1024,256]{1,0:T(8,128)(2,1)S(1)} %bitcast.7, bf16[256,1024]{1,0:T(8,128)(2,1)S(1)} %copy-done.3, bf16[1024,1024]{1,0:T(8,128)(2,1)S(1)} %get-tuple-element.15.w_ref), custom_call_target="tpu_custom_call" | custom-call | tf_op jit(solution)/shard_map/gate_project/pallas_call | solution.py:276
  38.3 3.5 %collective-permute-start = (bf16[256,1024]{1,0:T(8,128)(2,1)S(1)}, bf16[256,1024]{1,0:T(8,128)(2,1)S(1)}, u32[]{:S(2)}, u32[]{:S(2)}) collective-permute-start(bf16[256,1024]{1,0:T(8,128)(2,1)S(1)} %get-tuple-element.17), channel_id=1, source_target_pairs={{0,1},{1,0},{2,3},{3,2},{4,5},{5,4},{6,7},{7,6},{8,9},{9,8},{10,11... | collective-permute-start | bytes 1572872 | tf_op jit(solution)/shard_map/ppermute | solution.py:327
  41.9 2.1 %project.2 = f32[256,1024]{1,0:T(8,128)S(1)} custom-call(s32[1]{0:T(128)} %bitcast.6.chunks, bf16[256,1024]{1,0:T(8,128)(2,1)S(1)} %get-tuple-element.18.mix_ref, bf16[1024,4096]{1,0:T(8,128)(2,1)} %w_hbm.5), custom_call_target="tpu_custom_call" | custom-call | tf_op jit(solution)/shard_map/project/pallas_call | solution.py:301
  43.9 0.0 collective-permute-done
  43.9 0.2 add_convert_fusion.1
  44.1 2.7 %collective-permute-start.3 = (bf16[256,1024]{1,0:T(8,128)(2,1)S(1)}, bf16[256,1024]{1,0:T(8,128)(2,1)S(1)}, u32[]{:S(2)}, u32[]{:S(2)}) collective-permute-start(bf16[256,1024]{1,0:T(8,128)(2,1)S(1)} %add_convert_fusion.1), channel_id=1, source_target_pairs={{0,2},{2,0},{1,3},{3,1},{4,6},{6,4},{5,7},{7,5},{8,10},{10,8},{9,1... | collective-permute-start | bytes 1572872 | tf_op jit(solution)/shard_map/ppermute | solution.py:331
  46.8 0.1 pad_add_fusion.chunks
  46.9 3.5 %project.3 = (bf16[128,1024]{1,0:T(8,128)(2,1)S(1)}, bf16[128,1024]{1,0:T(8,128)(2,1)S(1)}, f32[256,1024]{1,0:T(8,128)S(1)}) custom-call(s32[2]{0:T(128)S(1)} %pad_add_fusion.chunks, bf16[256,1024]{1,0:T(8,128)(2,1)S(1)} %get-tuple-element.18.mix_ref, bf16[1024,4096]{1,0:T(8,128)(2,1)} %w_hbm.5), custom_call_target="tpu_custom_call" | custom-call | tf_op jit(solution)/shard_map/project/pallas_call | solution.py:301
  50.4 0.4 collective-permute-start.1
  50.8 0.2 collective-permute-start.2
  51.0 1.0 %collective-permute-done.1 = bf16[128,1024]{1,0:T(8,128)(2,1)S(1)} collective-permute-done((bf16[128,1024]{1,0:T(8,128)(2,1)S(1)}, bf16[128,1024]{1,0:T(8,128)(2,1)S(1)}, u32[]{:S(2)}, u32[]{:S(2)}) %collective-permute-start.1) | collective-permute-done | bytes 262176 | tf_op jit(solution)/shard_map/ppermute | solution.py:333
  52.0 0.4 collective-permute-done.2
  52.4 6.9 %collective-permute-done.3 = bf16[256,1024]{1,0:T(8,128)(2,1)S(1)} collective-permute-done((bf16[256,1024]{1,0:T(8,128)(2,1)S(1)}, bf16[256,1024]{1,0:T(8,128)(2,1)S(1)}, u32[]{:S(2)}, u32[]{:S(2)}) %collective-permute-start.3) | collective-permute-done | bytes 524320 | tf_op jit(solution)/shard_map/ppermute | solution.py:331
  59.2 1.0 %add_convert_fusion = bf16[256,1024]{1,0:T(8,128)(2,1)} fusion(bf16[256,1024]{1,0:T(8,128)(2,1)S(1)} %collective-permute-done.3, f32[256,1024]{1,0:T(8,128)S(1)} %get-tuple-element.19, bf16[128,1024]{1,0:T(8,128)(2,1)S(1)} %collective-permute-done.2, bf16[128,1024]{1,0:T(8,128)(2,1)S(1)} %collective-permute-done.1), kind=kLoop, calls=%fused_computation | loop fusion | flops 2097152 | bytes 2621440 | tf_op jit(solution)/shard_map/convert_element_type | solution.py:334
Async XLA Ops:
  2.1 19.9 %all-to-all-start = ((bf16[32,32,256]{2,1,0:T(8,128)(2,1)}), bf16[32,32,256]{2,1,0:T(8,128)(2,1)S(1)}, u32[]{:S(2)}, u32[]{:S(2)}) async-start(bf16[32,32,256]{2,1,0:T(8,128)(2,1)} %bitcast.3), calls=%async_computation | async-start | bytes 1048576 | tf_op jit(solution)/shard_map/all_to_all | solution.py:322
  11.8 10.1 %copy-start = (bf16[512,512]{1,0:T(8,128)(2,1)S(1)}, bf16[512,512]{1,0:T(8,128)(2,1)}, u32[]{:S(2)}) copy-start(bf16[512,512]{1,0:T(8,128)(2,1)} %constant.41.swap_hbm.swap_ref) | copy-start | bytes 1572868
  11.9 10.1 %copy-start.1 = (bf16[256,256]{1,0:T(8,128)(2,1)S(1)}, bf16[256,256]{1,0:T(8,128)(2,1)}, u32[]{:S(2)}) copy-start(bf16[256,256]{1,0:T(8,128)(2,1)} %constant.40.forth_hbm.forth_ref) | copy-start | bytes 393220
  11.9 10.1 %copy-start.2 = (bf16[512,512]{1,0:T(8,128)(2,1)S(1)}, bf16[512,512]{1,0:T(8,128)(2,1)}, u32[]{:S(2)}) copy-start(bf16[512,512]{1,0:T(8,128)(2,1)} %constant.45.unswap_ref) | copy-start | bytes 1572868
  11.9 10.1 %copy-start.4 = (f32[64,256]{1,0:T(8,128)S(1)}, f32[64,256]{1,0:T(8,128)}, u32[]{:S(2)}) copy-start(f32[64,256]{1,0:T(8,128)} %constant.34.clone.twist_hbm.twist_ref) | copy-start | bytes 196612
  11.9 10.1 %copy-start.5 = (bf16[256,256]{1,0:T(8,128)(2,1)S(1)}, bf16[256,256]{1,0:T(8,128)(2,1)}, u32[]{:S(2)}) copy-start(bf16[256,256]{1,0:T(8,128)(2,1)} %constant.44.back_ref) | copy-start | bytes 393220
  11.9 10.1 %copy-start.6 = (bf16[128,64]{1,0:T(8,128)(2,1)S(1)}, bf16[128,64]{1,0:T(8,128)(2,1)}, u32[]{:S(2)}) copy-start(bf16[128,64]{1,0:T(8,128)(2,1)} %constant.42.a_ref) | copy-start | bytes 49156
  11.9 10.1 %copy-start.7 = (bf16[64,128]{1,0:T(8,128)(2,1)S(1)}, bf16[64,128]{1,0:T(8,128)(2,1)}, u32[]{:S(2)}) copy-start(bf16[64,128]{1,0:T(8,128)(2,1)} %constant.43.a_back_ref) | copy-start | bytes 49156
  16.2 21.4 %copy-start.3 = (bf16[256,1024]{1,0:T(8,128)(2,1)S(1)}, bf16[256,1024]{1,0:T(8,128)(2,1)}, u32[]{:S(2)}) copy-start(bf16[256,1024]{1,0:T(8,128)(2,1)} %gate_ref.1) | copy-start | bytes 1572868
  38.3 5.6 %collective-permute-start = (bf16[256,1024]{1,0:T(8,128)(2,1)S(1)}, bf16[256,1024]{1,0:T(8,128)(2,1)S(1)}, u32[]{:S(2)}, u32[]{:S(2)}) collective-permute-start(bf16[256,1024]{1,0:T(8,128)(2,1)S(1)} %get-tuple-element.17), channel_id=1, source_target_pairs={{0,1},{1,0},{2,3},{3,2},{4,5},{5,4},{6,7},{7,6},{8,9},{9,8},{10,11... | collective-permute-start | bytes 1572872 | tf_op jit(solution)/shard_map/ppermute | solution.py:327
  44.1 15.1 %collective-permute-start.3 = (bf16[256,1024]{1,0:T(8,128)(2,1)S(1)}, bf16[256,1024]{1,0:T(8,128)(2,1)S(1)}, u32[]{:S(2)}, u32[]{:S(2)}) collective-permute-start(bf16[256,1024]{1,0:T(8,128)(2,1)S(1)} %add_convert_fusion.1), channel_id=1, source_target_pairs={{0,2},{2,0},{1,3},{3,1},{4,6},{6,4},{5,7},{7,5},{8,10},{10,8},{9,1... | collective-permute-start | bytes 1572872 | tf_op jit(solution)/shard_map/ppermute | solution.py:331
  50.4 1.6 %collective-permute-start.1 = (bf16[128,1024]{1,0:T(8,128)(2,1)S(1)}, bf16[128,1024]{1,0:T(8,128)(2,1)S(1)}, u32[]{:S(2)}, u32[]{:S(2)}) collective-permute-start(bf16[128,1024]{1,0:T(8,128)(2,1)S(1)} %get-tuple-element.20), channel_id=1, source_target_pairs={{0,1},{1,0},{2,3},{3,2},{4,5},{5,4},{6,7},{7,6},{8,9},{9,8},{10,11... | collective-permute-start | bytes 786440 | tf_op jit(solution)/shard_map/ppermute | solution.py:333
  50.8 1.6 %collective-permute-start.2 = (bf16[128,1024]{1,0:T(8,128)(2,1)S(1)}, bf16[128,1024]{1,0:T(8,128)(2,1)S(1)}, u32[]{:S(2)}, u32[]{:S(2)}) collective-permute-start(bf16[128,1024]{1,0:T(8,128)(2,1)S(1)} %get-tuple-element.21), channel_id=1, source_target_pairs={{0,1},{1,0},{2,3},{3,2},{4,5},{5,4},{6,7},{7,6},{8,9},{9,8},{10,11... | collective-permute-start | bytes 786440 | tf_op jit(solution)/shard_map/ppermute | solution.py:333

commit v8 on v7

--- a/solution.py
+++ b/solution.py
@@ -123,9 +123,19 @@
     chunks, x_ref, spec_ref, a_ref, a_back_ref, twist_ref, forth_ref, back_ref, swap_ref, unswap_ref, w_hbm,
     out_ref, w_ref, mid_ref, turn_ref, sem,
 ):
-    copies = weight_copies(chunks[0], w_hbm, w_ref, sem)
-    for copy in copies:
-        copy.start()
+    rows, cols = w_ref.shape[0] // PARTS, w_ref.shape[1]
+    start = pl.multiple_of(chunks[0] * cols, cols)
+
+    def weight_copy(k):
+        part = pl.ds(pl.multiple_of(k * rows, rows), rows)
+        return pltpu.make_async_copy(w_hbm.at[part, pl.ds(start, cols)], w_ref.at[part, :], sem.at[k])
+
+    def begin(k, carry):
+        weight_copy(k).start()
+        return carry
+
+    lax.fori_loop(0, PARTS, begin, 0)
+    copies = [weight_copy(k) for k in range(PARTS)]
     pieces = []
     for half in range(2):
         for g in range(2):
@@ -309,6 +319,39 @@
     )(chunks, mix, *in_hbm(w))
 
 
+def finish(home, near, far):
+    tokens, cols = home.shape
+    rows = tokens // PARTS
+    each = near[0].shape[0]
+
+    def kernel(home_ref, *refs):
+        near_refs, (far_ref, out_hbm, sum_ref, sem) = refs[: len(near)], refs[len(near) :]
+        copies = []
+        for k in range(PARTS):
+            part = slice(k * rows, (k + 1) * rows)
+            piece, first = divmod(k * rows, each)
+            other = near_refs[piece][first : first + rows, :]
+            total = home_ref[part, :] + other.astype(F32) + far_ref[part, :].astype(F32)
+            sum_ref[part, :] = total.astype(BF16)
+            copy = pltpu.make_async_copy(
+                sum_ref.at[pl.ds(k * rows, rows), :], out_hbm.at[pl.ds(k * rows, rows), :], sem.at[k]
+            )
+            copy.start()
+            copies.append(copy)
+        for copy in copies:
+            copy.wait()
+
+    return pl.pallas_call(
+        kernel,
+        out_shape=jax.ShapeDtypeStruct(home.shape, BF16),
+        in_specs=[pl.BlockSpec(memory_space=pltpu.VMEM)] * (2 + len(near)),
+        out_specs=pl.BlockSpec(memory_space=pltpu.HBM),
+        scratch_shapes=[pltpu.VMEM(home.shape, BF16), pltpu.SemaphoreType.DMA((PARTS,))],
+        compiler_params=pltpu.CompilerParams(vmem_limit_bytes=16 << 20),
+        name="finish",
+    )(home, *near, far)
+
+
 CORE_PAIR = [(0, 1), (1, 0), (2, 3), (3, 2)]
 CHIP_PAIR = [(0, 2), (2, 0), (1, 3), (3, 1)]
 
@@ -330,8 +373,8 @@
     mix, away_sum = lax.optimization_barrier((mix, away_sum))
     far = lax.ppermute(away_sum, "ch", CHIP_PAIR)
     *home_pair, home_own = project(jnp.stack([mine ^ 1, mine]), mix, out_weight, ((0, BF16, 2), (1, F32, 1)))
-    near = jnp.concatenate([lax.ppermute(piece, "ch", CORE_PAIR) for piece in home_pair])
-    return (home_own + near.astype(F32) + far.astype(F32)).astype(BF16)
+    near = [lax.ppermute(piece, "ch", CORE_PAIR) for piece in home_pair]
+    return finish(home_own, near, far)
 
 
 def solution(mesh):

time: 60.6 us -> 60 us (0.990)
  other arithmetic: 1.29 us -> 0.24 us
    convert_element_type x1 -> x0, other arithmetic: 1.05 us -> none  [per_device(): return (home_own + near.astype(F32) + far.astype(F32)).astype(BF16)]
    pallas_call x0 -> x1, Pallas kernels: none -> 0.88 us  [finish(): pl.pallas_call(kernel, out_shape=jax.ShapeDtypeStruct(home.shape, BF16),...]
where the time goes in v8:
time: 60 us; the launch traced here: 59.7 us
  starting transfers between devices  16.6 us (28%)
  Pallas kernels  15.6 us (26%)
  waiting for transfers between devices  14 us (23%)
  blocking collectives  13.1 us (22%)
    all_to_all x1, blocking collectives, per_device(): y = lax.all_to_all(y, 'ctx', 0, 0, tiled=True).reshape(width, tokens)  13.1 us
    all_to_all x1, starting transfers between devices, per_device(): x = lax.all_to_all(turned, 'ctx', 0, 0, tiled=True)  9.74 us
    ppermute x1, waiting for transfers between devices, per_device(): far = lax.ppermute(away_sum, 'ch', CHIP_PAIR)  6.85 us
    all_to_all x1, waiting for transfers between devices, per_device(): x = lax.all_to_all(turned, 'ctx', 0, 0, tiled=True)  5.75 us
    pallas_call x2, Pallas kernels, project(): pl.pallas_call(kernel, out_shape=tuple((jax.ShapeDtypeStruct((rows, cols)...  5.54 us
    pallas_call x1, Pallas kernels, filter_spectrum(): pl.pallas_call(filter_kernel, out_shape=jax.ShapeDtypeStruct((GROUP * BLO...  4.27 us
    ppermute x1, starting transfers between devices, per_device(): away_in = lax.ppermute(away_pair, 'ch', CORE_PAIR)  3.55 us
    ppermute x1, starting transfers between devices, per_device(): far = lax.ppermute(away_sum, 'ch', CHIP_PAIR)  2.71 us
  transfers between devices with their start and end apart: 5, of which 4 were waited for; matrix products, arithmetic and copies ran while one was open for 0% of the time, Pallas kernels for 16%

profile of v8, /device:TPU:1, one launch (start us, length us, event | category | flops | bytes accessed | tf_op | source)
XLA Modules:
  0.0 59.7 jit_solution(11019898736549574144)
XLA Ops:
  0.0 2.1 %turn.1 = bf16[1024,256]{1,0:T(8,128)(2,1)} custom-call(bf16[256,1024]{1,0:T(8,128)(2,1)} %v_hbm.1), custom_call_target="tpu_custom_call" | custom-call | tf_op jit(solution)/shard_map/turn/pallas_call | solution.py:241
  2.1 9.7 %all-to-all-start = ((bf16[32,32,256]{2,1,0:T(8,128)(2,1)}), bf16[32,32,256]{2,1,0:T(8,128)(2,1)S(1)}, u32[]{:S(2)}, u32[]{:S(2)}) async-start(bf16[32,32,256]{2,1,0:T(8,128)(2,1)} %bitcast.3), calls=%async_computation | async-start | bytes 1048576 | tf_op jit(solution)/shard_map/all_to_all | solution.py:365
  11.8 0.0 copy-start
  11.9 0.0 copy-start.1
  11.9 0.0 copy-start.2
  11.9 0.0 copy-start.4
  11.9 0.0 copy-start.5
  11.9 0.0 copy-start.6
  11.9 0.0 copy-start.7
  11.9 4.3 %filter_spectrum.1.spec_ref = bf16[2048,256]{1,0:T(8,128)(2,1)S(1)} custom-call(s32[1]{0:T(128)} %bitcast.4.which, bf16[8192,1024]{1,0:T(8,128)(2,1)} %h_hbm.1, bf16[128,64]{1,0:T(8,128)(2,1)} %constant.39.a_hbm, f32[64,256]{1,0:T(8,128)} %constant.34.clone.twist_hbm.twist_ref, bf16[256,256]{1,0:T(8,128)(2,1)} %constant.40.forth_hbm.forth_ref, ...), custom_call_target="tpu_custom_call" | custom-call | tf_op jit(solution)/shard_map/filter_spectrum/pallas_call | solution.py:186
  16.2 0.0 copy-start.3
  16.2 5.7 %all-to-all-done.x_ref = bf16[32,32,256]{2,1,0:T(8,128)(2,1)S(1)} async-done(((bf16[32,32,256]{2,1,0:T(8,128)(2,1)}), bf16[32,32,256]{2,1,0:T(8,128)(2,1)S(1)}, u32[]{:S(2)}, u32[]{:S(2)}) %all-to-all-start) | async-done | bytes 524320 | tf_op jit(solution)/shard_map/all_to_all | solution.py:365
  22.0 0.0 copy-done
  22.0 0.0 copy-done.1
  22.0 0.0 copy-done.2
  22.0 0.0 copy-done.4
  22.0 0.0 copy-done.5
  22.0 0.0 copy-done.6
  22.0 0.0 copy-done.7
  22.0 2.1 %convolve.1 = (bf16[32,32,256]{2,1,0:T(8,128)(2,1)S(1)}, bf16[1024,1024]{1,0:T(8,128)(2,1)S(1)}) custom-call(s32[1]{0:T(128)} %bitcast.2.chunks, bf16[32,32,256]{2,1,0:T(8,128)(2,1)S(1)} %all-to-all-done.x_ref, bf16[2048,256]{1,0:T(8,128)(2,1)S(1)} %filter_spectrum.1.spec_ref, bf16[128,64]{1,0:T(8,128)(2,1)S(1)} %copy-done.6, bf16[64,128]{1,0:T(8,128)(2,1)S(1)} %copy-done.7, ...), custom_call_target="tpu_custom_call" | custom-call | tf_op jit(solution)/shard_map/convolve/pallas_call | solution.py:210
  24.2 13.1 %all_to_all.10 = bf16[32,32,256]{2,1,0:T(8,128)(2,1)S(1)} all-to-all(bf16[32,32,256]{2,1,0:T(8,128)(2,1)S(1)} %get-tuple-element.14), channel_id=1, replica_groups=mesh['ctx'=32,'ch'=4] {'ctx'}, dimensions={0} | all-to-all | bytes 1048576 | tf_op jit(solution)/shard_map/all_to_all | solution.py:368
  37.2 0.0 copy-done.3
  37.2 0.7 %gate_project.1 = (bf16[256,1024]{1,0:T(8,128)(2,1)S(1)}, bf16[256,1024]{1,0:T(8,128)(2,1)S(1)}) custom-call(bf16[1024,256]{1,0:T(8,128)(2,1)S(1)} %bitcast.7, bf16[256,1024]{1,0:T(8,128)(2,1)S(1)} %copy-done.3, bf16[1024,1024]{1,0:T(8,128)(2,1)S(1)} %get-tuple-element.15.w_ref), custom_call_target="tpu_custom_call" | custom-call | tf_op jit(solution)/shard_map/gate_project/pallas_call | solution.py:286
  38.0 3.5 %collective-permute-start = (bf16[256,1024]{1,0:T(8,128)(2,1)S(1)}, bf16[256,1024]{1,0:T(8,128)(2,1)S(1)}, u32[]{:S(2)}, u32[]{:S(2)}) collective-permute-start(bf16[256,1024]{1,0:T(8,128)(2,1)S(1)} %get-tuple-element.17), channel_id=1, source_target_pairs={{0,1},{1,0},{2,3},{3,2},{4,5},{5,4},{6,7},{7,6},{8,9},{9,8},{10,11... | collective-permute-start | bytes 1572872 | tf_op jit(solution)/shard_map/ppermute | solution.py:370
  41.5 2.1 %project.2 = f32[256,1024]{1,0:T(8,128)S(1)} custom-call(s32[1]{0:T(128)} %bitcast.6.chunks, bf16[256,1024]{1,0:T(8,128)(2,1)S(1)} %get-tuple-element.18.mix_ref, bf16[1024,4096]{1,0:T(8,128)(2,1)} %w_hbm.5), custom_call_target="tpu_custom_call" | custom-call | tf_op jit(solution)/shard_map/project/pallas_call | solution.py:311
  43.6 0.0 collective-permute-done
  43.6 0.2 add_convert_fusion
  43.7 2.7 %collective-permute-start.3 = (bf16[256,1024]{1,0:T(8,128)(2,1)S(1)}, bf16[256,1024]{1,0:T(8,128)(2,1)S(1)}, u32[]{:S(2)}, u32[]{:S(2)}) collective-permute-start(bf16[256,1024]{1,0:T(8,128)(2,1)S(1)} %add_convert_fusion), channel_id=1, source_target_pairs={{0,2},{2,0},{1,3},{3,1},{4,6},{6,4},{5,7},{7,5},{8,10},{10,8},{9,1... | collective-permute-start | bytes 1572872 | tf_op jit(solution)/shard_map/ppermute | solution.py:374
  46.5 0.1 pad_add_fusion.chunks
  46.5 3.5 %project.3 = (bf16[128,1024]{1,0:T(8,128)(2,1)S(1)}, bf16[128,1024]{1,0:T(8,128)(2,1)S(1)}, f32[256,1024]{1,0:T(8,128)S(1)}) custom-call(s32[2]{0:T(128)S(1)} %pad_add_fusion.chunks, bf16[256,1024]{1,0:T(8,128)(2,1)S(1)} %get-tuple-element.18.mix_ref, bf16[1024,4096]{1,0:T(8,128)(2,1)} %w_hbm.5), custom_call_target="tpu_custom_call" | custom-call | tf_op jit(solution)/shard_map/project/pallas_call | solution.py:311
  50.0 0.4 collective-permute-start.1
  50.4 0.2 collective-permute-start.2
  50.6 1.0 %collective-permute-done.1.refs_0_ = bf16[128,1024]{1,0:T(8,128)(2,1)S(1)} collective-permute-done((bf16[128,1024]{1,0:T(8,128)(2,1)S(1)}, bf16[128,1024]{1,0:T(8,128)(2,1)S(1)}, u32[]{:S(2)}, u32[]{:S(2)}) %collective-permute-start.1) | collective-permute-done | bytes 262176 | tf_op jit(solution)/shard_map/ppermute | solution.py:376
  51.6 0.4 collective-permute-done.2.refs_1_
  52.0 6.9 %collective-permute-done.3.refs_2_ = bf16[256,1024]{1,0:T(8,128)(2,1)S(1)} collective-permute-done((bf16[256,1024]{1,0:T(8,128)(2,1)S(1)}, bf16[256,1024]{1,0:T(8,128)(2,1)S(1)}, u32[]{:S(2)}, u32[]{:S(2)}) %collective-permute-start.3) | collective-permute-done | bytes 524320 | tf_op jit(solution)/shard_map/ppermute | solution.py:374
  58.9 0.9 %finish.1 = bf16[256,1024]{1,0:T(8,128)(2,1)} custom-call(f32[256,1024]{1,0:T(8,128)S(1)} %get-tuple-element.19.home_ref, bf16[128,1024]{1,0:T(8,128)(2,1)S(1)} %collective-permute-done.1.refs_0_, bf16[128,1024]{1,0:T(8,128)(2,1)S(1)} %collective-permute-done.2.refs_1_, bf16[256,1024]{1,0:T(8,128)(2,1)S(1)} %collective-permute-done.3.refs_2_), custom_call_target="tpu_custom_call" | custom-call | tf_op jit(solution)/shard_map/finish/pallas_call | solution.py:344
Async XLA Ops:
  2.1 19.9 %all-to-all-start = ((bf16[32,32,256]{2,1,0:T(8,128)(2,1)}), bf16[32,32,256]{2,1,0:T(8,128)(2,1)S(1)}, u32[]{:S(2)}, u32[]{:S(2)}) async-start(bf16[32,32,256]{2,1,0:T(8,128)(2,1)} %bitcast.3), calls=%async_computation | async-start | bytes 1048576 | tf_op jit(solution)/shard_map/all_to_all | solution.py:365
  11.8 10.1 %copy-start = (bf16[512,512]{1,0:T(8,128)(2,1)S(1)}, bf16[512,512]{1,0:T(8,128)(2,1)}, u32[]{:S(2)}) copy-start(bf16[512,512]{1,0:T(8,128)(2,1)} %constant.41.swap_hbm.swap_ref) | copy-start | bytes 1572868
  11.9 10.1 %copy-start.1 = (bf16[256,256]{1,0:T(8,128)(2,1)S(1)}, bf16[256,256]{1,0:T(8,128)(2,1)}, u32[]{:S(2)}) copy-start(bf16[256,256]{1,0:T(8,128)(2,1)} %constant.40.forth_hbm.forth_ref) | copy-start | bytes 393220
  11.9 10.1 %copy-start.2 = (bf16[512,512]{1,0:T(8,128)(2,1)S(1)}, bf16[512,512]{1,0:T(8,128)(2,1)}, u32[]{:S(2)}) copy-start(bf16[512,512]{1,0:T(8,128)(2,1)} %constant.45.unswap_ref) | copy-start | bytes 1572868
  11.9 10.1 %copy-start.4 = (f32[64,256]{1,0:T(8,128)S(1)}, f32[64,256]{1,0:T(8,128)}, u32[]{:S(2)}) copy-start(f32[64,256]{1,0:T(8,128)} %constant.34.clone.twist_hbm.twist_ref) | copy-start | bytes 196612
  11.9 10.1 %copy-start.5 = (bf16[256,256]{1,0:T(8,128)(2,1)S(1)}, bf16[256,256]{1,0:T(8,128)(2,1)}, u32[]{:S(2)}) copy-start(bf16[256,256]{1,0:T(8,128)(2,1)} %constant.44.back_ref) | copy-start | bytes 393220
  11.9 10.1 %copy-start.6 = (bf16[128,64]{1,0:T(8,128)(2,1)S(1)}, bf16[128,64]{1,0:T(8,128)(2,1)}, u32[]{:S(2)}) copy-start(bf16[128,64]{1,0:T(8,128)(2,1)} %constant.42.a_ref) | copy-start | bytes 49156
  11.9 10.1 %copy-start.7 = (bf16[64,128]{1,0:T(8,128)(2,1)S(1)}, bf16[64,128]{1,0:T(8,128)(2,1)}, u32[]{:S(2)}) copy-start(bf16[64,128]{1,0:T(8,128)(2,1)} %constant.43.a_back_ref) | copy-start | bytes 49156
  16.2 21.0 %copy-start.3 = (bf16[256,1024]{1,0:T(8,128)(2,1)S(1)}, bf16[256,1024]{1,0:T(8,128)(2,1)}, u32[]{:S(2)}) copy-start(bf16[256,1024]{1,0:T(8,128)(2,1)} %gate_ref.1) | copy-start | bytes 1572868
  38.0 5.6 %collective-permute-start = (bf16[256,1024]{1,0:T(8,128)(2,1)S(1)}, bf16[256,1024]{1,0:T(8,128)(2,1)S(1)}, u32[]{:S(2)}, u32[]{:S(2)}) collective-permute-start(bf16[256,1024]{1,0:T(8,128)(2,1)S(1)} %get-tuple-element.17), channel_id=1, source_target_pairs={{0,1},{1,0},{2,3},{3,2},{4,5},{5,4},{6,7},{7,6},{8,9},{9,8},{10,11... | collective-permute-start | bytes 1572872 | tf_op jit(solution)/shard_map/ppermute | solution.py:370
  43.7 15.1 %collective-permute-start.3 = (bf16[256,1024]{1,0:T(8,128)(2,1)S(1)}, bf16[256,1024]{1,0:T(8,128)(2,1)S(1)}, u32[]{:S(2)}, u32[]{:S(2)}) collective-permute-start(bf16[256,1024]{1,0:T(8,128)(2,1)S(1)} %add_convert_fusion), channel_id=1, source_target_pairs={{0,2},{2,0},{1,3},{3,1},{4,6},{6,4},{5,7},{7,5},{8,10},{10,8},{9,1... | collective-permute-start | bytes 1572872 | tf_op jit(solution)/shard_map/ppermute | solution.py:374
  50.0 1.6 %collective-permute-start.1 = (bf16[128,1024]{1,0:T(8,128)(2,1)S(1)}, bf16[128,1024]{1,0:T(8,128)(2,1)S(1)}, u32[]{:S(2)}, u32[]{:S(2)}) collective-permute-start(bf16[128,1024]{1,0:T(8,128)(2,1)S(1)} %get-tuple-element.20), channel_id=1, source_target_pairs={{0,1},{1,0},{2,3},{3,2},{4,5},{5,4},{6,7},{7,6},{8,9},{9,8},{10,11... | collective-permute-start | bytes 786440 | tf_op jit(solution)/shard_map/ppermute | solution.py:376
  50.4 1.6 %collective-permute-start.2 = (bf16[128,1024]{1,0:T(8,128)(2,1)S(1)}, bf16[128,1024]{1,0:T(8,128)(2,1)S(1)}, u32[]{:S(2)}, u32[]{:S(2)}) collective-permute-start(bf16[128,1024]{1,0:T(8,128)(2,1)S(1)} %get-tuple-element.21), channel_id=1, source_target_pairs={{0,1},{1,0},{2,3},{3,2},{4,5},{5,4},{6,7},{7,6},{8,9},{9,8},{10,11... | collective-permute-start | bytes 786440 | tf_op jit(solution)/shard_map/ppermute | solution.py:376

commit v9 on v8

--- a/solution.py
+++ b/solution.py
@@ -2,6 +2,7 @@
 
 import jax
 import jax.numpy as jnp
+import ml_dtypes
 import numpy as np
 from jax import lax
 from jax.experimental import pallas as pl
@@ -36,32 +37,44 @@
     cos, sin = np.cos(angle), np.sin(angle)
     forth = np.block([[cos, -sin], [sin, cos]])
     back = np.block([[cos, sin], [-sin, cos]])
-    rows = np.arange(HALF * SUB)
-    swap = np.zeros((HALF * SUB, HALF * SUB))
-    swap[(rows % SUB) * HALF + rows // SUB, rows] = 1.0
-    bf = lambda a: jnp.asarray(a.astype(np.float32)).astype(BF16)
-    return dict(
-        a_filter=bf(stage_a(natural)),
+    rows = np.arange(SUB * SUB)
+    swap = np.zeros((SUB * SUB, SUB * SUB))
+    swap[(rows % SUB) * SUB + rows // SUB, rows] = 1.0
+    bf = lambda a: a.astype(np.float32).astype(ml_dtypes.bfloat16)
+
+    def two(a):
+        high = bf(a)
+        return high, bf(a - high.astype(np.float64))
+
+    made = dict(
+        a_filter=np.concatenate(two(stage_a(natural)), 1),
         a_value=bf(stage_a(stored)),
         a_back=bf(stage_a_back(stored)),
-        twist=jnp.asarray(np.concatenate([np.cos(twist), -np.sin(twist)], 1).astype(np.float32)),
+        twist=np.concatenate([np.cos(twist), -np.sin(twist)], 1).astype(np.float32),
         forth=bf(forth),
+        forth_rest=two(forth)[1],
         back=bf(back),
         swap=bf(swap),
-        unswap=bf(swap.T),
     )
+    return {name: jnp.asarray(table) for name, table in made.items()}
 
 
 def dot(left, right):
     return jnp.dot(left, right, preferred_element_type=F32)
+
+
+def lane_of(half, high, g):
+    return ((half * 2 + high) * 2 + g) * SPAN
 
 
 def stage_a_rows(swapped, a_table, twist, mid_ref):
     t_re = jnp.concatenate([twist[:, :SPAN]] * 2, 1)
     t_im = jnp.concatenate([twist[:, SPAN:]] * 2, 1)
     for c in range(SUB):
-        block = swapped[c * HALF : (c + 1) * HALF, :]
-        rows = jnp.concatenate([block[:, : 2 * SPAN], block[:, 2 * SPAN :]], 0)
+        block = swapped[c * SUB : (c + 1) * SUB, :]
+        rows = jnp.concatenate([block[:, k * 2 * SPAN : (k + 1) * 2 * SPAN] for k in range(4)], 0)
+        if a_table.shape[1] > BLOCKS:
+            rows = jnp.concatenate([rows, rows], 0)
         spec = dot(a_table, rows)
         re, im = spec[:BLOCKS], spec[BLOCKS:]
         out_re = (re * t_re - im * t_im).astype(BF16)
@@ -79,8 +92,8 @@
 
 
 def filter_kernel(
-    which, h_hbm, a_hbm, twist_hbm, forth_hbm, swap_hbm, out_ref,
-    slab_ref, a_ref, twist_ref, forth_ref, swap_ref, gather_ref, mid_ref, slab_sem, table_sem,
+    which, h_hbm, a_hbm, twist_hbm, forth_hbm, rest_hbm, swap_hbm, out_ref,
+    slab_ref, a_ref, twist_ref, forth_ref, rest_ref, swap_ref, gather_ref, mid_ref, slab_sem, table_sem,
 ):
     lane_block = pl.multiple_of((which[0] // 4) * SPAN, SPAN)
     piece = LENGTH // SLABS
@@ -92,7 +105,7 @@
         )
         for k in range(SLABS)
     ]
-    pairs = [(a_hbm, a_ref), (twist_hbm, twist_ref), (forth_hbm, forth_ref), (swap_hbm, swap_ref)]
+    pairs = [(a_hbm, a_ref), (twist_hbm, twist_ref), (forth_hbm, forth_ref), (rest_hbm, rest_ref), (swap_hbm, swap_ref)]
     loads = [pltpu.make_async_copy(s, d, table_sem.at[k]) for k, (s, d) in enumerate(pairs)]
     for copy in slabs + loads:
         copy.start()
@@ -103,12 +116,12 @@
     for block in range(BLOCKS):
         if block % (BLOCKS // SLABS) == 0:
             slabs[block // (BLOCKS // SLABS)].wait()
-        half, a = divmod(block, HALF)
+        half, high, a = block // HALF, block // SUB % 2, block % SUB
         turned = lax.dot_general(
             pick, slab_ref[block * SPAN : (block + 1) * SPAN, :], (((1,), (1,)), ((), ())), preferred_element_type=F32
         ).astype(BF16)
         for g in range(2):
-            lane = (half * 2 + g) * SPAN
+            lane = lane_of(half, high, g)
             gather_ref[a * SUB : (a + 1) * SUB, lane : lane + SPAN] = turned[g * SUB : (g + 1) * SUB]
     for copy in loads:
         copy.wait()
@@ -116,11 +129,12 @@
     stage_a_rows(swapped, a_ref[...], twist_ref[...], mid_ref)
     for k in range(GROUP * BLOCKS // CHUNK):
         part = slice(k * CHUNK, (k + 1) * CHUNK)
-        out_ref[part, :] = dot(mid_ref[part, :], forth_ref[...]).astype(out_ref.dtype)
+        mid = mid_ref[part, :]
+        out_ref[part, :] = (dot(mid, forth_ref[...]) + dot(mid, rest_ref[...])).astype(out_ref.dtype)
 
 
 def conv_kernel(
-    chunks, x_ref, spec_ref, a_ref, a_back_ref, twist_ref, forth_ref, back_ref, swap_ref, unswap_ref, w_hbm,
+    chunks, x_ref, spec_ref, a_ref, a_back_ref, twist_ref, forth_ref, back_ref, swap_ref, w_hbm,
     out_ref, w_ref, mid_ref, turn_ref, sem,
 ):
     rows, cols = w_ref.shape[0] // PARTS, w_ref.shape[1]
@@ -138,9 +152,12 @@
     copies = [weight_copy(k) for k in range(PARTS)]
     pieces = []
     for half in range(2):
-        for g in range(2):
-            piece = x_ref[:, g * SUB : (g + 1) * SUB, half * SPAN : (half + 1) * SPAN]
-            pieces.append(piece.reshape(HALF * SUB, SPAN))
+        for high in range(2):
+            for g in range(2):
+                piece = x_ref[
+                    high * SUB : (high + 1) * SUB, g * SUB : (g + 1) * SUB, half * SPAN : (half + 1) * SPAN
+                ]
+                pieces.append(piece.reshape(SUB * SUB, SPAN))
     swapped = dot(swap_ref[...], jnp.concatenate(pieces, 1)).astype(BF16)
     twist = twist_ref[...]
     stage_a_rows(swapped, a_ref[...], twist, mid_ref)
@@ -165,15 +182,16 @@
                 jnp.concatenate([mid_ref[at : at + BLOCKS, :SPAN], mid_ref[at : at + BLOCKS, SPAN:]], 0)
             )
         y = dot(a_back_ref[...], jnp.concatenate(sides, 1)).astype(BF16)
-        turn_ref[c * HALF : (c + 1) * HALF, : 2 * SPAN] = y[:HALF]
-        turn_ref[c * HALF : (c + 1) * HALF, 2 * SPAN :] = y[HALF:]
-    result = dot(unswap_ref[...], turn_ref[...]).astype(BF16)
+        for k in range(4):
+            turn_ref[c * SUB : (c + 1) * SUB, k * 2 * SPAN : (k + 1) * 2 * SPAN] = y[k * SUB : (k + 1) * SUB]
+    result = dot(swap_ref[...], turn_ref[...]).astype(BF16)
     for half in range(2):
-        for g in range(2):
-            lane = (half * 2 + g) * SPAN
-            out_ref[:, g * SUB : (g + 1) * SUB, half * SPAN : (half + 1) * SPAN] = result[:, lane : lane + SPAN].reshape(
-                HALF, SUB, SPAN
-            )
+        for high in range(2):
+            for g in range(2):
+                lane = lane_of(half, high, g)
+                out_ref[
+                    high * SUB : (high + 1) * SUB, g * SUB : (g + 1) * SUB, half * SPAN : (half + 1) * SPAN
+                ] = result[:, lane : lane + SPAN].reshape(SUB, SUB, SPAN)
     for copy in copies:
         copy.wait()
 
@@ -186,22 +204,23 @@
     return pl.pallas_call(
         filter_kernel,
         out_shape=jax.ShapeDtypeStruct((GROUP * BLOCKS, 2 * SPAN), BF16),
-        in_specs=[pl.BlockSpec(memory_space=pltpu.SMEM)] + [pl.BlockSpec(memory_space=pltpu.HBM)] * 5,
+        in_specs=[pl.BlockSpec(memory_space=pltpu.SMEM)] + [pl.BlockSpec(memory_space=pltpu.HBM)] * 6,
         out_specs=pl.BlockSpec(memory_space=pltpu.VMEM),
         scratch_shapes=[
             pltpu.VMEM((LENGTH, SPAN), BF16),
-            pltpu.VMEM((2 * BLOCKS, BLOCKS), BF16),
+            pltpu.VMEM((2 * BLOCKS, 2 * BLOCKS), BF16),
             pltpu.VMEM((BLOCKS, 2 * SPAN), F32),
             pltpu.VMEM((2 * SPAN, 2 * SPAN), BF16),
-            pltpu.VMEM((HALF * SUB, HALF * SUB), BF16),
-            pltpu.VMEM((HALF * SUB, 4 * SPAN), BF16),
+            pltpu.VMEM((2 * SPAN, 2 * SPAN), BF16),
+            pltpu.VMEM((SUB * SUB, SUB * SUB), BF16),
+            pltpu.VMEM((SUB * SUB, 8 * SPAN), BF16),
             pltpu.VMEM((GROUP * BLOCKS, 2 * SPAN), BF16),
             pltpu.SemaphoreType.DMA((SLABS,)),
-            pltpu.SemaphoreType.DMA((4,)),
+            pltpu.SemaphoreType.DMA((5,)),
         ],
         compiler_params=pltpu.CompilerParams(vmem_limit_bytes=32 << 20),
         name="filter_spectrum",
-    )(which, *in_hbm(long_filter, t["a_filter"], t["twist"], t["forth"], t["swap"]))
+    )(which, *in_hbm(long_filter, t["a_filter"], t["twist"], t["forth"], t["forth_rest"], t["swap"]))
 
 
 def convolve(chunks, x, spec, w, t):
@@ -210,17 +229,17 @@
     return pl.pallas_call(
         conv_kernel,
         out_shape=(pltpu.VMEM((HALF, GROUP, 2 * SPAN), BF16), pltpu.VMEM((inner, cols), BF16)),
-        in_specs=[pl.BlockSpec(memory_space=pltpu.SMEM)] + [vmem] * 9 + [pl.BlockSpec(memory_space=pltpu.HBM)],
+        in_specs=[pl.BlockSpec(memory_space=pltpu.SMEM)] + [vmem] * 8 + [pl.BlockSpec(memory_space=pltpu.HBM)],
         out_specs=(vmem, vmem),
         scratch_shapes=[
             pltpu.VMEM((GROUP * BLOCKS, 2 * SPAN), BF16),
-            pltpu.VMEM((HALF * SUB, 4 * SPAN), BF16),
+            pltpu.VMEM((SUB * SUB, 8 * SPAN), BF16),
             pltpu.SemaphoreType.DMA((PARTS,)),
         ],
         compiler_params=pltpu.CompilerParams(vmem_limit_bytes=32 << 20),
         name="convolve",
     )(
-        chunks, x, spec, t["a_value"], t["a_back"], t["twist"], t["forth"], t["back"], t["swap"], t["unswap"], *in_hbm(w)
+        chunks, x, spec, t["a_value"], t["a_back"], t["twist"], t["forth"], t["back"], t["swap"], *in_hbm(w)
     )
 
 

time: 60 us -> 59.9 us (level)
  transfers between devices with their start and end apart: 5 -> 5, of which waited for: 4 -> 4; matrix products, arithmetic and copies ran while one was open for 0% -> 0% of each run, Pallas kernels for 16% -> 17%
where the time goes in v9:
time: 59.9 us; the launch traced here: 59.6 us
  starting transfers between devices  16.6 us (28%)
  Pallas kernels  15.8 us (26%)
  waiting for transfers between devices  13.8 us (23%)
  blocking collectives  13.1 us (22%)
    all_to_all x1, blocking collectives, per_device(): y = lax.all_to_all(y, 'ctx', 0, 0, tiled=True).reshape(width, tokens)  13.1 us
    all_to_all x1, starting transfers between devices, per_device(): x = lax.all_to_all(turned, 'ctx', 0, 0, tiled=True)  9.74 us
    ppermute x1, waiting for transfers between devices, per_device(): far = lax.ppermute(away_sum, 'ch', CHIP_PAIR)  6.86 us
    pallas_call x2, Pallas kernels, project(): pl.pallas_call(kernel, out_shape=tuple((jax.ShapeDtypeStruct((rows, cols)...  5.54 us
    all_to_all x1, waiting for transfers between devices, per_device(): x = lax.all_to_all(turned, 'ctx', 0, 0, tiled=True)  5.5 us
    pallas_call x1, Pallas kernels, filter_spectrum(): pl.pallas_call(filter_kernel, out_shape=jax.ShapeDtypeStruct((GROUP * BLO...  4.53 us
    ppermute x1, starting transfers between devices, per_device(): away_in = lax.ppermute(away_pair, 'ch', CORE_PAIR)  3.55 us
    ppermute x1, starting transfers between devices, per_device(): far = lax.ppermute(away_sum, 'ch', CHIP_PAIR)  2.7 us
  transfers between devices with their start and end apart: 5, of which 4 were waited for; matrix products, arithmetic and copies ran while one was open for 0% of the time, Pallas kernels for 17%

profile of v9, /device:TPU:1, one launch (start us, length us, event | category | flops | bytes accessed | tf_op | source)
XLA Modules:
  0.0 59.6 jit_solution(11009796893003726858)
XLA Ops:
  0.0 2.1 %turn.1 = bf16[1024,256]{1,0:T(8,128)(2,1)} custom-call(bf16[256,1024]{1,0:T(8,128)(2,1)} %v_hbm.1), custom_call_target="tpu_custom_call" | custom-call | tf_op jit(solution)/shard_map/turn/pallas_call | solution.py:260
  2.1 9.7 %all-to-all-start = ((bf16[32,32,256]{2,1,0:T(8,128)(2,1)}), bf16[32,32,256]{2,1,0:T(8,128)(2,1)S(1)}, u32[]{:S(2)}, u32[]{:S(2)}) async-start(bf16[32,32,256]{2,1,0:T(8,128)(2,1)} %bitcast.3), calls=%async_computation | async-start | bytes 1048576 | tf_op jit(solution)/shard_map/all_to_all | solution.py:384
  11.8 0.0 copy-start
  11.9 0.0 copy-start.1
  11.9 0.0 copy-start.3
  11.9 0.0 copy-start.4
  11.9 0.0 copy-start.5
  11.9 0.0 copy-start.6
  11.9 4.5 %filter_spectrum.1.spec_ref = bf16[2048,256]{1,0:T(8,128)(2,1)S(1)} custom-call(s32[1]{0:T(128)} %bitcast.4.which, bf16[8192,1024]{1,0:T(8,128)(2,1)} %h_hbm.1, bf16[128,128]{1,0:T(8,128)(2,1)} %constant.31.clone.a_hbm, f32[64,256]{1,0:T(8,128)} %constant.34.clone.twist_hbm.twist_ref, bf16[256,256]{1,0:T(8,128)(2,1)} %constant.35.clone.forth_hbm.forth_ref, ...), custom_call_target="tpu_custom_call" | custom-call | tf_op jit(solution)/shard_map/filter_spectrum/pallas_call | solution.py:204
  16.5 0.0 copy-start.2
  16.5 5.5 %all-to-all-done.x_ref = bf16[32,32,256]{2,1,0:T(8,128)(2,1)S(1)} async-done(((bf16[32,32,256]{2,1,0:T(8,128)(2,1)}), bf16[32,32,256]{2,1,0:T(8,128)(2,1)S(1)}, u32[]{:S(2)}, u32[]{:S(2)}) %all-to-all-start) | async-done | bytes 524320 | tf_op jit(solution)/shard_map/all_to_all | solution.py:384
  22.0 0.0 copy-done
  22.0 0.0 copy-done.1
  22.0 0.0 copy-done.3
  22.0 0.0 copy-done.4
  22.0 0.0 copy-done.5
  22.0 0.0 copy-done.6
  22.0 2.0 %convolve.1 = (bf16[32,32,256]{2,1,0:T(8,128)(2,1)S(1)}, bf16[1024,1024]{1,0:T(8,128)(2,1)S(1)}) custom-call(s32[1]{0:T(128)} %bitcast.2.chunks, bf16[32,32,256]{2,1,0:T(8,128)(2,1)S(1)} %all-to-all-done.x_ref, bf16[2048,256]{1,0:T(8,128)(2,1)S(1)} %filter_spectrum.1.spec_ref, bf16[128,64]{1,0:T(8,128)(2,1)S(1)} %copy-done.5, bf16[64,128]{1,0:T(8,128)(2,1)S(1)} %copy-done.6, ...), custom_call_target="tpu_custom_call" | custom-call | tf_op jit(solution)/shard_map/convolve/pallas_call | solution.py:229
  24.0 13.1 %all_to_all.10 = bf16[32,32,256]{2,1,0:T(8,128)(2,1)S(1)} all-to-all(bf16[32,32,256]{2,1,0:T(8,128)(2,1)S(1)} %get-tuple-element.14), channel_id=1, replica_groups=mesh['ctx'=32,'ch'=4] {'ctx'}, dimensions={0} | all-to-all | bytes 1048576 | tf_op jit(solution)/shard_map/all_to_all | solution.py:387
  37.1 0.0 copy-done.2
  37.1 0.7 %gate_project.1 = (bf16[256,1024]{1,0:T(8,128)(2,1)S(1)}, bf16[256,1024]{1,0:T(8,128)(2,1)S(1)}) custom-call(bf16[1024,256]{1,0:T(8,128)(2,1)S(1)} %bitcast.7, bf16[256,1024]{1,0:T(8,128)(2,1)S(1)} %copy-done.2, bf16[1024,1024]{1,0:T(8,128)(2,1)S(1)} %get-tuple-element.15.w_ref), custom_call_target="tpu_custom_call" | custom-call | tf_op jit(solution)/shard_map/gate_project/pallas_call | solution.py:305
  37.8 3.5 %collective-permute-start = (bf16[256,1024]{1,0:T(8,128)(2,1)S(1)}, bf16[256,1024]{1,0:T(8,128)(2,1)S(1)}, u32[]{:S(2)}, u32[]{:S(2)}) collective-permute-start(bf16[256,1024]{1,0:T(8,128)(2,1)S(1)} %get-tuple-element.17), channel_id=1, source_target_pairs={{0,1},{1,0},{2,3},{3,2},{4,5},{5,4},{6,7},{7,6},{8,9},{9,8},{10,11... | collective-permute-start | bytes 1572872 | tf_op jit(solution)/shard_map/ppermute | solution.py:389
  41.4 2.0 %project.2 = f32[256,1024]{1,0:T(8,128)S(1)} custom-call(s32[1]{0:T(128)} %bitcast.6.chunks, bf16[256,1024]{1,0:T(8,128)(2,1)S(1)} %get-tuple-element.18.mix_ref, bf16[1024,4096]{1,0:T(8,128)(2,1)} %w_hbm.5), custom_call_target="tpu_custom_call" | custom-call | tf_op jit(solution)/shard_map/project/pallas_call | solution.py:330
  43.4 0.0 collective-permute-done
  43.4 0.2 add_convert_fusion
  43.6 2.7 %collective-permute-start.3 = (bf16[256,1024]{1,0:T(8,128)(2,1)S(1)}, bf16[256,1024]{1,0:T(8,128)(2,1)S(1)}, u32[]{:S(2)}, u32[]{:S(2)}) collective-permute-start(bf16[256,1024]{1,0:T(8,128)(2,1)S(1)} %add_convert_fusion), channel_id=1, source_target_pairs={{0,2},{2,0},{1,3},{3,1},{4,6},{6,4},{5,7},{7,5},{8,10},{10,8},{9,1... | collective-permute-start | bytes 1572872 | tf_op jit(solution)/shard_map/ppermute | solution.py:393
  46.3 0.1 pad_add_fusion.chunks
  46.4 3.5 %project.3 = (bf16[128,1024]{1,0:T(8,128)(2,1)S(1)}, bf16[128,1024]{1,0:T(8,128)(2,1)S(1)}, f32[256,1024]{1,0:T(8,128)S(1)}) custom-call(s32[2]{0:T(128)S(1)} %pad_add_fusion.chunks, bf16[256,1024]{1,0:T(8,128)(2,1)S(1)} %get-tuple-element.18.mix_ref, bf16[1024,4096]{1,0:T(8,128)(2,1)} %w_hbm.5), custom_call_target="tpu_custom_call" | custom-call | tf_op jit(solution)/shard_map/project/pallas_call | solution.py:330
  49.9 0.4 collective-permute-start.1
  50.3 0.2 collective-permute-start.2
  50.5 1.0 %collective-permute-done.1.refs_0_ = bf16[128,1024]{1,0:T(8,128)(2,1)S(1)} collective-permute-done((bf16[128,1024]{1,0:T(8,128)(2,1)S(1)}, bf16[128,1024]{1,0:T(8,128)(2,1)S(1)}, u32[]{:S(2)}, u32[]{:S(2)}) %collective-permute-start.1) | collective-permute-done | bytes 262176 | tf_op jit(solution)/shard_map/ppermute | solution.py:395
  51.5 0.4 collective-permute-done.2.refs_1_
  51.9 6.9 %collective-permute-done.3.refs_2_ = bf16[256,1024]{1,0:T(8,128)(2,1)S(1)} collective-permute-done((bf16[256,1024]{1,0:T(8,128)(2,1)S(1)}, bf16[256,1024]{1,0:T(8,128)(2,1)S(1)}, u32[]{:S(2)}, u32[]{:S(2)}) %collective-permute-start.3) | collective-permute-done | bytes 524320 | tf_op jit(solution)/shard_map/ppermute | solution.py:393
  58.7 0.9 %finish.1 = bf16[256,1024]{1,0:T(8,128)(2,1)} custom-call(f32[256,1024]{1,0:T(8,128)S(1)} %get-tuple-element.19.home_ref, bf16[128,1024]{1,0:T(8,128)(2,1)S(1)} %collective-permute-done.1.refs_0_, bf16[128,1024]{1,0:T(8,128)(2,1)S(1)} %collective-permute-done.2.refs_1_, bf16[256,1024]{1,0:T(8,128)(2,1)S(1)} %collective-permute-done.3.refs_2_), custom_call_target="tpu_custom_call" | custom-call | tf_op jit(solution)/shard_map/finish/pallas_call | solution.py:363
Async XLA Ops:
  2.1 19.9 %all-to-all-start = ((bf16[32,32,256]{2,1,0:T(8,128)(2,1)}), bf16[32,32,256]{2,1,0:T(8,128)(2,1)S(1)}, u32[]{:S(2)}, u32[]{:S(2)}) async-start(bf16[32,32,256]{2,1,0:T(8,128)(2,1)} %bitcast.3), calls=%async_computation | async-start | bytes 1048576 | tf_op jit(solution)/shard_map/all_to_all | solution.py:384
  11.8 10.1 %copy-start = (bf16[256,256]{1,0:T(8,128)(2,1)S(1)}, bf16[256,256]{1,0:T(8,128)(2,1)}, u32[]{:S(2)}) copy-start(bf16[256,256]{1,0:T(8,128)(2,1)} %constant.35.clone.forth_hbm.forth_ref) | copy-start | bytes 393220
  11.9 10.1 %copy-start.1 = (bf16[256,256]{1,0:T(8,128)(2,1)S(1)}, bf16[256,256]{1,0:T(8,128)(2,1)}, u32[]{:S(2)}) copy-start(bf16[256,256]{1,0:T(8,128)(2,1)} %constant.38.clone.swap_hbm.swap_ref) | copy-start | bytes 393220
  11.9 10.1 %copy-start.3 = (f32[64,256]{1,0:T(8,128)S(1)}, f32[64,256]{1,0:T(8,128)}, u32[]{:S(2)}) copy-start(f32[64,256]{1,0:T(8,128)} %constant.34.clone.twist_hbm.twist_ref) | copy-start | bytes 196612
  11.9 10.1 %copy-start.4 = (bf16[256,256]{1,0:T(8,128)(2,1)S(1)}, bf16[256,256]{1,0:T(8,128)(2,1)}, u32[]{:S(2)}) copy-start(bf16[256,256]{1,0:T(8,128)(2,1)} %constant.37.clone.back_ref) | copy-start | bytes 393220
  11.9 10.1 %copy-start.5 = (bf16[128,64]{1,0:T(8,128)(2,1)S(1)}, bf16[128,64]{1,0:T(8,128)(2,1)}, u32[]{:S(2)}) copy-start(bf16[128,64]{1,0:T(8,128)(2,1)} %constant.32.clone.a_ref) | copy-start | bytes 49156
  11.9 10.1 %copy-start.6 = (bf16[64,128]{1,0:T(8,128)(2,1)S(1)}, bf16[64,128]{1,0:T(8,128)(2,1)}, u32[]{:S(2)}) copy-start(bf16[64,128]{1,0:T(8,128)(2,1)} %constant.33.clone.a_back_ref) | copy-start | bytes 49156
  16.5 20.6 %copy-start.2 = (bf16[256,1024]{1,0:T(8,128)(2,1)S(1)}, bf16[256,1024]{1,0:T(8,128)(2,1)}, u32[]{:S(2)}) copy-start(bf16[256,1024]{1,0:T(8,128)(2,1)} %gate_ref.1) | copy-start | bytes 1572868
  37.8 5.6 %collective-permute-start = (bf16[256,1024]{1,0:T(8,128)(2,1)S(1)}, bf16[256,1024]{1,0:T(8,128)(2,1)S(1)}, u32[]{:S(2)}, u32[]{:S(2)}) collective-permute-start(bf16[256,1024]{1,0:T(8,128)(2,1)S(1)} %get-tuple-element.17), channel_id=1, source_target_pairs={{0,1},{1,0},{2,3},{3,2},{4,5},{5,4},{6,7},{7,6},{8,9},{9,8},{10,11... | collective-permute-start | bytes 1572872 | tf_op jit(solution)/shard_map/ppermute | solution.py:389
  43.6 15.1 %collective-permute-start.3 = (bf16[256,1024]{1,0:T(8,128)(2,1)S(1)}, bf16[256,1024]{1,0:T(8,128)(2,1)S(1)}, u32[]{:S(2)}, u32[]{:S(2)}) collective-permute-start(bf16[256,1024]{1,0:T(8,128)(2,1)S(1)} %add_convert_fusion), channel_id=1, source_target_pairs={{0,2},{2,0},{1,3},{3,1},{4,6},{6,4},{5,7},{7,5},{8,10},{10,8},{9,1... | collective-permute-start | bytes 1572872 | tf_op jit(solution)/shard_map/ppermute | solution.py:393
  49.9 1.6 %collective-permute-start.1 = (bf16[128,1024]{1,0:T(8,128)(2,1)S(1)}, bf16[128,1024]{1,0:T(8,128)(2,1)S(1)}, u32[]{:S(2)}, u32[]{:S(2)}) collective-permute-start(bf16[128,1024]{1,0:T(8,128)(2,1)S(1)} %get-tuple-element.20), channel_id=1, source_target_pairs={{0,1},{1,0},{2,3},{3,2},{4,5},{5,4},{6,7},{7,6},{8,9},{9,8},{10,11... | collective-permute-start | bytes 786440 | tf_op jit(solution)/shard_map/ppermute | solution.py:395
  50.3 1.6 %collective-permute-start.2 = (bf16[128,1024]{1,0:T(8,128)(2,1)S(1)}, bf16[128,1024]{1,0:T(8,128)(2,1)S(1)}, u32[]{:S(2)}, u32[]{:S(2)}) collective-permute-start(bf16[128,1024]{1,0:T(8,128)(2,1)S(1)} %get-tuple-element.21), channel_id=1, source_target_pairs={{0,1},{1,0},{2,3},{3,2},{4,5},{5,4},{6,7},{7,6},{8,9},{9,8},{10,11... | collective-permute-start | bytes 786440 | tf_op jit(solution)/shard_map/ppermute | solution.py:395

commit v10 on v9

--- a/solution.py
+++ b/solution.py
@@ -243,26 +243,42 @@
     )
 
 
-def turn_kernel(v_hbm, out_ref, in_ref, sem):
-    width = v_hbm.shape[1] // 4
-    copies = [
-        pltpu.make_async_copy(v_hbm.at[:, pl.ds(k * width, width)], in_ref.at[k], sem.at[k]) for k in range(4)
+TURN = 2
+
+
+def turn_kernel(v_hbm, out_hbm, in_ref, turned_ref, in_sem, out_sem):
+    width = v_hbm.shape[1] // TURN
+    loads = [
+        pltpu.make_async_copy(v_hbm.at[:, pl.ds(k * width, width)], in_ref.at[k], in_sem.at[k]) for k in range(TURN)
     ]
-    for copy in copies:
-        copy.start()
-    for k in range(4):
-        copies[k].wait()
-        out_ref[k * width : (k + 1) * width, :] = jnp.transpose(in_ref[k], (1, 0))
+    stores = [
+        pltpu.make_async_copy(turned_ref.at[k], out_hbm.at[pl.ds(k * width, width), :], out_sem.at[k])
+        for k in range(TURN)
+    ]
+    for load in loads:
+        load.start()
+    for k in range(TURN):
+        loads[k].wait()
+        turned_ref[k] = jnp.transpose(in_ref[k], (1, 0))
+        stores[k].start()
+    for store in stores:
+        store.wait()
 
 
 def turn(v):
     tokens, width = v.shape
+    hbm = pl.BlockSpec(memory_space=pltpu.HBM)
     return pl.pallas_call(
         turn_kernel,
-        out_shape=pltpu.VMEM((width, tokens), BF16),
-        in_specs=[pl.BlockSpec(memory_space=pltpu.HBM)],
-        out_specs=pl.BlockSpec(memory_space=pltpu.VMEM),
-        scratch_shapes=[pltpu.VMEM((4, tokens, width // 4), BF16), pltpu.SemaphoreType.DMA((4,))],
+        out_shape=jax.ShapeDtypeStruct((width, tokens), BF16),
+        in_specs=[hbm],
+        out_specs=hbm,
+        scratch_shapes=[
+            pltpu.VMEM((TURN, tokens, width // TURN), BF16),
+            pltpu.VMEM((TURN, width // TURN, tokens), BF16),
+            pltpu.SemaphoreType.DMA((TURN,)),
+            pltpu.SemaphoreType.DMA((TURN,)),
+        ],
         compiler_params=pltpu.CompilerParams(vmem_limit_bytes=16 << 20),
         name="turn",
     )(*in_hbm(v))

time: 59.9 us -> 59.7 us (level)
  no operation moved by 1% of the time
where the time goes in v10:
time: 59.7 us; the launch traced here: 59.4 us
  starting transfers between devices  16.6 us (28%)
  Pallas kernels  15.6 us (26%)
  waiting for transfers between devices  13.8 us (23%)
  blocking collectives  13 us (22%)
    all_to_all x1, blocking collectives, per_device(): y = lax.all_to_all(y, 'ctx', 0, 0, tiled=True).reshape(width, tokens)  13 us
    all_to_all x1, starting transfers between devices, per_device(): x = lax.all_to_all(turned, 'ctx', 0, 0, tiled=True)  9.74 us
    ppermute x1, waiting for transfers between devices, per_device(): far = lax.ppermute(away_sum, 'ch', CHIP_PAIR)  6.86 us
    pallas_call x2, Pallas kernels, project(): pl.pallas_call(kernel, out_shape=tuple((jax.ShapeDtypeStruct((rows, cols)...  5.54 us
    all_to_all x1, waiting for transfers between devices, per_device(): x = lax.all_to_all(turned, 'ctx', 0, 0, tiled=True)  5.5 us
    pallas_call x1, Pallas kernels, filter_spectrum(): pl.pallas_call(filter_kernel, out_shape=jax.ShapeDtypeStruct((GROUP * BLO...  4.53 us
    ppermute x1, starting transfers between devices, per_device(): away_in = lax.ppermute(away_pair, 'ch', CORE_PAIR)  3.55 us
    ppermute x1, starting transfers between devices, per_device(): far = lax.ppermute(away_sum, 'ch', CHIP_PAIR)  2.7 us
  transfers between devices with their start and end apart: 5, of which 4 were waited for; matrix products, arithmetic and copies ran while one was open for 0% of the time, Pallas kernels for 17%

profile of v10, /device:TPU:1, one launch (start us, length us, event | category | flops | bytes accessed | tf_op | source)
XLA Modules:
  0.0 59.4 jit_solution(10616682161731331536)
XLA Ops:
  0.0 1.9 %turn.1 = bf16[1024,256]{1,0:T(8,128)(2,1)} custom-call(bf16[256,1024]{1,0:T(8,128)(2,1)} %v_hbm.1), custom_call_target="tpu_custom_call" | custom-call | tf_op jit(solution)/shard_map/turn/pallas_call | solution.py:271
  1.9 9.7 %all-to-all-start = ((bf16[32,32,256]{2,1,0:T(8,128)(2,1)}), bf16[32,32,256]{2,1,0:T(8,128)(2,1)S(1)}, u32[]{:S(2)}, u32[]{:S(2)}) async-start(bf16[32,32,256]{2,1,0:T(8,128)(2,1)} %bitcast.3), calls=%async_computation | async-start | bytes 1048576 | tf_op jit(solution)/shard_map/all_to_all | solution.py:400
  11.7 0.0 copy-start
  11.7 0.0 copy-start.1
  11.7 0.0 copy-start.3
  11.7 0.0 copy-start.4
  11.7 0.0 copy-start.5
  11.8 0.0 copy-start.6
  11.8 4.5 %filter_spectrum.1.spec_ref = bf16[2048,256]{1,0:T(8,128)(2,1)S(1)} custom-call(s32[1]{0:T(128)} %bitcast.4.which, bf16[8192,1024]{1,0:T(8,128)(2,1)} %h_hbm.1, bf16[128,128]{1,0:T(8,128)(2,1)} %constant.31.clone.a_hbm, f32[64,256]{1,0:T(8,128)} %constant.34.clone.twist_hbm.twist_ref, bf16[256,256]{1,0:T(8,128)(2,1)} %constant.35.clone.forth_hbm.forth_ref, ...), custom_call_target="tpu_custom_call" | custom-call | tf_op jit(solution)/shard_map/filter_spectrum/pallas_call | solution.py:204
  16.3 0.0 copy-start.2
  16.3 5.5 %all-to-all-done.x_ref = bf16[32,32,256]{2,1,0:T(8,128)(2,1)S(1)} async-done(((bf16[32,32,256]{2,1,0:T(8,128)(2,1)}), bf16[32,32,256]{2,1,0:T(8,128)(2,1)S(1)}, u32[]{:S(2)}, u32[]{:S(2)}) %all-to-all-start) | async-done | bytes 524320 | tf_op jit(solution)/shard_map/all_to_all | solution.py:400
  21.8 0.0 copy-done
  21.8 0.0 copy-done.1
  21.8 0.0 copy-done.3
  21.8 0.0 copy-done.4
  21.8 0.0 copy-done.5
  21.8 0.0 copy-done.6
  21.9 2.0 %convolve.1 = (bf16[32,32,256]{2,1,0:T(8,128)(2,1)S(1)}, bf16[1024,1024]{1,0:T(8,128)(2,1)S(1)}) custom-call(s32[1]{0:T(128)} %bitcast.2.chunks, bf16[32,32,256]{2,1,0:T(8,128)(2,1)S(1)} %all-to-all-done.x_ref, bf16[2048,256]{1,0:T(8,128)(2,1)S(1)} %filter_spectrum.1.spec_ref, bf16[128,64]{1,0:T(8,128)(2,1)S(1)} %copy-done.5, bf16[64,128]{1,0:T(8,128)(2,1)S(1)} %copy-done.6, ...), custom_call_target="tpu_custom_call" | custom-call | tf_op jit(solution)/shard_map/convolve/pallas_call | solution.py:229
  23.8 13.0 %all_to_all.10 = bf16[32,32,256]{2,1,0:T(8,128)(2,1)S(1)} all-to-all(bf16[32,32,256]{2,1,0:T(8,128)(2,1)S(1)} %get-tuple-element.14), channel_id=1, replica_groups=mesh['ctx'=32,'ch'=4] {'ctx'}, dimensions={0} | all-to-all | bytes 1048576 | tf_op jit(solution)/shard_map/all_to_all | solution.py:403
  36.9 0.0 copy-done.2
  36.9 0.7 %gate_project.1 = (bf16[256,1024]{1,0:T(8,128)(2,1)S(1)}, bf16[256,1024]{1,0:T(8,128)(2,1)S(1)}) custom-call(bf16[1024,256]{1,0:T(8,128)(2,1)S(1)} %bitcast.7, bf16[256,1024]{1,0:T(8,128)(2,1)S(1)} %copy-done.2, bf16[1024,1024]{1,0:T(8,128)(2,1)S(1)} %get-tuple-element.15.w_ref), custom_call_target="tpu_custom_call" | custom-call | tf_op jit(solution)/shard_map/gate_project/pallas_call | solution.py:321
  37.6 3.5 %collective-permute-start = (bf16[256,1024]{1,0:T(8,128)(2,1)S(1)}, bf16[256,1024]{1,0:T(8,128)(2,1)S(1)}, u32[]{:S(2)}, u32[]{:S(2)}) collective-permute-start(bf16[256,1024]{1,0:T(8,128)(2,1)S(1)} %get-tuple-element.17), channel_id=1, source_target_pairs={{0,1},{1,0},{2,3},{3,2},{4,5},{5,4},{6,7},{7,6},{8,9},{9,8},{10,11... | collective-permute-start | bytes 1572872 | tf_op jit(solution)/shard_map/ppermute | solution.py:405
  41.2 2.0 %project.2 = f32[256,1024]{1,0:T(8,128)S(1)} custom-call(s32[1]{0:T(128)} %bitcast.6.chunks, bf16[256,1024]{1,0:T(8,128)(2,1)S(1)} %get-tuple-element.18.mix_ref, bf16[1024,4096]{1,0:T(8,128)(2,1)} %w_hbm.5), custom_call_target="tpu_custom_call" | custom-call | tf_op jit(solution)/shard_map/project/pallas_call | solution.py:346
  43.3 0.0 collective-permute-done
  43.3 0.2 add_convert_fusion
  43.4 2.7 %collective-permute-start.3 = (bf16[256,1024]{1,0:T(8,128)(2,1)S(1)}, bf16[256,1024]{1,0:T(8,128)(2,1)S(1)}, u32[]{:S(2)}, u32[]{:S(2)}) collective-permute-start(bf16[256,1024]{1,0:T(8,128)(2,1)S(1)} %add_convert_fusion), channel_id=1, source_target_pairs={{0,2},{2,0},{1,3},{3,1},{4,6},{6,4},{5,7},{7,5},{8,10},{10,8},{9,1... | collective-permute-start | bytes 1572872 | tf_op jit(solution)/shard_map/ppermute | solution.py:409
  46.1 0.1 pad_add_fusion.chunks
  46.2 3.5 %project.3 = (bf16[128,1024]{1,0:T(8,128)(2,1)S(1)}, bf16[128,1024]{1,0:T(8,128)(2,1)S(1)}, f32[256,1024]{1,0:T(8,128)S(1)}) custom-call(s32[2]{0:T(128)S(1)} %pad_add_fusion.chunks, bf16[256,1024]{1,0:T(8,128)(2,1)S(1)} %get-tuple-element.18.mix_ref, bf16[1024,4096]{1,0:T(8,128)(2,1)} %w_hbm.5), custom_call_target="tpu_custom_call" | custom-call | tf_op jit(solution)/shard_map/project/pallas_call | solution.py:346
  49.7 0.4 collective-permute-start.1
  50.1 0.2 collective-permute-start.2
  50.3 1.0 %collective-permute-done.1.refs_0_ = bf16[128,1024]{1,0:T(8,128)(2,1)S(1)} collective-permute-done((bf16[128,1024]{1,0:T(8,128)(2,1)S(1)}, bf16[128,1024]{1,0:T(8,128)(2,1)S(1)}, u32[]{:S(2)}, u32[]{:S(2)}) %collective-permute-start.1) | collective-permute-done | bytes 262176 | tf_op jit(solution)/shard_map/ppermute | solution.py:411
  51.3 0.4 collective-permute-done.2.refs_1_
  51.7 6.9 %collective-permute-done.3.refs_2_ = bf16[256,1024]{1,0:T(8,128)(2,1)S(1)} collective-permute-done((bf16[256,1024]{1,0:T(8,128)(2,1)S(1)}, bf16[256,1024]{1,0:T(8,128)(2,1)S(1)}, u32[]{:S(2)}, u32[]{:S(2)}) %collective-permute-start.3) | collective-permute-done | bytes 524320 | tf_op jit(solution)/shard_map/ppermute | solution.py:409
  58.6 0.9 %finish.1 = bf16[256,1024]{1,0:T(8,128)(2,1)} custom-call(f32[256,1024]{1,0:T(8,128)S(1)} %get-tuple-element.19.home_ref, bf16[128,1024]{1,0:T(8,128)(2,1)S(1)} %collective-permute-done.1.refs_0_, bf16[128,1024]{1,0:T(8,128)(2,1)S(1)} %collective-permute-done.2.refs_1_, bf16[256,1024]{1,0:T(8,128)(2,1)S(1)} %collective-permute-done.3.refs_2_), custom_call_target="tpu_custom_call" | custom-call | tf_op jit(solution)/shard_map/finish/pallas_call | solution.py:379
Async XLA Ops:
  1.9 19.9 %all-to-all-start = ((bf16[32,32,256]{2,1,0:T(8,128)(2,1)}), bf16[32,32,256]{2,1,0:T(8,128)(2,1)S(1)}, u32[]{:S(2)}, u32[]{:S(2)}) async-start(bf16[32,32,256]{2,1,0:T(8,128)(2,1)} %bitcast.3), calls=%async_computation | async-start | bytes 1048576 | tf_op jit(solution)/shard_map/all_to_all | solution.py:400
  11.7 10.1 %copy-start = (bf16[256,256]{1,0:T(8,128)(2,1)S(1)}, bf16[256,256]{1,0:T(8,128)(2,1)}, u32[]{:S(2)}) copy-start(bf16[256,256]{1,0:T(8,128)(2,1)} %constant.35.clone.forth_hbm.forth_ref) | copy-start | bytes 393220
  11.7 10.1 %copy-start.1 = (bf16[256,256]{1,0:T(8,128)(2,1)S(1)}, bf16[256,256]{1,0:T(8,128)(2,1)}, u32[]{:S(2)}) copy-start(bf16[256,256]{1,0:T(8,128)(2,1)} %constant.38.clone.swap_hbm.swap_ref) | copy-start | bytes 393220
  11.7 10.1 %copy-start.3 = (f32[64,256]{1,0:T(8,128)S(1)}, f32[64,256]{1,0:T(8,128)}, u32[]{:S(2)}) copy-start(f32[64,256]{1,0:T(8,128)} %constant.34.clone.twist_hbm.twist_ref) | copy-start | bytes 196612
  11.7 10.1 %copy-start.4 = (bf16[256,256]{1,0:T(8,128)(2,1)S(1)}, bf16[256,256]{1,0:T(8,128)(2,1)}, u32[]{:S(2)}) copy-start(bf16[256,256]{1,0:T(8,128)(2,1)} %constant.37.clone.back_ref) | copy-start | bytes 393220
  11.7 10.1 %copy-start.5 = (bf16[128,64]{1,0:T(8,128)(2,1)S(1)}, bf16[128,64]{1,0:T(8,128)(2,1)}, u32[]{:S(2)}) copy-start(bf16[128,64]{1,0:T(8,128)(2,1)} %constant.32.clone.a_ref) | copy-start | bytes 49156
  11.8 10.1 %copy-start.6 = (bf16[64,128]{1,0:T(8,128)(2,1)S(1)}, bf16[64,128]{1,0:T(8,128)(2,1)}, u32[]{:S(2)}) copy-start(bf16[64,128]{1,0:T(8,128)(2,1)} %constant.33.clone.a_back_ref) | copy-start | bytes 49156
  16.3 20.6 %copy-start.2 = (bf16[256,1024]{1,0:T(8,128)(2,1)S(1)}, bf16[256,1024]{1,0:T(8,128)(2,1)}, u32[]{:S(2)}) copy-start(bf16[256,1024]{1,0:T(8,128)(2,1)} %gate_ref.1) | copy-start | bytes 1572868
  37.6 5.6 %collective-permute-start = (bf16[256,1024]{1,0:T(8,128)(2,1)S(1)}, bf16[256,1024]{1,0:T(8,128)(2,1)S(1)}, u32[]{:S(2)}, u32[]{:S(2)}) collective-permute-start(bf16[256,1024]{1,0:T(8,128)(2,1)S(1)} %get-tuple-element.17), channel_id=1, source_target_pairs={{0,1},{1,0},{2,3},{3,2},{4,5},{5,4},{6,7},{7,6},{8,9},{9,8},{10,11... | collective-permute-start | bytes 1572872 | tf_op jit(solution)/shard_map/ppermute | solution.py:405
  43.4 15.1 %collective-permute-start.3 = (bf16[256,1024]{1,0:T(8,128)(2,1)S(1)}, bf16[256,1024]{1,0:T(8,128)(2,1)S(1)}, u32[]{:S(2)}, u32[]{:S(2)}) collective-permute-start(bf16[256,1024]{1,0:T(8,128)(2,1)S(1)} %add_convert_fusion), channel_id=1, source_target_pairs={{0,2},{2,0},{1,3},{3,1},{4,6},{6,4},{5,7},{7,5},{8,10},{10,8},{9,1... | collective-permute-start | bytes 1572872 | tf_op jit(solution)/shard_map/ppermute | solution.py:409
  49.7 1.6 %collective-permute-start.1 = (bf16[128,1024]{1,0:T(8,128)(2,1)S(1)}, bf16[128,1024]{1,0:T(8,128)(2,1)S(1)}, u32[]{:S(2)}, u32[]{:S(2)}) collective-permute-start(bf16[128,1024]{1,0:T(8,128)(2,1)S(1)} %get-tuple-element.20), channel_id=1, source_target_pairs={{0,1},{1,0},{2,3},{3,2},{4,5},{5,4},{6,7},{7,6},{8,9},{9,8},{10,11... | collective-permute-start | bytes 786440 | tf_op jit(solution)/shard_map/ppermute | solution.py:411
  50.1 1.6 %collective-permute-start.2 = (bf16[128,1024]{1,0:T(8,128)(2,1)S(1)}, bf16[128,1024]{1,0:T(8,128)(2,1)S(1)}, u32[]{:S(2)}, u32[]{:S(2)}) collective-permute-start(bf16[128,1024]{1,0:T(8,128)(2,1)S(1)} %get-tuple-element.21), channel_id=1, source_target_pairs={{0,1},{1,0},{2,3},{3,2},{4,5},{5,4},{6,7},{7,6},{8,9},{9,8},{10,11... | collective-permute-start | bytes 786440 | tf_op jit(solution)/shard_map/ppermute | solution.py:411

commit v11 on v10

--- a/solution.py
+++ b/solution.py
@@ -310,10 +310,16 @@
 
 
 def gate_kernel(y_ref, gate_ref, w_ref, mix_ref, out_ref):
-    turned = jnp.transpose(y_ref[...], (1, 0))
-    mix = (gate_ref[...].astype(F32) * turned.astype(F32)).astype(BF16)
-    mix_ref[...] = mix
-    out_ref[...] = dot(mix, w_ref[...]).astype(BF16)
+    rows = w_ref.shape[0] // PARTS
+    total = None
+    for k in range(PARTS):
+        part = slice(k * rows, (k + 1) * rows)
+        turned = jnp.transpose(y_ref[part, :], (1, 0))
+        mix = (gate_ref[:, part].astype(F32) * turned.astype(F32)).astype(BF16)
+        mix_ref[:, part] = mix
+        product = dot(mix, w_ref[part, :])
+        total = product if total is None else total + product
+    out_ref[...] = total.astype(BF16)
 
 
 def gate_project(y, gate, w):

time: 59.7 us -> 59.8 us (level)
  no operation moved by 1% of the time
where the time goes in v11:
time: 59.8 us; the launch traced here: 59.5 us
  starting transfers between devices  16.6 us (28%)
  Pallas kernels  15.6 us (26%)
  waiting for transfers between devices  13.8 us (23%)
  blocking collectives  13 us (22%)
    all_to_all x1, blocking collectives, per_device(): y = lax.all_to_all(y, 'ctx', 0, 0, tiled=True).reshape(width, tokens)  13 us
    all_to_all x1, starting transfers between devices, per_device(): x = lax.all_to_all(turned, 'ctx', 0, 0, tiled=True)  9.74 us
    ppermute x1, waiting for transfers between devices, per_device(): far = lax.ppermute(away_sum, 'ch', CHIP_PAIR)  6.86 us
    pallas_call x2, Pallas kernels, project(): pl.pallas_call(kernel, out_shape=tuple((jax.ShapeDtypeStruct((rows, cols)...  5.54 us
    all_to_all x1, waiting for transfers between devices, per_device(): x = lax.all_to_all(turned, 'ctx', 0, 0, tiled=True)  5.5 us
    pallas_call x1, Pallas kernels, filter_spectrum(): pl.pallas_call(filter_kernel, out_shape=jax.ShapeDtypeStruct((GROUP * BLO...  4.53 us
    ppermute x1, starting transfers between devices, per_device(): away_in = lax.ppermute(away_pair, 'ch', CORE_PAIR)  3.55 us
    ppermute x1, starting transfers between devices, per_device(): far = lax.ppermute(away_sum, 'ch', CHIP_PAIR)  2.7 us
  transfers between devices with their start and end apart: 5, of which 4 were waited for; matrix products, arithmetic and copies ran while one was open for 0% of the time, Pallas kernels for 17%

profile of v11, /device:TPU:1, one launch (start us, length us, event | category | flops | bytes accessed | tf_op | source)
XLA Modules:
  0.0 59.5 jit_solution(2352201620465377838)
XLA Ops:
  0.0 1.9 %turn.1 = bf16[1024,256]{1,0:T(8,128)(2,1)} custom-call(bf16[256,1024]{1,0:T(8,128)(2,1)} %v_hbm.1), custom_call_target="tpu_custom_call" | custom-call | tf_op jit(solution)/shard_map/turn/pallas_call | solution.py:271
  1.9 9.7 %all-to-all-start = ((bf16[32,32,256]{2,1,0:T(8,128)(2,1)}), bf16[32,32,256]{2,1,0:T(8,128)(2,1)S(1)}, u32[]{:S(2)}, u32[]{:S(2)}) async-start(bf16[32,32,256]{2,1,0:T(8,128)(2,1)} %bitcast.3), calls=%async_computation | async-start | bytes 1048576 | tf_op jit(solution)/shard_map/all_to_all | solution.py:406
  11.7 0.0 copy-start
  11.7 0.0 copy-start.1
  11.7 0.0 copy-start.3
  11.7 0.0 copy-start.4
  11.7 0.0 copy-start.5
  11.8 0.0 copy-start.6
  11.8 4.5 %filter_spectrum.1.spec_ref = bf16[2048,256]{1,0:T(8,128)(2,1)S(1)} custom-call(s32[1]{0:T(128)} %bitcast.4.which, bf16[8192,1024]{1,0:T(8,128)(2,1)} %h_hbm.1, bf16[128,128]{1,0:T(8,128)(2,1)} %constant.31.clone.a_hbm, f32[64,256]{1,0:T(8,128)} %constant.34.clone.twist_hbm.twist_ref, bf16[256,256]{1,0:T(8,128)(2,1)} %constant.35.clone.forth_hbm.forth_ref, ...), custom_call_target="tpu_custom_call" | custom-call | tf_op jit(solution)/shard_map/filter_spectrum/pallas_call | solution.py:204
  16.3 0.0 copy-start.2
  16.3 5.5 %all-to-all-done.x_ref = bf16[32,32,256]{2,1,0:T(8,128)(2,1)S(1)} async-done(((bf16[32,32,256]{2,1,0:T(8,128)(2,1)}), bf16[32,32,256]{2,1,0:T(8,128)(2,1)S(1)}, u32[]{:S(2)}, u32[]{:S(2)}) %all-to-all-start) | async-done | bytes 524320 | tf_op jit(solution)/shard_map/all_to_all | solution.py:406
  21.8 0.0 copy-done
  21.8 0.0 copy-done.1
  21.8 0.0 copy-done.3
  21.8 0.0 copy-done.4
  21.8 0.0 copy-done.5
  21.8 0.0 copy-done.6
  21.9 2.0 %convolve.1 = (bf16[32,32,256]{2,1,0:T(8,128)(2,1)S(1)}, bf16[1024,1024]{1,0:T(8,128)(2,1)S(1)}) custom-call(s32[1]{0:T(128)} %bitcast.2.chunks, bf16[32,32,256]{2,1,0:T(8,128)(2,1)S(1)} %all-to-all-done.x_ref, bf16[2048,256]{1,0:T(8,128)(2,1)S(1)} %filter_spectrum.1.spec_ref, bf16[128,64]{1,0:T(8,128)(2,1)S(1)} %copy-done.5, bf16[64,128]{1,0:T(8,128)(2,1)S(1)} %copy-done.6, ...), custom_call_target="tpu_custom_call" | custom-call | tf_op jit(solution)/shard_map/convolve/pallas_call | solution.py:229
  23.8 13.0 %all_to_all.10 = bf16[32,32,256]{2,1,0:T(8,128)(2,1)S(1)} all-to-all(bf16[32,32,256]{2,1,0:T(8,128)(2,1)S(1)} %get-tuple-element.14), channel_id=1, replica_groups=mesh['ctx'=32,'ch'=4] {'ctx'}, dimensions={0} | all-to-all | bytes 1048576 | tf_op jit(solution)/shard_map/all_to_all | solution.py:409
  36.9 0.0 copy-done.2
  36.9 0.8 %gate_project.1 = (bf16[256,1024]{1,0:T(8,128)(2,1)S(1)}, bf16[256,1024]{1,0:T(8,128)(2,1)S(1)}) custom-call(bf16[1024,256]{1,0:T(8,128)(2,1)S(1)} %bitcast.7, bf16[256,1024]{1,0:T(8,128)(2,1)S(1)} %copy-done.2, bf16[1024,1024]{1,0:T(8,128)(2,1)S(1)} %get-tuple-element.15.w_ref), custom_call_target="tpu_custom_call" | custom-call | tf_op jit(solution)/shard_map/gate_project/pallas_call | solution.py:327
  37.7 3.5 %collective-permute-start = (bf16[256,1024]{1,0:T(8,128)(2,1)S(1)}, bf16[256,1024]{1,0:T(8,128)(2,1)S(1)}, u32[]{:S(2)}, u32[]{:S(2)}) collective-permute-start(bf16[256,1024]{1,0:T(8,128)(2,1)S(1)} %get-tuple-element.17), channel_id=1, source_target_pairs={{0,1},{1,0},{2,3},{3,2},{4,5},{5,4},{6,7},{7,6},{8,9},{9,8},{10,11... | collective-permute-start | bytes 1572872 | tf_op jit(solution)/shard_map/ppermute | solution.py:411
  41.2 2.0 %project.2 = f32[256,1024]{1,0:T(8,128)S(1)} custom-call(s32[1]{0:T(128)} %bitcast.6.chunks, bf16[256,1024]{1,0:T(8,128)(2,1)S(1)} %get-tuple-element.18.mix_ref, bf16[1024,4096]{1,0:T(8,128)(2,1)} %w_hbm.5), custom_call_target="tpu_custom_call" | custom-call | tf_op jit(solution)/shard_map/project/pallas_call | solution.py:352
  43.3 0.0 collective-permute-done
  43.3 0.2 add_convert_fusion
  43.5 2.7 %collective-permute-start.3 = (bf16[256,1024]{1,0:T(8,128)(2,1)S(1)}, bf16[256,1024]{1,0:T(8,128)(2,1)S(1)}, u32[]{:S(2)}, u32[]{:S(2)}) collective-permute-start(bf16[256,1024]{1,0:T(8,128)(2,1)S(1)} %add_convert_fusion), channel_id=1, source_target_pairs={{0,2},{2,0},{1,3},{3,1},{4,6},{6,4},{5,7},{7,5},{8,10},{10,8},{9,1... | collective-permute-start | bytes 1572872 | tf_op jit(solution)/shard_map/ppermute | solution.py:415
  46.2 0.1 pad_add_fusion.chunks
  46.2 3.5 %project.3 = (bf16[128,1024]{1,0:T(8,128)(2,1)S(1)}, bf16[128,1024]{1,0:T(8,128)(2,1)S(1)}, f32[256,1024]{1,0:T(8,128)S(1)}) custom-call(s32[2]{0:T(128)S(1)} %pad_add_fusion.chunks, bf16[256,1024]{1,0:T(8,128)(2,1)S(1)} %get-tuple-element.18.mix_ref, bf16[1024,4096]{1,0:T(8,128)(2,1)} %w_hbm.5), custom_call_target="tpu_custom_call" | custom-call | tf_op jit(solution)/shard_map/project/pallas_call | solution.py:352
  49.7 0.4 collective-permute-start.1
  50.1 0.2 collective-permute-start.2
  50.3 1.0 %collective-permute-done.1.refs_0_ = bf16[128,1024]{1,0:T(8,128)(2,1)S(1)} collective-permute-done((bf16[128,1024]{1,0:T(8,128)(2,1)S(1)}, bf16[128,1024]{1,0:T(8,128)(2,1)S(1)}, u32[]{:S(2)}, u32[]{:S(2)}) %collective-permute-start.1) | collective-permute-done | bytes 262176 | tf_op jit(solution)/shard_map/ppermute | solution.py:417
  51.3 0.4 collective-permute-done.2.refs_1_
  51.7 6.9 %collective-permute-done.3.refs_2_ = bf16[256,1024]{1,0:T(8,128)(2,1)S(1)} collective-permute-done((bf16[256,1024]{1,0:T(8,128)(2,1)S(1)}, bf16[256,1024]{1,0:T(8,128)(2,1)S(1)}, u32[]{:S(2)}, u32[]{:S(2)}) %collective-permute-start.3) | collective-permute-done | bytes 524320 | tf_op jit(solution)/shard_map/ppermute | solution.py:415
  58.6 0.9 %finish.1 = bf16[256,1024]{1,0:T(8,128)(2,1)} custom-call(f32[256,1024]{1,0:T(8,128)S(1)} %get-tuple-element.19.home_ref, bf16[128,1024]{1,0:T(8,128)(2,1)S(1)} %collective-permute-done.1.refs_0_, bf16[128,1024]{1,0:T(8,128)(2,1)S(1)} %collective-permute-done.2.refs_1_, bf16[256,1024]{1,0:T(8,128)(2,1)S(1)} %collective-permute-done.3.refs_2_), custom_call_target="tpu_custom_call" | custom-call | tf_op jit(solution)/shard_map/finish/pallas_call | solution.py:385
Async XLA Ops:
  1.9 19.9 %all-to-all-start = ((bf16[32,32,256]{2,1,0:T(8,128)(2,1)}), bf16[32,32,256]{2,1,0:T(8,128)(2,1)S(1)}, u32[]{:S(2)}, u32[]{:S(2)}) async-start(bf16[32,32,256]{2,1,0:T(8,128)(2,1)} %bitcast.3), calls=%async_computation | async-start | bytes 1048576 | tf_op jit(solution)/shard_map/all_to_all | solution.py:406
  11.7 10.1 %copy-start = (bf16[256,256]{1,0:T(8,128)(2,1)S(1)}, bf16[256,256]{1,0:T(8,128)(2,1)}, u32[]{:S(2)}) copy-start(bf16[256,256]{1,0:T(8,128)(2,1)} %constant.35.clone.forth_hbm.forth_ref) | copy-start | bytes 393220
  11.7 10.1 %copy-start.1 = (bf16[256,256]{1,0:T(8,128)(2,1)S(1)}, bf16[256,256]{1,0:T(8,128)(2,1)}, u32[]{:S(2)}) copy-start(bf16[256,256]{1,0:T(8,128)(2,1)} %constant.38.clone.swap_hbm.swap_ref) | copy-start | bytes 393220
  11.7 10.1 %copy-start.3 = (f32[64,256]{1,0:T(8,128)S(1)}, f32[64,256]{1,0:T(8,128)}, u32[]{:S(2)}) copy-start(f32[64,256]{1,0:T(8,128)} %constant.34.clone.twist_hbm.twist_ref) | copy-start | bytes 196612
  11.7 10.1 %copy-start.4 = (bf16[256,256]{1,0:T(8,128)(2,1)S(1)}, bf16[256,256]{1,0:T(8,128)(2,1)}, u32[]{:S(2)}) copy-start(bf16[256,256]{1,0:T(8,128)(2,1)} %constant.37.clone.back_ref) | copy-start | bytes 393220
  11.7 10.1 %copy-start.5 = (bf16[128,64]{1,0:T(8,128)(2,1)S(1)}, bf16[128,64]{1,0:T(8,128)(2,1)}, u32[]{:S(2)}) copy-start(bf16[128,64]{1,0:T(8,128)(2,1)} %constant.32.clone.a_ref) | copy-start | bytes 49156
  11.8 10.1 %copy-start.6 = (bf16[64,128]{1,0:T(8,128)(2,1)S(1)}, bf16[64,128]{1,0:T(8,128)(2,1)}, u32[]{:S(2)}) copy-start(bf16[64,128]{1,0:T(8,128)(2,1)} %constant.33.clone.a_back_ref) | copy-start | bytes 49156
  16.3 20.6 %copy-start.2 = (bf16[256,1024]{1,0:T(8,128)(2,1)S(1)}, bf16[256,1024]{1,0:T(8,128)(2,1)}, u32[]{:S(2)}) copy-start(bf16[256,1024]{1,0:T(8,128)(2,1)} %gate_ref.1) | copy-start | bytes 1572868
  37.7 5.6 %collective-permute-start = (bf16[256,1024]{1,0:T(8,128)(2,1)S(1)}, bf16[256,1024]{1,0:T(8,128)(2,1)S(1)}, u32[]{:S(2)}, u32[]{:S(2)}) collective-permute-start(bf16[256,1024]{1,0:T(8,128)(2,1)S(1)} %get-tuple-element.17), channel_id=1, source_target_pairs={{0,1},{1,0},{2,3},{3,2},{4,5},{5,4},{6,7},{7,6},{8,9},{9,8},{10,11... | collective-permute-start | bytes 1572872 | tf_op jit(solution)/shard_map/ppermute | solution.py:411
  43.5 15.1 %collective-permute-start.3 = (bf16[256,1024]{1,0:T(8,128)(2,1)S(1)}, bf16[256,1024]{1,0:T(8,128)(2,1)S(1)}, u32[]{:S(2)}, u32[]{:S(2)}) collective-permute-start(bf16[256,1024]{1,0:T(8,128)(2,1)S(1)} %add_convert_fusion), channel_id=1, source_target_pairs={{0,2},{2,0},{1,3},{3,1},{4,6},{6,4},{5,7},{7,5},{8,10},{10,8},{9,1... | collective-permute-start | bytes 1572872 | tf_op jit(solution)/shard_map/ppermute | solution.py:415
  49.7 1.6 %collective-permute-start.1 = (bf16[128,1024]{1,0:T(8,128)(2,1)S(1)}, bf16[128,1024]{1,0:T(8,128)(2,1)S(1)}, u32[]{:S(2)}, u32[]{:S(2)}) collective-permute-start(bf16[128,1024]{1,0:T(8,128)(2,1)S(1)} %get-tuple-element.20), channel_id=1, source_target_pairs={{0,1},{1,0},{2,3},{3,2},{4,5},{5,4},{6,7},{7,6},{8,9},{9,8},{10,11... | collective-permute-start | bytes 786440 | tf_op jit(solution)/shard_map/ppermute | solution.py:417
  50.1 1.6 %collective-permute-start.2 = (bf16[128,1024]{1,0:T(8,128)(2,1)S(1)}, bf16[128,1024]{1,0:T(8,128)(2,1)S(1)}, u32[]{:S(2)}, u32[]{:S(2)}) collective-permute-start(bf16[128,1024]{1,0:T(8,128)(2,1)S(1)} %get-tuple-element.21), channel_id=1, source_target_pairs={{0,1},{1,0},{2,3},{3,2},{4,5},{5,4},{6,7},{7,6},{8,9},{9,8},{10,11... | collective-permute-start | bytes 786440 | tf_op jit(solution)/shard_map/ppermute | solution.py:417

commit v12 on v11

--- a/solution.py
+++ b/solution.py
@@ -360,15 +360,18 @@
     )(chunks, mix, *in_hbm(w))
 
 
+OUT_PARTS = 8
+
+
 def finish(home, near, far):
     tokens, cols = home.shape
-    rows = tokens // PARTS
+    rows = tokens // OUT_PARTS
     each = near[0].shape[0]
 
     def kernel(home_ref, *refs):
         near_refs, (far_ref, out_hbm, sum_ref, sem) = refs[: len(near)], refs[len(near) :]
         copies = []
-        for k in range(PARTS):
+        for k in range(OUT_PARTS):
             part = slice(k * rows, (k + 1) * rows)
             piece, first = divmod(k * rows, each)
             other = near_refs[piece][first : first + rows, :]
@@ -387,7 +390,7 @@
         out_shape=jax.ShapeDtypeStruct(home.shape, BF16),
         in_specs=[pl.BlockSpec(memory_space=pltpu.VMEM)] * (2 + len(near)),
         out_specs=pl.BlockSpec(memory_space=pltpu.HBM),
-        scratch_shapes=[pltpu.VMEM(home.shape, BF16), pltpu.SemaphoreType.DMA((PARTS,))],
+        scratch_shapes=[pltpu.VMEM(home.shape, BF16), pltpu.SemaphoreType.DMA((OUT_PARTS,))],
         compiler_params=pltpu.CompilerParams(vmem_limit_bytes=16 << 20),
         name="finish",
     )(home, *near, far)

time: 59.8 us -> 59.8 us (level)
  no operation moved by 1% of the time
where the time goes in v12:
time: 59.8 us; the launch traced here: 59.5 us
  starting transfers between devices  16.6 us (28%)
  Pallas kernels  15.6 us (26%)
  waiting for transfers between devices  13.8 us (23%)
  blocking collectives  13 us (22%)
    all_to_all x1, blocking collectives, per_device(): y = lax.all_to_all(y, 'ctx', 0, 0, tiled=True).reshape(width, tokens)  13 us
    all_to_all x1, starting transfers between devices, per_device(): x = lax.all_to_all(turned, 'ctx', 0, 0, tiled=True)  9.74 us
    ppermute x1, waiting for transfers between devices, per_device(): far = lax.ppermute(away_sum, 'ch', CHIP_PAIR)  6.86 us
    pallas_call x2, Pallas kernels, project(): pl.pallas_call(kernel, out_shape=tuple((jax.ShapeDtypeStruct((rows, cols)...  5.54 us
    all_to_all x1, waiting for transfers between devices, per_device(): x = lax.all_to_all(turned, 'ctx', 0, 0, tiled=True)  5.5 us
    pallas_call x1, Pallas kernels, filter_spectrum(): pl.pallas_call(filter_kernel, out_shape=jax.ShapeDtypeStruct((GROUP * BLO...  4.53 us
    ppermute x1, starting transfers between devices, per_device(): away_in = lax.ppermute(away_pair, 'ch', CORE_PAIR)  3.55 us
    ppermute x1, starting transfers between devices, per_device(): far = lax.ppermute(away_sum, 'ch', CHIP_PAIR)  2.7 us
  transfers between devices with their start and end apart: 5, of which 4 were waited for; matrix products, arithmetic and copies ran while one was open for 0% of the time, Pallas kernels for 17%

profile of v12, /device:TPU:1, one launch (start us, length us, event | category | flops | bytes accessed | tf_op | source)
XLA Modules:
  0.0 59.5 jit_solution(16381647156470261428)
XLA Ops:
  0.0 1.9 %turn.1 = bf16[1024,256]{1,0:T(8,128)(2,1)} custom-call(bf16[256,1024]{1,0:T(8,128)(2,1)} %v_hbm.1), custom_call_target="tpu_custom_call" | custom-call | tf_op jit(solution)/shard_map/turn/pallas_call | solution.py:271
  1.9 9.7 %all-to-all-start = ((bf16[32,32,256]{2,1,0:T(8,128)(2,1)}), bf16[32,32,256]{2,1,0:T(8,128)(2,1)S(1)}, u32[]{:S(2)}, u32[]{:S(2)}) async-start(bf16[32,32,256]{2,1,0:T(8,128)(2,1)} %bitcast.3), calls=%async_computation | async-start | bytes 1048576 | tf_op jit(solution)/shard_map/all_to_all | solution.py:409
  11.7 0.0 copy-start
  11.7 0.0 copy-start.1
  11.7 0.0 copy-start.3
  11.7 0.0 copy-start.4
  11.7 0.0 copy-start.5
  11.8 0.0 copy-start.6
  11.8 4.5 %filter_spectrum.1.spec_ref = bf16[2048,256]{1,0:T(8,128)(2,1)S(1)} custom-call(s32[1]{0:T(128)} %bitcast.4.which, bf16[8192,1024]{1,0:T(8,128)(2,1)} %h_hbm.1, bf16[128,128]{1,0:T(8,128)(2,1)} %constant.31.clone.a_hbm, f32[64,256]{1,0:T(8,128)} %constant.34.clone.twist_hbm.twist_ref, bf16[256,256]{1,0:T(8,128)(2,1)} %constant.35.clone.forth_hbm.forth_ref, ...), custom_call_target="tpu_custom_call" | custom-call | tf_op jit(solution)/shard_map/filter_spectrum/pallas_call | solution.py:204
  16.3 0.0 copy-start.2
  16.3 5.5 %all-to-all-done.x_ref = bf16[32,32,256]{2,1,0:T(8,128)(2,1)S(1)} async-done(((bf16[32,32,256]{2,1,0:T(8,128)(2,1)}), bf16[32,32,256]{2,1,0:T(8,128)(2,1)S(1)}, u32[]{:S(2)}, u32[]{:S(2)}) %all-to-all-start) | async-done | bytes 524320 | tf_op jit(solution)/shard_map/all_to_all | solution.py:409
  21.8 0.0 copy-done
  21.8 0.0 copy-done.1
  21.8 0.0 copy-done.3
  21.8 0.0 copy-done.4
  21.8 0.0 copy-done.5
  21.8 0.0 copy-done.6
  21.9 2.0 %convolve.1 = (bf16[32,32,256]{2,1,0:T(8,128)(2,1)S(1)}, bf16[1024,1024]{1,0:T(8,128)(2,1)S(1)}) custom-call(s32[1]{0:T(128)} %bitcast.2.chunks, bf16[32,32,256]{2,1,0:T(8,128)(2,1)S(1)} %all-to-all-done.x_ref, bf16[2048,256]{1,0:T(8,128)(2,1)S(1)} %filter_spectrum.1.spec_ref, bf16[128,64]{1,0:T(8,128)(2,1)S(1)} %copy-done.5, bf16[64,128]{1,0:T(8,128)(2,1)S(1)} %copy-done.6, ...), custom_call_target="tpu_custom_call" | custom-call | tf_op jit(solution)/shard_map/convolve/pallas_call | solution.py:229
  23.8 13.0 %all_to_all.10 = bf16[32,32,256]{2,1,0:T(8,128)(2,1)S(1)} all-to-all(bf16[32,32,256]{2,1,0:T(8,128)(2,1)S(1)} %get-tuple-element.14), channel_id=1, replica_groups=mesh['ctx'=32,'ch'=4] {'ctx'}, dimensions={0} | all-to-all | bytes 1048576 | tf_op jit(solution)/shard_map/all_to_all | solution.py:412
  36.9 0.0 copy-done.2
  36.9 0.8 %gate_project.1 = (bf16[256,1024]{1,0:T(8,128)(2,1)S(1)}, bf16[256,1024]{1,0:T(8,128)(2,1)S(1)}) custom-call(bf16[1024,256]{1,0:T(8,128)(2,1)S(1)} %bitcast.7, bf16[256,1024]{1,0:T(8,128)(2,1)S(1)} %copy-done.2, bf16[1024,1024]{1,0:T(8,128)(2,1)S(1)} %get-tuple-element.15.w_ref), custom_call_target="tpu_custom_call" | custom-call | tf_op jit(solution)/shard_map/gate_project/pallas_call | solution.py:327
  37.7 3.5 %collective-permute-start = (bf16[256,1024]{1,0:T(8,128)(2,1)S(1)}, bf16[256,1024]{1,0:T(8,128)(2,1)S(1)}, u32[]{:S(2)}, u32[]{:S(2)}) collective-permute-start(bf16[256,1024]{1,0:T(8,128)(2,1)S(1)} %get-tuple-element.17), channel_id=1, source_target_pairs={{0,1},{1,0},{2,3},{3,2},{4,5},{5,4},{6,7},{7,6},{8,9},{9,8},{10,11... | collective-permute-start | bytes 1572872 | tf_op jit(solution)/shard_map/ppermute | solution.py:414
  41.2 2.0 %project.2 = f32[256,1024]{1,0:T(8,128)S(1)} custom-call(s32[1]{0:T(128)} %bitcast.6.chunks, bf16[256,1024]{1,0:T(8,128)(2,1)S(1)} %get-tuple-element.18.mix_ref, bf16[1024,4096]{1,0:T(8,128)(2,1)} %w_hbm.5), custom_call_target="tpu_custom_call" | custom-call | tf_op jit(solution)/shard_map/project/pallas_call | solution.py:352
  43.3 0.0 collective-permute-done
  43.3 0.2 add_convert_fusion
  43.5 2.7 %collective-permute-start.3 = (bf16[256,1024]{1,0:T(8,128)(2,1)S(1)}, bf16[256,1024]{1,0:T(8,128)(2,1)S(1)}, u32[]{:S(2)}, u32[]{:S(2)}) collective-permute-start(bf16[256,1024]{1,0:T(8,128)(2,1)S(1)} %add_convert_fusion), channel_id=1, source_target_pairs={{0,2},{2,0},{1,3},{3,1},{4,6},{6,4},{5,7},{7,5},{8,10},{10,8},{9,1... | collective-permute-start | bytes 1572872 | tf_op jit(solution)/shard_map/ppermute | solution.py:418
  46.2 0.1 pad_add_fusion.chunks
  46.2 3.5 %project.3 = (bf16[128,1024]{1,0:T(8,128)(2,1)S(1)}, bf16[128,1024]{1,0:T(8,128)(2,1)S(1)}, f32[256,1024]{1,0:T(8,128)S(1)}) custom-call(s32[2]{0:T(128)S(1)} %pad_add_fusion.chunks, bf16[256,1024]{1,0:T(8,128)(2,1)S(1)} %get-tuple-element.18.mix_ref, bf16[1024,4096]{1,0:T(8,128)(2,1)} %w_hbm.5), custom_call_target="tpu_custom_call" | custom-call | tf_op jit(solution)/shard_map/project/pallas_call | solution.py:352
  49.7 0.4 collective-permute-start.1
  50.1 0.2 collective-permute-start.2
  50.3 1.0 %collective-permute-done.1.refs_0_ = bf16[128,1024]{1,0:T(8,128)(2,1)S(1)} collective-permute-done((bf16[128,1024]{1,0:T(8,128)(2,1)S(1)}, bf16[128,1024]{1,0:T(8,128)(2,1)S(1)}, u32[]{:S(2)}, u32[]{:S(2)}) %collective-permute-start.1) | collective-permute-done | bytes 262176 | tf_op jit(solution)/shard_map/ppermute | solution.py:420
  51.3 0.4 collective-permute-done.2.refs_1_
  51.7 6.9 %collective-permute-done.3.refs_2_ = bf16[256,1024]{1,0:T(8,128)(2,1)S(1)} collective-permute-done((bf16[256,1024]{1,0:T(8,128)(2,1)S(1)}, bf16[256,1024]{1,0:T(8,128)(2,1)S(1)}, u32[]{:S(2)}, u32[]{:S(2)}) %collective-permute-start.3) | collective-permute-done | bytes 524320 | tf_op jit(solution)/shard_map/ppermute | solution.py:418
  58.6 0.9 %finish.1 = bf16[256,1024]{1,0:T(8,128)(2,1)} custom-call(f32[256,1024]{1,0:T(8,128)S(1)} %get-tuple-element.19.home_ref, bf16[128,1024]{1,0:T(8,128)(2,1)S(1)} %collective-permute-done.1.refs_0_, bf16[128,1024]{1,0:T(8,128)(2,1)S(1)} %collective-permute-done.2.refs_1_, bf16[256,1024]{1,0:T(8,128)(2,1)S(1)} %collective-permute-done.3.refs_2_), custom_call_target="tpu_custom_call" | custom-call | tf_op jit(solution)/shard_map/finish/pallas_call | solution.py:388
Async XLA Ops:
  1.9 19.9 %all-to-all-start = ((bf16[32,32,256]{2,1,0:T(8,128)(2,1)}), bf16[32,32,256]{2,1,0:T(8,128)(2,1)S(1)}, u32[]{:S(2)}, u32[]{:S(2)}) async-start(bf16[32,32,256]{2,1,0:T(8,128)(2,1)} %bitcast.3), calls=%async_computation | async-start | bytes 1048576 | tf_op jit(solution)/shard_map/all_to_all | solution.py:409
  11.7 10.1 %copy-start = (bf16[256,256]{1,0:T(8,128)(2,1)S(1)}, bf16[256,256]{1,0:T(8,128)(2,1)}, u32[]{:S(2)}) copy-start(bf16[256,256]{1,0:T(8,128)(2,1)} %constant.35.clone.forth_hbm.forth_ref) | copy-start | bytes 393220
  11.7 10.1 %copy-start.1 = (bf16[256,256]{1,0:T(8,128)(2,1)S(1)}, bf16[256,256]{1,0:T(8,128)(2,1)}, u32[]{:S(2)}) copy-start(bf16[256,256]{1,0:T(8,128)(2,1)} %constant.38.clone.swap_hbm.swap_ref) | copy-start | bytes 393220
  11.7 10.1 %copy-start.3 = (f32[64,256]{1,0:T(8,128)S(1)}, f32[64,256]{1,0:T(8,128)}, u32[]{:S(2)}) copy-start(f32[64,256]{1,0:T(8,128)} %constant.34.clone.twist_hbm.twist_ref) | copy-start | bytes 196612
  11.7 10.1 %copy-start.4 = (bf16[256,256]{1,0:T(8,128)(2,1)S(1)}, bf16[256,256]{1,0:T(8,128)(2,1)}, u32[]{:S(2)}) copy-start(bf16[256,256]{1,0:T(8,128)(2,1)} %constant.37.clone.back_ref) | copy-start | bytes 393220
  11.7 10.1 %copy-start.5 = (bf16[128,64]{1,0:T(8,128)(2,1)S(1)}, bf16[128,64]{1,0:T(8,128)(2,1)}, u32[]{:S(2)}) copy-start(bf16[128,64]{1,0:T(8,128)(2,1)} %constant.32.clone.a_ref) | copy-start | bytes 49156
  11.8 10.1 %copy-start.6 = (bf16[64,128]{1,0:T(8,128)(2,1)S(1)}, bf16[64,128]{1,0:T(8,128)(2,1)}, u32[]{:S(2)}) copy-start(bf16[64,128]{1,0:T(8,128)(2,1)} %constant.33.clone.a_back_ref) | copy-start | bytes 49156
  16.3 20.6 %copy-start.2 = (bf16[256,1024]{1,0:T(8,128)(2,1)S(1)}, bf16[256,1024]{1,0:T(8,128)(2,1)}, u32[]{:S(2)}) copy-start(bf16[256,1024]{1,0:T(8,128)(2,1)} %gate_ref.1) | copy-start | bytes 1572868
  37.7 5.6 %collective-permute-start = (bf16[256,1024]{1,0:T(8,128)(2,1)S(1)}, bf16[256,1024]{1,0:T(8,128)(2,1)S(1)}, u32[]{:S(2)}, u32[]{:S(2)}) collective-permute-start(bf16[256,1024]{1,0:T(8,128)(2,1)S(1)} %get-tuple-element.17), channel_id=1, source_target_pairs={{0,1},{1,0},{2,3},{3,2},{4,5},{5,4},{6,7},{7,6},{8,9},{9,8},{10,11... | collective-permute-start | bytes 1572872 | tf_op jit(solution)/shard_map/ppermute | solution.py:414
  43.5 15.1 %collective-permute-start.3 = (bf16[256,1024]{1,0:T(8,128)(2,1)S(1)}, bf16[256,1024]{1,0:T(8,128)(2,1)S(1)}, u32[]{:S(2)}, u32[]{:S(2)}) collective-permute-start(bf16[256,1024]{1,0:T(8,128)(2,1)S(1)} %add_convert_fusion), channel_id=1, source_target_pairs={{0,2},{2,0},{1,3},{3,1},{4,6},{6,4},{5,7},{7,5},{8,10},{10,8},{9,1... | collective-permute-start | bytes 1572872 | tf_op jit(solution)/shard_map/ppermute | solution.py:418
  49.7 1.6 %collective-permute-start.1 = (bf16[128,1024]{1,0:T(8,128)(2,1)S(1)}, bf16[128,1024]{1,0:T(8,128)(2,1)S(1)}, u32[]{:S(2)}, u32[]{:S(2)}) collective-permute-start(bf16[128,1024]{1,0:T(8,128)(2,1)S(1)} %get-tuple-element.20), channel_id=1, source_target_pairs={{0,1},{1,0},{2,3},{3,2},{4,5},{5,4},{6,7},{7,6},{8,9},{9,8},{10,11... | collective-permute-start | bytes 786440 | tf_op jit(solution)/shard_map/ppermute | solution.py:420
  50.1 1.6 %collective-permute-start.2 = (bf16[128,1024]{1,0:T(8,128)(2,1)S(1)}, bf16[128,1024]{1,0:T(8,128)(2,1)S(1)}, u32[]{:S(2)}, u32[]{:S(2)}) collective-permute-start(bf16[128,1024]{1,0:T(8,128)(2,1)S(1)} %get-tuple-element.21), channel_id=1, source_target_pairs={{0,1},{1,0},{2,3},{3,2},{4,5},{5,4},{6,7},{7,6},{8,9},{9,8},{10,11... | collective-permute-start | bytes 786440 | tf_op jit(solution)/shard_map/ppermute | solution.py:420
